TPU v7x, 128 devices: a whole 4x4x4 slice. The times are simulated.
128 devices in a mesh: leaf: 64 (over z, y, x), rhs: 2 (over core).
Axes of the slice: x: 4, y: 4, z: 4, core: 2. Of those that a mesh axis runs over, the one named last changes fastest.
Arguments:
- rhs_block: bfloat16 [128, 524288], P('rhs', 'leaf'), may hold values from -6 to 6
- basis_t: bfloat16 [2048, 64, 256], P('leaf'), may hold values from -0.375 to 0.375
- near_blocks: bfloat16 [2048, 5, 256, 256], P('leaf'), may hold values from -0.15625 to 0.15625
- near_list: int32 [2048, 5], P('leaf'), may hold values from 0 to 2047, as said below
- leaf_transfer: bfloat16 [2048, 64, 64], P('leaf'), may hold values from -0.25 to 0.25
- couple_list: int32 [2048, 4], P('leaf'), may hold values from 0 to 2047, as said below
- leaf_couple: bfloat16 [2048, 4, 64, 64], P('leaf'), may hold values from -0.375 to 0.375
- top_transfer: bfloat16 [126, 64, 64], replicated, may hold values from -0.625 to 0.625
- top_couple: bfloat16 [126, 64, 64], replicated, may hold values from -0.75 to 0.75
Outputs:
- first_image: bfloat16 [128, 524288], P('rhs', 'leaf')
- second_image: bfloat16 [128, 524288], P('rhs', 'leaf')
Inputs may be any that keep to these rules, and one draw needn't show every extreme that they name: near_list[l, 0] = l; the other entries of a row are distinct leaves at distances 1 to 16 from l, and one of them at distance exactly 16. `couple_list`: the entries of a row are distinct leaves at distances 16 + 1 to 32 from l, one of them at distance exactly 32.
All inputs are finite; a program needn't handle non-finite values.
Results may differ from a plain program's by a relative error of at most 0.0058.
Values may be sent and summed in bfloat16 or wider, within the bound.
No kernel may reach another device: no remote copies, remote signals or barrier semaphores. Data moves between devices by JAX's collectives and lax.ppermute only.
A program may use at most 128 MiB of HBM per device.

v0:
```python
import jax
import jax.numpy as jnp
from jax import lax
from jax.sharding import PartitionSpec as P

REACH = 16
FARR = 32


def extended(cells, sides, width):
    for axis, dim in sides:
        count = lax.axis_size(axis)
        ends = count - 1
        head = lax.slice_in_dim(cells, 0, width, axis=dim)
        tail = lax.slice_in_dim(cells, cells.shape[dim] - width, cells.shape[dim], axis=dim)
        cells = jnp.concatenate(
            [
                lax.ppermute(tail, axis, [(i, (i + 1) % count) for i in range(ends)]),
                cells,
                lax.ppermute(head, axis, [((i + 1) % count, i) for i in range(ends)]),
            ],
            axis=dim,
        )
    return cells


def swapped(value, axis, apart):
    mask = 2**apart
    pairs = [(source, source ^ mask) for source in range(lax.axis_size(axis))]
    return lax.ppermute(value, axis, pairs)


def pick_row(table, row_id):
    return lax.dynamic_index_in_dim(table, row_id, 0, keepdims=False)


def near_rows(vectors, points):
    return extended(vectors, (("leaf", 1),), REACH * points)


def coef_rows(coefficients):
    return extended(coefficients, (("leaf", 0),), FARR)


def top_tree(node_coef, device, top_transfer, top_couple):
    hp = lax.Precision.HIGHEST
    devices = lax.axis_size("leaf")
    levels = devices.bit_length() - 1
    couplings = []
    current = node_coef
    for height in range(levels):
        nodes = devices >> height
        offset = 2 * devices - 2 * nodes
        node_id = device >> height
        other = swapped(current, "leaf", height)
        couple_here = pick_row(top_couple, offset + node_id).astype(jnp.float32)
        couplings.append(jnp.dot(couple_here, other, precision=hp))
        own_map = pick_row(top_transfer, offset + node_id).astype(jnp.float32)
        sib_map = pick_row(top_transfer, offset + jnp.bitwise_xor(node_id, 1)).astype(jnp.float32)
        current = jnp.dot(own_map.T, current, precision=hp) + jnp.dot(
            sib_map.T, other, precision=hp
        )
    descent = jnp.zeros_like(node_coef)
    for height in reversed(range(levels)):
        nodes = devices >> height
        offset = 2 * devices - 2 * nodes
        node_id = device >> height
        trans_here = pick_row(top_transfer, offset + node_id).astype(jnp.float32)
        descent = couplings[height] + jnp.dot(trans_here, descent, precision=hp)
    return descent


def apply_once(
    vectors,
    basis_t,
    near_blocks,
    near_list,
    leaf_transfer,
    couple_list,
    leaf_couple,
    top_transfer,
    top_couple,
):
    columns = vectors.shape[0]
    leaves = basis_t.shape[0]
    points = basis_t.shape[2]
    device = lax.axis_index("leaf")
    first_leaf = device * leaves
    own_rows = vectors.reshape(columns, leaves, points)
    near_width = near_list.shape[1]
    couple_width = couple_list.shape[1]
    near_shift = near_list - first_leaf
    couple_shift = couple_list - first_leaf
    local_ids = (near_shift + REACH).reshape(-1)
    source_ids = (couple_shift + FARR).reshape(-1)
    rimmed = near_rows(vectors, points).reshape(columns, leaves + 2 * REACH, points)
    picked = jnp.take(rimmed, local_ids, axis=1).reshape(columns, leaves, near_width, points)
    near_part = jnp.einsum(
        "lspr,qlsr->qlp", near_blocks, picked, preferred_element_type=jnp.float32
    )
    coefficients = jnp.einsum(
        "lkp,qlp->lkq", basis_t, own_rows, preferred_element_type=jnp.float32
    ).astype(jnp.bfloat16)
    coef_cycle = coef_rows(coefficients)
    partners = jnp.take(coef_cycle, source_ids, axis=0).reshape(
        leaves, couple_width, coefficients.shape[1], columns
    )
    coupled = jnp.einsum(
        "lskm,lsmq->lkq", leaf_couple, partners, preferred_element_type=jnp.float32
    )
    node_coef = jnp.einsum(
        "lkm,lkq->mq", leaf_transfer, coefficients, preferred_element_type=jnp.float32
    )
    descent = top_tree(node_coef, device, top_transfer, top_couple)
    local_far = coupled + jnp.einsum(
        "lkm,mq->lkq", leaf_transfer.astype(jnp.float32), descent, precision=lax.Precision.HIGHEST
    )
    local_far = local_far.astype(jnp.bfloat16)
    far_part = jnp.einsum("lkp,lkq->qlp", basis_t, local_far, preferred_element_type=jnp.float32)
    return (near_part + far_part).reshape(columns, leaves * points).astype(jnp.bfloat16)


def on_device(
    rhs_block,
    basis_t,
    near_blocks,
    near_list,
    leaf_transfer,
    couple_list,
    leaf_couple,
    top_transfer,
    top_couple,
):
    first_image = apply_once(
        rhs_block,
        basis_t,
        near_blocks,
        near_list,
        leaf_transfer,
        couple_list,
        leaf_couple,
        top_transfer,
        top_couple,
    )
    second_image = apply_once(
        first_image,
        basis_t,
        near_blocks,
        near_list,
        leaf_transfer,
        couple_list,
        leaf_couple,
        top_transfer,
        top_couple,
    )
    return (first_image, second_image)


def solution(mesh):
    in_specs = (
        P("rhs", "leaf"),
        P("leaf", None, None),
        P("leaf", None, None, None),
        P("leaf", None),
        P("leaf", None, None),
        P("leaf", None),
        P("leaf", None, None, None),
        P(),
        P(),
    )
    out_specs = (P("rhs", "leaf"), P("rhs", "leaf"))
    return jax.shard_map(
        on_device, mesh=mesh, in_specs=in_specs, out_specs=out_specs, check_vma=False
    )
```

profile of v0, /device:TPU:96, one launch (start us, length us, event | category | flops | bytes accessed | tf_op | source)
XLA Modules:
  0.0 242.4 jit_solution(16028633981212691088)
XLA Ops:
  7.1 6.7 %collective-permute-start.3 = (bf16[32,64,64]{2,1,0:T(8,128)(2,1)}, bf16[32,64,64]{2,1,0:T(8,128)(2,1)}, u32[]{:S(2)}, u32[]{:S(2)}) collective-permute-start(bf16[32,64,64]{2,1,0:T(8,128)(2,1)} %convolution_convert_fusion.1), channel_id=1, source_target_pairs={{2,0},{4,2},{6,4},{8,6},{10,8},{12,10},{14,12},{16,14},{18,16},{20... | collective-permute-start | bytes 786440 | tf_op jit(solution)/shard_map/ppermute | solution.py:20
  16.3 3.9 %collective-permute-start = (bf16[64,4096]{1,0:T(8,128)(2,1)}, bf16[64,4096]{1,0:T(8,128)(2,1)}, u32[]{:S(2)}, u32[]{:S(2)}) collective-permute-start(bf16[64,4096]{1,0:T(8,128)(2,1)} %get-tuple-element.23), channel_id=1, source_target_pairs={{0,2},{2,4},{4,6},{6,8},{8,10},{10,12},{12,14},{14,16},{16,18},{18... | collective-permute-start | bytes 1572872 | tf_op jit(solution)/shard_map/ppermute | solution.py:18
  20.3 6.2 %collective-permute-start.1 = (bf16[64,4096]{1,0:T(8,128)(2,1)}, bf16[64,4096]{1,0:T(8,128)(2,1)}, u32[]{:S(2)}, u32[]{:S(2)}) collective-permute-start(bf16[64,4096]{1,0:T(8,128)(2,1)} %get-tuple-element.24), channel_id=1, source_target_pairs={{2,0},{4,2},{6,4},{8,6},{10,8},{12,10},{14,12},{16,14},{18,16},{20... | collective-permute-start | bytes 1572872 | tf_op jit(solution)/shard_map/ppermute | solution.py:20
  27.0 8.1 %constant_dynamic-slice_fusion.1 = (bf16[1,64,64]{0,2,1:T(8,128)(2,1)}, bf16[1,64,64]{0,2,1:T(8,128)(2,1)}, bf16[1,64,64]{0,2,1:T(8,128)(2,1)}, bf16[1,64,64]{0,...) fusion(bf16[126,64,64]{0,2,1:T(8,128)(2,1)S(1)} %copy-done.1, ...), kind=kLoop, calls=%fused_computation.125 | loop fusion | bytes 180268 | tf_op jit(solution)/shard_map/jit(dynamic_index_in_dim)/dynamic_slice | solution.py:34
  38.9 4.7 %constant_dynamic-slice_fusion.16 = (bf16[1,64,64]{0,2,1:T(8,128)(2,1)}, bf16[1,64,64]{0,2,1:T(8,128)(2,1)}, bf16[1,64,64]{0,2,1:T(8,128)(2,1)}, bf16[1,64,64]{0...) fusion(bf16[126,64,64]{0,2,1:T(8,128)(2,1)S(1)} %copy-done.2, s32[]{:T(128)S(6)} %select_n.81, ...), kind=kLoop, calls=%fused_computation.140 | loop fusion | bytes 98328 | tf_op jit(solution)/shard_map/jit(dynamic_index_in_dim)/dynamic_slice | solution.py:34
  57.0 5.2 %collective-permute-done.5 = f32[64,64]{1,0:T(8,128)S(1)} collective-permute-done((f32[64,64]{1,0:T(8,128)S(1)}, f32[64,64]{1,0:T(8,128)S(1)}, u32[]{:S(2)}, u32[]{:S(2)}) %collective-permute-start.5) | collective-permute-done | bytes 16416 | tf_op jit(solution)/shard_map/ppermute | solution.py:30
  62.7 3.7 %collective-permute-done.6 = f32[64,64]{1,0:T(8,128)S(1)} collective-permute-done((f32[64,64]{1,0:T(8,128)S(1)}, f32[64,64]{1,0:T(8,128)S(1)}, u32[]{:S(2)}, u32[]{:S(2)}) %collective-permute-start.6) | collective-permute-done | bytes 16416 | tf_op jit(solution)/shard_map/ppermute | solution.py:30
  66.9 5.2 %collective-permute-done.7 = f32[64,64]{1,0:T(8,128)S(1)} collective-permute-done((f32[64,64]{1,0:T(8,128)S(1)}, f32[64,64]{1,0:T(8,128)S(1)}, u32[]{:S(2)}, u32[]{:S(2)}) %collective-permute-start.7) | collective-permute-done | bytes 16416 | tf_op jit(solution)/shard_map/ppermute | solution.py:30
  94.9 3.6 %gather_fusion.1 = bf16[128,64,64]{2,1,0:T(8,128)(2,1)} fusion(bf16[96,64,64]{2,1,0:T(8,128)(2,1)} %pad_maximum_fusion.2, s32[1024]{0:T(1024)S(1)} %pad_clamp_fusion), kind=kCustom, calls=%fused_computation.1.clone | custom fusion | bytes 2097664 | tf_op jit(solution)/shard_map/jit(_take)/gather | solution.py:105
  104.8 9.3 %gather_fusion = bf16[160,64,256]{2,1,0:T(8,128)(2,1)} fusion(bf16[64,64,256]{2,0,1:T(8,128)(2,1)} %bitcast.249, s32[1024]{0:T(1024)S(1)} %pad_clamp_fusion.1), kind=kCustom, calls=%fused_computation.clone | custom fusion | bytes 10486400 | tf_op jit(solution)/shard_map/jit(_take)/gather | solution.py:97
  114.1 5.3 %broadcast_select_fusion.1 = bf16[160,64,256]{2,1,0:T(8,128)(2,1)} fusion(bf16[160,64,256]{2,1,0:T(8,128)(2,1)} %gather_fusion, pred[160]{0:T(512)(128)(4,1)S(1)} %compare_and_fusion.1), kind=kLoop, calls=%fused_computation.5 | loop fusion | flops 2621440 | bytes 10485920 | tf_op jit(solution)/shard_map/jit(_take)/select_n | solution.py:97
  119.4 13.2 %fusion.83 = f32[32,64,256,1]{2,1,3,0:T(8,128)} fusion(bf16[64,32,5,256]{3,0,2,1:T(8,128)(2,1)} %bitcast.247, bf16[32,5,256,256]{3,2,1,0:T(8,128)(2,1)} %param.15), kind=kOutput, calls=%fused_computation.152 | convolution fusion | flops 1342177280 | bytes 28311552 | tf_op jit(solution)/shard_map/lspr,qlsr->qlp/dot_general | solution.py:98
  132.6 4.6 %fusion.1 = bf16[32,64,256]{2,1,0:T(8,128)(2,1)} fusion(f32[32,64,256,1]{2,1,3,0:T(8,128)} %fusion.83, bf16[32,64,256]{2,1,0:T(8,128)(2,1)S(1)} %copy-done.3, f32[32,64,64]{1,2,0:T(8,128)} %convolution_bitcast_fusion.1, bf16[32,4,64,64]{3,2,1,0:T(8,128)(2,1)} %bitcast.258, bf16[32,4,64,64]{3,2,1,0:T(8,128)(2,1)S(1)} %copy-done), kind=kOutput, calls=%fused_computation.13 | convolution fusion | flops 135528448 | bytes 6815744 | tf_op jit(solution)/shard_map/lkp,lkq->qlp/dot_general | solution.py:119
  140.9 8.1 %collective-permute-start.13 = (bf16[32,64,64]{1,2,0:T(8,128)(2,1)S(1)}, bf16[32,64,64]{1,2,0:T(8,128)(2,1)S(1)}, u32[]{:S(2)}, u32[]{:S(2)}) collective-permute-start(bf16[32,64,64]{1,2,0:T(8,128)(2,1)S(1)} %fusion.7), channel_id=1, source_target_pairs={{2,0},{4,2},{6,4},{8,6},{10,8},{12,10},{14,12},{16,14},{18,16},{20... | collective-permute-start | bytes 786440 | tf_op jit(solution)/shard_map/ppermute | solution.py:20
  159.8 3.7 %collective-permute-done.16 = f32[64,64]{1,0:T(8,128)S(1)} collective-permute-done((f32[64,64]{1,0:T(8,128)S(1)}, f32[64,64]{1,0:T(8,128)S(1)}, u32[]{:S(2)}, u32[]{:S(2)}) %collective-permute-start.16) | collective-permute-done | bytes 16416 | tf_op jit(solution)/shard_map/ppermute | solution.py:30
  164.0 5.2 %collective-permute-done.17 = f32[64,64]{1,0:T(8,128)S(1)} collective-permute-done((f32[64,64]{1,0:T(8,128)S(1)}, f32[64,64]{1,0:T(8,128)S(1)}, u32[]{:S(2)}, u32[]{:S(2)}) %collective-permute-start.17) | collective-permute-done | bytes 16416 | tf_op jit(solution)/shard_map/ppermute | solution.py:30
  169.7 3.7 %collective-permute-done.18 = f32[64,64]{1,0:T(8,128)S(1)} collective-permute-done((f32[64,64]{1,0:T(8,128)S(1)}, f32[64,64]{1,0:T(8,128)S(1)}, u32[]{:S(2)}, u32[]{:S(2)}) %collective-permute-start.18) | collective-permute-done | bytes 16416 | tf_op jit(solution)/shard_map/ppermute | solution.py:30
  173.6 7.4 %collective-permute-start.19 = (f32[64,64]{1,0:T(8,128)S(1)}, f32[64,64]{1,0:T(8,128)S(1)}, u32[]{:S(2)}, u32[]{:S(2)}) collective-permute-start(f32[64,64]{1,0:T(8,128)S(1)} %convolution_add_fusion.1), channel_id=1, source_target_pairs={{0,64},{2,66},{4,68},{6,70},{8,72},{10,74},{12,76},{14,78},{16,80}... | collective-permute-start | bytes 49160 | tf_op jit(solution)/shard_map/ppermute | solution.py:30
  184.0 8.1 %collective-permute-start.11 = (bf16[64,4096]{1,0:T(8,128)(2,1)}, bf16[64,4096]{1,0:T(8,128)(2,1)}, u32[]{:S(2)}, u32[]{:S(2)}) collective-permute-start(bf16[64,4096]{1,0:T(8,128)(2,1)} %get-tuple-element.5), channel_id=1, source_target_pairs={{2,0},{4,2},{6,4},{8,6},{10,8},{12,10},{14,12},{16,14},{18,16},{20... | collective-permute-start | bytes 1572872 | tf_op jit(solution)/shard_map/ppermute | solution.py:20
  198.0 3.6 %gather_fusion.3 = bf16[128,64,64]{1,2,0:T(8,128)(2,1)} fusion(bf16[96,64,64]{1,2,0:T(8,128)(2,1)} %pad_maximum_fusion.3, s32[1024]{0:T(1024)S(1)} %pad_clamp_fusion), kind=kCustom, calls=%fused_computation.3.clone | custom fusion | bytes 2097664 | tf_op jit(solution)/shard_map/jit(_take)/gather | solution.py:105
  207.8 9.3 %gather_fusion.2 = bf16[160,64,256]{2,1,0:T(8,128)(2,1)} fusion(bf16[64,64,256]{2,0,1:T(8,128)(2,1)} %bitcast.248, s32[1024]{0:T(1024)S(1)} %pad_clamp_fusion.1), kind=kCustom, calls=%fused_computation.2.clone | custom fusion | bytes 10486400 | tf_op jit(solution)/shard_map/jit(_take)/gather | solution.py:97
  217.1 5.3 %broadcast_select_fusion = bf16[160,64,256]{2,1,0:T(8,128)(2,1)} fusion(bf16[160,64,256]{2,1,0:T(8,128)(2,1)} %gather_fusion.2, pred[160]{0:T(512)(128)(4,1)S(1)} %compare_and_fusion.1), kind=kLoop, calls=%fused_computation.4 | loop fusion | flops 2621440 | bytes 10485920 | tf_op jit(solution)/shard_map/jit(_take)/select_n | solution.py:97
  222.5 13.2 %fusion.85 = f32[32,64,256,1]{2,1,3,0:T(8,128)} fusion(bf16[64,32,5,256]{3,0,2,1:T(8,128)(2,1)} %bitcast.246, bf16[32,5,256,256]{3,2,1,0:T(8,128)(2,1)} %param.15), kind=kOutput, calls=%fused_computation.154 | convolution fusion | flops 1342177280 | bytes 28311552 | tf_op jit(solution)/shard_map/lspr,qlsr->qlp/dot_general | solution.py:98
  235.6 4.5 %fusion.2 = bf16[32,8,8,256]{3,2,1,0:T(8,128)(2,1)} fusion(bf16[32,64,256]{2,1,0:T(8,128)(2,1)S(1)} %copy-done.3, f32[32,64,256,1]{2,1,3,0:T(8,128)} %fusion.85, f32[32,64,64]{1,2,0:T(8,128)} %convolution_bitcast_fusion, bf16[32,4,64,64]{2,3,1,0:T(8,128)(2,1)} %bitcast.257, bf16[32,4,64,64]{3,2,1,0:T(8,128)(2,1)S(1)} %copy-done), kind=kOutput, calls=%fused_computation.20 | convolution fusion | flops 135528448 | bytes 6815744 | tf_op jit(solution)/shard_map/lkp,lkq->qlp/dot_general | solution.py:119
  (160 shorter events, 89.3 us)
Async XLA Ops:
  0.6 132.0 %copy-start = (bf16[32,4,64,64]{3,2,1,0:T(8,128)(2,1)S(1)}, bf16[32,4,64,64]{3,2,1,0:T(8,128)(2,1)}, u32[]{:S(2)}) copy-start(bf16[32,4,64,64]{3,2,1,0:T(8,128)(2,1)} %param.19) | copy-start | bytes 3145732
  3.6 23.3 %copy-start.1 = (bf16[126,64,64]{0,2,1:T(8,128)(2,1)S(1)}, bf16[126,64,64]{0,2,1:T(8,128)(2,1)}, u32[]{:S(2)}) copy-start(bf16[126,64,64]{0,2,1:T(8,128)(2,1)} %param.20) | copy-start | bytes 3096580
  3.6 88.4 %collective-permute-start.2 = (bf16[32,64,64]{2,1,0:T(8,128)(2,1)}, bf16[32,64,64]{2,1,0:T(8,128)(2,1)}, u32[]{:S(2)}, u32[]{:S(2)}) collective-permute-start(bf16[32,64,64]{2,1,0:T(8,128)(2,1)} %convolution_convert_fusion.1), channel_id=1, source_target_pairs={{0,2},{2,4},{4,6},{6,8},{8,10},{10,12},{12,14},{14,16},{16,18},{18... | collective-permute-start | bytes 786440 | tf_op jit(solution)/shard_map/ppermute | solution.py:18
  7.1 84.9 %collective-permute-start.3 = (bf16[32,64,64]{2,1,0:T(8,128)(2,1)}, bf16[32,64,64]{2,1,0:T(8,128)(2,1)}, u32[]{:S(2)}, u32[]{:S(2)}) collective-permute-start(bf16[32,64,64]{2,1,0:T(8,128)(2,1)} %convolution_convert_fusion.1), channel_id=1, source_target_pairs={{2,0},{4,2},{6,4},{8,6},{10,8},{12,10},{14,12},{16,14},{18,16},{20... | collective-permute-start | bytes 786440 | tf_op jit(solution)/shard_map/ppermute | solution.py:20
  15.2 41.2 %collective-permute-start.4 = (f32[64,64]{0,1:T(8,128)S(1)}, f32[64,64]{0,1:T(8,128)S(1)}, u32[]{:S(2)}, u32[]{:S(2)}) collective-permute-start(f32[64,64]{0,1:T(8,128)S(1)} %bitcast.260), channel_id=1, source_target_pairs={{0,2},{2,0},{4,6},{6,4},{8,10},{10,8},{12,14},{14,12},{16,18},{18,... | collective-permute-start | bytes 49160 | tf_op jit(solution)/shard_map/ppermute | solution.py:30
  16.3 85.5 %collective-permute-start = (bf16[64,4096]{1,0:T(8,128)(2,1)}, bf16[64,4096]{1,0:T(8,128)(2,1)}, u32[]{:S(2)}, u32[]{:S(2)}) collective-permute-start(bf16[64,4096]{1,0:T(8,128)(2,1)} %get-tuple-element.23), channel_id=1, source_target_pairs={{0,2},{2,4},{4,6},{6,8},{8,10},{10,12},{12,14},{14,16},{16,18},{18... | collective-permute-start | bytes 1572872 | tf_op jit(solution)/shard_map/ppermute | solution.py:18
  20.3 81.6 %collective-permute-start.1 = (bf16[64,4096]{1,0:T(8,128)(2,1)}, bf16[64,4096]{1,0:T(8,128)(2,1)}, u32[]{:S(2)}, u32[]{:S(2)}) collective-permute-start(bf16[64,4096]{1,0:T(8,128)(2,1)} %get-tuple-element.24), channel_id=1, source_target_pairs={{2,0},{4,2},{6,4},{8,6},{10,8},{12,10},{14,12},{16,14},{18,16},{20... | collective-permute-start | bytes 1572872 | tf_op jit(solution)/shard_map/ppermute | solution.py:20
  56.4 24.9 %copy-start.14 = (bf16[1,64,64]{0,2,1:T(8,128)(2,1)S(1)}, bf16[1,64,64]{0,2,1:T(8,128)(2,1)}, u32[]{:S(2)}) copy-start(bf16[1,64,64]{0,2,1:T(8,128)(2,1)} %get-tuple-element.8) | copy-start | bytes 24580
  56.7 5.5 %collective-permute-start.5 = (f32[64,64]{1,0:T(8,128)S(1)}, f32[64,64]{1,0:T(8,128)S(1)}, u32[]{:S(2)}, u32[]{:S(2)}) collective-permute-start(f32[64,64]{1,0:T(8,128)S(1)} %convolution_add_fusion.20), channel_id=1, source_target_pairs={{0,4},{2,6},{4,0},{6,2},{8,12},{10,14},{12,8},{14,10},{16,20},{18,... | collective-permute-start | bytes 49160 | tf_op jit(solution)/shard_map/ppermute | solution.py:30
  62.4 4.0 %collective-permute-start.6 = (f32[64,64]{1,0:T(8,128)S(1)}, f32[64,64]{1,0:T(8,128)S(1)}, u32[]{:S(2)}, u32[]{:S(2)}) collective-permute-start(f32[64,64]{1,0:T(8,128)S(1)} %convolution_add_fusion.18), channel_id=1, source_target_pairs={{0,8},{2,10},{4,12},{6,14},{8,0},{10,2},{12,4},{14,6},{16,24},{18,... | collective-permute-start | bytes 49160 | tf_op jit(solution)/shard_map/ppermute | solution.py:30
  66.6 5.5 %collective-permute-start.7 = (f32[64,64]{1,0:T(8,128)S(1)}, f32[64,64]{1,0:T(8,128)S(1)}, u32[]{:S(2)}, u32[]{:S(2)}) collective-permute-start(f32[64,64]{1,0:T(8,128)S(1)} %convolution_add_fusion.16), channel_id=1, source_target_pairs={{0,16},{2,18},{4,20},{6,22},{8,24},{10,26},{12,28},{14,30},{16,0},... | collective-permute-start | bytes 49160 | tf_op jit(solution)/shard_map/ppermute | solution.py:30
  72.3 4.0 %collective-permute-start.8 = (f32[64,64]{1,0:T(8,128)S(1)}, f32[64,64]{1,0:T(8,128)S(1)}, u32[]{:S(2)}, u32[]{:S(2)}) collective-permute-start(f32[64,64]{1,0:T(8,128)S(1)} %convolution_add_fusion.14), channel_id=1, source_target_pairs={{0,32},{2,34},{4,36},{6,38},{8,40},{10,42},{12,44},{14,46},{16,48}... | collective-permute-start | bytes 49160 | tf_op jit(solution)/shard_map/ppermute | solution.py:30
  77.1 9.8 %collective-permute-start.9 = (f32[64,64]{1,0:T(8,128)}, f32[64,64]{1,0:T(8,128)}, u32[]{:S(2)}, u32[]{:S(2)}) collective-permute-start(f32[64,64]{1,0:T(8,128)} %convolution_add_fusion.12), channel_id=1, source_target_pairs={{0,64},{2,66},{4,68},{6,70},{8,72},{10,74},{12,76},{14,78},{16,80}... | collective-permute-start | bytes 49160 | tf_op jit(solution)/shard_map/ppermute | solution.py:30
  139.0 57.5 %collective-permute-start.12 = (bf16[32,64,64]{1,2,0:T(8,128)(2,1)S(1)}, bf16[32,64,64]{1,2,0:T(8,128)(2,1)S(1)}, u32[]{:S(2)}, u32[]{:S(2)}) collective-permute-start(bf16[32,64,64]{1,2,0:T(8,128)(2,1)S(1)} %fusion.7), channel_id=1, source_target_pairs={{0,2},{2,4},{4,6},{6,8},{8,10},{10,12},{12,14},{14,16},{16,18},{18... | collective-permute-start | bytes 786440 | tf_op jit(solution)/shard_map/ppermute | solution.py:18
  140.9 55.6 %collective-permute-start.13 = (bf16[32,64,64]{1,2,0:T(8,128)(2,1)S(1)}, bf16[32,64,64]{1,2,0:T(8,128)(2,1)S(1)}, u32[]{:S(2)}, u32[]{:S(2)}) collective-permute-start(bf16[32,64,64]{1,2,0:T(8,128)(2,1)S(1)} %fusion.7), channel_id=1, source_target_pairs={{2,0},{4,2},{6,4},{8,6},{10,8},{12,10},{14,12},{16,14},{18,16},{20... | collective-permute-start | bytes 786440 | tf_op jit(solution)/shard_map/ppermute | solution.py:20
  149.3 4.0 %collective-permute-start.14 = (f32[64,64]{0,1:T(8,128)S(1)}, f32[64,64]{0,1:T(8,128)S(1)}, u32[]{:S(2)}, u32[]{:S(2)}) collective-permute-start(f32[64,64]{0,1:T(8,128)S(1)} %bitcast.261), channel_id=1, source_target_pairs={{0,2},{2,0},{4,6},{6,4},{8,10},{10,8},{12,14},{14,12},{16,18},{18,... | collective-permute-start | bytes 49160 | tf_op jit(solution)/shard_map/ppermute | solution.py:30
  149.7 46.7 %copy-start.7 = (bf16[32,8,8,256]{3,2,0,1:T(8,128)(2,1)}, bf16[32,8,8,256]{3,2,0,1:T(8,128)(2,1)S(1)}, u32[]{:S(2)}) copy-start(bf16[32,8,8,256]{3,2,0,1:T(8,128)(2,1)S(1)} %copy.97) | copy-start | bytes 3145732
  153.6 5.7 %collective-permute-start.15 = (f32[64,64]{1,0:T(8,128)S(1)}, f32[64,64]{1,0:T(8,128)S(1)}, u32[]{:S(2)}, u32[]{:S(2)}) collective-permute-start(f32[64,64]{1,0:T(8,128)S(1)} %convolution_add_fusion.9), channel_id=1, source_target_pairs={{0,4},{2,6},{4,0},{6,2},{8,12},{10,14},{12,8},{14,10},{16,20},{18,... | collective-permute-start | bytes 49160 | tf_op jit(solution)/shard_map/ppermute | solution.py:30
  159.5 4.0 %collective-permute-start.16 = (f32[64,64]{1,0:T(8,128)S(1)}, f32[64,64]{1,0:T(8,128)S(1)}, u32[]{:S(2)}, u32[]{:S(2)}) collective-permute-start(f32[64,64]{1,0:T(8,128)S(1)} %convolution_add_fusion.7), channel_id=1, source_target_pairs={{0,8},{2,10},{4,12},{6,14},{8,0},{10,2},{12,4},{14,6},{16,24},{18,... | collective-permute-start | bytes 49160 | tf_op jit(solution)/shard_map/ppermute | solution.py:30
  163.7 5.5 %collective-permute-start.17 = (f32[64,64]{1,0:T(8,128)S(1)}, f32[64,64]{1,0:T(8,128)S(1)}, u32[]{:S(2)}, u32[]{:S(2)}) collective-permute-start(f32[64,64]{1,0:T(8,128)S(1)} %convolution_add_fusion.5), channel_id=1, source_target_pairs={{0,16},{2,18},{4,20},{6,22},{8,24},{10,26},{12,28},{14,30},{16,0},... | collective-permute-start | bytes 49160 | tf_op jit(solution)/shard_map/ppermute | solution.py:30
  169.4 4.0 %collective-permute-start.18 = (f32[64,64]{1,0:T(8,128)S(1)}, f32[64,64]{1,0:T(8,128)S(1)}, u32[]{:S(2)}, u32[]{:S(2)}) collective-permute-start(f32[64,64]{1,0:T(8,128)S(1)} %convolution_add_fusion.3), channel_id=1, source_target_pairs={{0,32},{2,34},{4,36},{6,38},{8,40},{10,42},{12,44},{14,46},{16,48}... | collective-permute-start | bytes 49160 | tf_op jit(solution)/shard_map/ppermute | solution.py:30
  173.6 18.5 %collective-permute-start.19 = (f32[64,64]{1,0:T(8,128)S(1)}, f32[64,64]{1,0:T(8,128)S(1)}, u32[]{:S(2)}, u32[]{:S(2)}) collective-permute-start(f32[64,64]{1,0:T(8,128)S(1)} %convolution_add_fusion.1), channel_id=1, source_target_pairs={{0,64},{2,66},{4,68},{6,70},{8,72},{10,74},{12,76},{14,78},{16,80}... | collective-permute-start | bytes 49160 | tf_op jit(solution)/shard_map/ppermute | solution.py:30
  182.1 22.8 %collective-permute-start.10 = (bf16[64,4096]{1,0:T(8,128)(2,1)}, bf16[64,4096]{1,0:T(8,128)(2,1)}, u32[]{:S(2)}, u32[]{:S(2)}) collective-permute-start(bf16[64,4096]{1,0:T(8,128)(2,1)} %get-tuple-element.4), channel_id=1, source_target_pairs={{0,2},{2,4},{4,6},{6,8},{8,10},{10,12},{12,14},{14,16},{16,18},{18... | collective-permute-start | bytes 1572872 | tf_op jit(solution)/shard_map/ppermute | solution.py:18
  184.0 20.9 %collective-permute-start.11 = (bf16[64,4096]{1,0:T(8,128)(2,1)}, bf16[64,4096]{1,0:T(8,128)(2,1)}, u32[]{:S(2)}, u32[]{:S(2)}) collective-permute-start(bf16[64,4096]{1,0:T(8,128)(2,1)} %get-tuple-element.5), channel_id=1, source_target_pairs={{2,0},{4,2},{6,4},{8,6},{10,8},{12,10},{14,12},{16,14},{18,16},{20... | collective-permute-start | bytes 1572872 | tf_op jit(solution)/shard_map/ppermute | solution.py:20
  (17 other events, 167.0 us)
where the time goes:
time: 244 us; the launch traced here: 242 us
  local copies, waits for them, and re-layouts  71.9 us (29%)
  matrix products  55.9 us (23%)
  starting transfers between devices  51.8 us (21%)
  waiting for transfers between devices  37 us (15%)
  other arithmetic  24.4 us (10%)
    ppermute x12, waiting for transfers between devices, swapped(): return lax.ppermute(value, axis, pairs)  37 us
    ppermute x4, starting transfers between devices, extended(): lax.ppermute(head, axis, [((i + 1) % count, i) for i in range(ends)])  29.1 us
    dot_general x2, matrix products, apply_once(): jnp.einsum('lspr,qlsr->qlp', near_blocks, picked, preferred_element_type=...  26.4 us
    unnamed x59, local copies, waits for them, and re-layouts  25.3 us
    gather x2, local copies, waits for them, and re-layouts, apply_once(): jnp.take(rimmed, local_ids, axis=1)  18.6 us
    dynamic_slice x2, local copies, waits for them, and re-layouts, pick_row(): return lax.dynamic_index_in_dim(table, row_id, 0, keepdims=False)  12.7 us
    ppermute x12, starting transfers between devices, swapped(): return lax.ppermute(value, axis, pairs)  11.5 us
    ppermute x4, starting transfers between devices, extended(): lax.ppermute(tail, axis, [(i, (i + 1) % count) for i in range(ends)])  11.3 us
  transfers between devices with their start and end apart: 20, of which 9 were waited for; matrix products, arithmetic and copies ran while one was open for 31% of the time, Pallas kernels for 0%

commit v1 on v0

v1 whole, which is shorter than its diff:
```python
import jax
import jax.numpy as jnp
from jax import lax
from jax.experimental import pallas as pl
from jax.experimental.pallas import tpu as pltpu
from jax.sharding import PartitionSpec as P

REACH = 16
FARR = 32
BF = jnp.bfloat16
F32 = jnp.float32
NT = (((1,), (1,)), ((), ()))
NN = (((1,), (0,)), ((), ()))


def mm(a, b, dims=NN):
    return lax.dot_general(a, b, dims, preferred_element_type=F32)


def exact(a, b, dims=NN):
    return lax.dot_general(
        a, b, dims, precision=lax.Precision.HIGHEST, preferred_element_type=F32
    )


def params(mib, *semantics):
    return pltpu.CompilerParams(
        vmem_limit_bytes=mib * 2**20, dimension_semantics=semantics or None
    )


def head_body(v, basis, trans, left, right, coef, node, acc):
    step = pl.program_id(0)
    steps = pl.num_programs(0)
    points = basis.shape[2]

    @pl.when(step == 0)
    def _():
        acc[...] = jnp.zeros_like(acc)

    @pl.when(step < steps // 2)
    def _():
        left[...] = v[...]

    @pl.when(step >= steps // 2)
    def _():
        right[...] = v[...]

    total = acc[...]
    for pair in range(basis.shape[0] // 2):
        parts = [
            mm(v[:, leaf * points : (leaf + 1) * points], basis[leaf], NT)
            for leaf in (2 * pair, 2 * pair + 1)
        ]
        both = jnp.concatenate(parts, axis=1).astype(BF)
        width = both.shape[1]
        coef[:, pair * width : (pair + 1) * width] = both
        total += mm(both, trans[pair * width : (pair + 1) * width, :])
    acc[...] = total
    node[...] = total


def head(vectors, basis_t, trans2):
    columns, own = vectors.shape
    leaves, rank, points = basis_t.shape
    steps = 4
    wide = own // steps
    some = leaves // steps
    half = steps // 2
    return pl.pallas_call(
        head_body,
        grid=(steps,),
        in_specs=[
            pl.BlockSpec((columns, wide), lambda i: (0, i)),
            pl.BlockSpec((some, rank, points), lambda i: (i, 0, 0)),
            pl.BlockSpec((some * rank, rank), lambda i: (i, 0)),
        ],
        out_specs=[
            pl.BlockSpec((columns, wide), lambda i: (0, jnp.minimum(i, half - 1))),
            pl.BlockSpec((columns, wide), lambda i: (0, jnp.maximum(i - half, 0))),
            pl.BlockSpec((columns, some * rank), lambda i: (0, i)),
            pl.BlockSpec((columns, rank), lambda i: (0, 0)),
        ],
        out_shape=[
            jax.ShapeDtypeStruct((columns, own // 2), BF),
            jax.ShapeDtypeStruct((columns, own // 2), BF),
            jax.ShapeDtypeStruct((columns, leaves * rank), BF),
            jax.ShapeDtypeStruct((columns, rank), F32),
        ],
        scratch_shapes=[pltpu.VMEM((columns, rank), F32)],
        compiler_params=params(60, "arbitrary"),
        cost_estimate=pl.CostEstimate(
            flops=200_000_000, bytes_accessed=6_000_000, transcendentals=0
        ),
        name="head",
    )(vectors, basis_t, trans2)


def table_body(levels, trans, couple, up, down, own, pair, sems):
    device = lax.axis_index("leaf")
    copies = []
    for t in range(levels):
        offset = 2 * (1 << levels) - 2 * ((1 << levels) >> t)
        here = offset + (device >> t)
        there = offset + ((device >> t) ^ 1)
        copies.append(pltpu.make_async_copy(trans.at[here], own.at[t, 0], sems.at[3 * t]))
        copies.append(pltpu.make_async_copy(trans.at[there], own.at[t, 1], sems.at[3 * t + 1]))
        copies.append(pltpu.make_async_copy(couple.at[here], pair.at[t], sems.at[3 * t + 2]))
    for copy in copies:
        copy.start()
    for copy in copies:
        copy.wait()
    up[...] = own[...].astype(F32)
    down[0] = pair[0].astype(F32)
    path = own[0, 0].astype(F32)
    for t in range(1, levels):
        down[t] = exact(path, pair[t].astype(F32))
        if t + 1 < levels:
            path = exact(path, own[t, 0].astype(F32))


def table(top_transfer, top_couple):
    rank = top_transfer.shape[1]
    devices = lax.axis_size("leaf")
    levels = devices.bit_length() - 1
    return pl.pallas_call(
        lambda *refs: table_body(levels, *refs),
        in_specs=[pl.BlockSpec(memory_space=pl.ANY)] * 2,
        out_specs=[pl.BlockSpec(memory_space=pltpu.VMEM)] * 2,
        out_shape=[
            jax.ShapeDtypeStruct((levels, 2, rank, rank), F32),
            jax.ShapeDtypeStruct((levels, rank, rank), F32),
        ],
        scratch_shapes=[
            pltpu.VMEM((levels, 2, rank, rank), BF),
            pltpu.VMEM((levels, rank, rank), BF),
            pltpu.SemaphoreType.DMA((3 * levels,)),
        ],
        compiler_params=params(60),
        cost_estimate=pl.CostEstimate(
            flops=10_000_000, bytes_accessed=3_000_000, transcendentals=0
        ),
        name="table",
    )(top_transfer, top_couple)


def tail_body(more, *refs):
    (near_list, couple_list, own_l, own_r, halo_l, halo_r, coef_own, coef_l, coef_r) = refs[:9]
    (top, near, basis, trans, couple) = refs[9:14]
    if more:
        image, left, right, coef, node = refs[14:19]
        wide, table_ref, descent, acc, sems = refs[19:]
    else:
        (image,) = refs[14:15]
        wide, table_ref, descent, sems = refs[15:]
    step = pl.program_id(0)
    steps = pl.num_programs(0)
    some = near.shape[0]
    points = basis.shape[2]
    rank = basis.shape[1]
    leaves = some * steps
    first = lax.axis_index("leaf") * leaves
    half = own_l.shape[1]

    @pl.when(step == 0)
    def _():
        copies = [
            pltpu.make_async_copy(ref, wide.at[:, i * half : (i + 1) * half], sems.at[i])
            for i, ref in enumerate((halo_l, own_l, own_r, halo_r))
        ]
        for copy in copies:
            copy.start()
        for part, ref in enumerate((coef_l, coef_own, coef_r)):
            for pair in range(leaves // 2):
                both = ref[:, 2 * rank * pair : 2 * rank * (pair + 1)]
                table_ref[part * leaves + 2 * pair] = both[:, :rank]
                table_ref[part * leaves + 2 * pair + 1] = both[:, rank:]
        high = top[...].astype(BF)
        descent[0] = high
        descent[1] = (top[...] - high.astype(F32)).astype(BF)
        if more:
            acc[...] = jnp.zeros_like(acc)
        for copy in copies:
            copy.wait()

    results = []
    for i in range(some):
        leaf = step * some + i
        moved = trans[i * rank : (i + 1) * rank, :]
        local = mm(descent[0], moved, NT) + mm(descent[1], moved, NT)
        for s in range(couple.shape[1]):
            source = couple_list[leaf, s] - first + FARR
            local += mm(table_ref[source], couple[i, s], NT)
        total = mm(local.astype(BF), basis[i])
        for s in range(near.shape[1]):
            source = near_list[leaf, s] - first + REACH
            start = pl.multiple_of(source * points, points)
            total += mm(wide[:, pl.ds(start, points)], near[i, s], NT)
        results.append(total.astype(BF))
        image[:, i * points : (i + 1) * points] = results[i]

    if more:
        @pl.when(step < steps // 2)
        def _():
            for i in range(some):
                left[:, i * points : (i + 1) * points] = results[i]

        @pl.when(step >= steps // 2)
        def _():
            for i in range(some):
                right[:, i * points : (i + 1) * points] = results[i]

        total = acc[...]
        for pair in range(some // 2):
            parts = [mm(results[i], basis[i], NT) for i in (2 * pair, 2 * pair + 1)]
            both = jnp.concatenate(parts, axis=1).astype(BF)
            width = both.shape[1]
            coef[:, pair * width : (pair + 1) * width] = both
            total += mm(both, trans[pair * width : (pair + 1) * width, :])
        acc[...] = total
        node[...] = total


def tail(more, lists, halves, halos, coefs, top, near_blocks, basis_t, trans2, leaf_couple):
    columns, half_wide = halves[0].shape
    leaves, rank, points = basis_t.shape
    kn = near_blocks.shape[1]
    kc = leaf_couple.shape[1]
    some = 2
    steps = leaves // some
    half = steps // 2
    anywhere = pl.BlockSpec(memory_space=pl.ANY)
    whole = pl.BlockSpec((columns, leaves * rank), lambda i, *_: (0, 0))
    in_specs = (
        [anywhere] * 4
        + [whole] * 3
        + [
            pl.BlockSpec((columns, rank), lambda i, *_: (0, 0)),
            pl.BlockSpec((some, kn, points, points), lambda i, *_: (i, 0, 0, 0)),
            pl.BlockSpec((some, rank, points), lambda i, *_: (i, 0, 0)),
            pl.BlockSpec((some * rank, rank), lambda i, *_: (i, 0)),
            pl.BlockSpec((some, kc, rank, rank), lambda i, *_: (i, 0, 0, 0)),
        ]
    )
    out_specs = [pl.BlockSpec((columns, some * points), lambda i, *_: (0, i))]
    out_shape = [jax.ShapeDtypeStruct((columns, leaves * points), BF)]
    scratch = [
        pltpu.VMEM((columns, 4 * half_wide), BF),
        pltpu.VMEM((3 * leaves, columns, rank), BF),
        pltpu.VMEM((2, columns, rank), BF),
    ]
    if more:
        out_specs += [
            pl.BlockSpec((columns, some * points), lambda i, *_: (0, jnp.minimum(i, half - 1))),
            pl.BlockSpec((columns, some * points), lambda i, *_: (0, jnp.maximum(i - half, 0))),
            pl.BlockSpec((columns, some * rank), lambda i, *_: (0, i)),
            pl.BlockSpec((columns, rank), lambda i, *_: (0, 0)),
        ]
        out_shape += [
            jax.ShapeDtypeStruct((columns, half_wide), BF),
            jax.ShapeDtypeStruct((columns, half_wide), BF),
            jax.ShapeDtypeStruct((columns, leaves * rank), BF),
            jax.ShapeDtypeStruct((columns, rank), F32),
        ]
        scratch.append(pltpu.VMEM((columns, rank), F32))
    scratch.append(pltpu.SemaphoreType.DMA((4,)))
    return pl.pallas_call(
        lambda *refs: tail_body(more, *refs),
        grid_spec=pltpu.PrefetchScalarGridSpec(
            num_scalar_prefetch=2,
            grid=(steps,),
            in_specs=in_specs,
            out_specs=out_specs,
            scratch_shapes=scratch,
        ),
        out_shape=out_shape,
        compiler_params=params(44, "arbitrary"),
        cost_estimate=pl.CostEstimate(
            flops=1_700_000_000, bytes_accessed=30_000_000, transcendentals=0
        ),
        name="tail",
    )(*lists, *halves, *halos, *coefs, top, near_blocks, basis_t, trans2, leaf_couple)


def from_left(value):
    ends = lax.axis_size("leaf") - 1
    return lax.ppermute(value, "leaf", [(i, i + 1) for i in range(ends)])


def from_right(value):
    ends = lax.axis_size("leaf") - 1
    return lax.ppermute(value, "leaf", [(i + 1, i) for i in range(ends)])


def swapped(value, mask):
    return lax.ppermute(value, "leaf", [(i, i ^ mask) for i in range(lax.axis_size("leaf"))])


def exchange(left, right, coef, node, up, down):
    levels = up.shape[0]
    top = jnp.zeros_like(node)
    held = None
    for t in range(levels):
        mask = (1 << t) if t % 2 == 0 else 3 << (t - 1)
        other = swapped(node, mask)
        top += exact(other, down[t], NT)
        if t == 1:
            left, right, coef, other = lax.optimization_barrier((left, right, coef, other))
            held = (from_left(right), from_right(left), from_left(coef), from_right(coef))
        if t + 1 < levels:
            node = exact(node, up[t, 0]) + exact(other, up[t, 1])
    return top, held[:2], (held[2], coef, held[3])


def on_device(
    rhs_block,
    basis_t,
    near_blocks,
    near_list,
    leaf_transfer,
    couple_list,
    leaf_couple,
    top_transfer,
    top_couple,
):
    leaves, rank, _ = leaf_transfer.shape
    trans2 = leaf_transfer.reshape(leaves * rank, rank)
    lists = (near_list, couple_list)
    fixed = (near_blocks, basis_t, trans2, leaf_couple)
    up, down = table(top_transfer, top_couple)
    left, right, coef, node = head(rhs_block, basis_t, trans2)
    top, halos, coefs = exchange(left, right, coef, node, up, down)
    first_image, left, right, coef, node = tail(
        True, lists, (left, right), halos, (coefs[1], coefs[0], coefs[2]), top, *fixed
    )
    top, halos, coefs = exchange(left, right, coef, node, up, down)
    (second_image,) = tail(
        False, lists, (left, right), halos, (coefs[1], coefs[0], coefs[2]), top, *fixed
    )
    return (first_image, second_image)


def solution(mesh):
    in_specs = (
        P("rhs", "leaf"),
        P("leaf", None, None),
        P("leaf", None, None, None),
        P("leaf", None),
        P("leaf", None, None),
        P("leaf", None),
        P("leaf", None, None, None),
        P(),
        P(),
    )
    out_specs = (P("rhs", "leaf"), P("rhs", "leaf"))
    return jax.shard_map(
        on_device, mesh=mesh, in_specs=in_specs, out_specs=out_specs, check_vma=False
    )
```

time: 244 us -> 165 us (0.68)
  the two profiles are of different devices: /device:TPU:96 before, /device:TPU:30 now
where the time goes in v1:
time: 165 us; the launch traced here: 162 us
  starting transfers between devices  55.6 us (34%)
  Pallas kernels  51.4 us (31%)
  waiting for transfers between devices  28.2 us (17%)
  matrix products  17.7 us (11%)
  local copies, waits for them, and re-layouts  8.31 us (5%)
    pallas_call x2, Pallas kernels, tail(): pl.pallas_call(lambda *refs: tail_body(more, *refs), grid_spec=pltpu.Pref...  43.2 us
    ppermute x12, waiting for transfers between devices, swapped(): lax.ppermute(value, 'leaf', [(i, i ^ mask) for i in range(lax.axis_size('...  28.2 us
    ppermute x12, starting transfers between devices, swapped(): lax.ppermute(value, 'leaf', [(i, i ^ mask) for i in range(lax.axis_size('...  24.8 us
    ppermute x4, starting transfers between devices, from_left(): return lax.ppermute(value, 'leaf', [(i, i + 1) for i in range(ends)])  21.1 us
    dot_general x32, matrix products, exact(): lax.dot_general(a, b, dims, precision=lax.Precision.HIGHEST, preferred_el...  17.7 us
    ppermute x4, starting transfers between devices, from_right(): return lax.ppermute(value, 'leaf', [(i + 1, i) for i in range(ends)])  9.68 us
    unnamed x30, local copies, waits for them, and re-layouts  8.31 us
    pallas_call x1, Pallas kernels, head(): pl.pallas_call(head_body, grid=(steps,), in_specs=[pl.BlockSpec((columns,...  5.32 us
  transfers between devices with their start and end apart: 20, of which 8 were waited for; matrix products, arithmetic and copies ran while one was open for 14% of the time, Pallas kernels for 2%

profile of v1, /device:TPU:30, one launch (start us, length us, event | category | flops | bytes accessed | tf_op | source)
XLA Modules:
  0.0 162.4 jit_solution(9733711337506915315)
XLA Ops:
  0.6 5.3 %head.1 = (bf16[64,4096]{1,0:T(8,128)(2,1)}, bf16[64,4096]{1,0:T(8,128)(2,1)}, bf16[64,2048]{1,0:T(8,128)(2,1)}, f32[64,64]{1,0:T(8,128)}) custom-call(bf16[64,8192]{1,0:T(8,128)(2,1)} %v.1, bf16[32,64,256]{2,1,0:T(8,128)(2,1)} %refs_11_.3, bf16[2048,64]{1,0:T(8,128)(2,1)} %bitcast.113), custom_call_target="tpu_custom_call" | custom-call | flops 200000000 | bytes 6000000 | tf_op jit(solution)/shard_map/head/pallas_call | solution.py:70
  6.9 4.1 %copy.11.refs_0_ = bf16[126,64,64]{2,1,0:T(8,128)(2,1)} copy(bf16[126,64,64]{0,2,1:T(8,128)(2,1)S(1)} %copy-done.7) | data formatting | bytes 2064384 | tf_op args[7]
  11.0 4.0 %copy.12.refs_1_ = bf16[126,64,64]{2,1,0:T(8,128)(2,1)} copy(bf16[126,64,64]{0,2,1:T(8,128)(2,1)S(1)} %copy-done.8) | data formatting | bytes 2064384 | tf_op args[8]
  15.0 2.8 %table.1 = (f32[6,2,64,64]{3,2,1,0:T(8,128)}, f32[6,64,64]{2,1,0:T(8,128)}) custom-call(bf16[126,64,64]{2,1,0:T(8,128)(2,1)} %copy.11.refs_0_, bf16[126,64,64]{2,1,0:T(8,128)(2,1)} %copy.12.refs_1_), custom_call_target="tpu_custom_call" | custom-call | flops 10000000 | bytes 3000000 | tf_op jit(solution)/shard_map/table/pallas_call | solution.py:126
  22.2 3.1 %collective-permute-done.1 = f32[64,64]{1,0:T(8,128)S(1)} collective-permute-done((f32[64,64]{1,0:T(8,128)S(1)}, f32[64,64]{1,0:T(8,128)S(1)}, u32[]{:S(2)}, u32[]{:S(2)}) %collective-permute-start.1) | collective-permute-done | bytes 16416 | tf_op jit(solution)/shard_map/ppermute | solution.py:296
  27.9 4.9 %collective-permute-start.4 = (bf16[64,2048]{1,0:T(8,128)(2,1)S(1)}, bf16[64,2048]{1,0:T(8,128)(2,1)S(1)}, u32[]{:S(2)}, u32[]{:S(2)}) collective-permute-start(bf16[64,2048]{1,0:T(8,128)(2,1)S(1)} %copy-done.5), channel_id=1, source_target_pairs={{0,2},{2,4},{4,6},{6,8},{8,10},{10,12},{12,14},{14,16},{16,18},{18... | collective-permute-start | bytes 786440 | tf_op jit(solution)/shard_map/ppermute | solution.py:287
  32.8 1.9 %collective-permute-start.5 = (bf16[64,2048]{1,0:T(8,128)(2,1)S(1)}, bf16[64,2048]{1,0:T(8,128)(2,1)S(1)}, u32[]{:S(2)}, u32[]{:S(2)}) collective-permute-start(bf16[64,2048]{1,0:T(8,128)(2,1)S(1)} %copy-done.5), channel_id=1, source_target_pairs={{2,0},{4,2},{6,4},{8,6},{10,8},{12,10},{14,12},{16,14},{18,16},{20... | collective-permute-start | bytes 786440 | tf_op jit(solution)/shard_map/ppermute | solution.py:292
  34.8 8.1 %collective-permute-start.2 = (bf16[64,4096]{1,0:T(8,128)(2,1)}, bf16[64,4096]{1,0:T(8,128)(2,1)S(1)}, u32[]{:S(2)}, u32[]{:S(2)}) collective-permute-start(bf16[64,4096]{1,0:T(8,128)(2,1)} %get-tuple-element.26.refs_3_), channel_id=1, source_target_pairs={{0,2},{2,4},{4,6},{6,8},{8,10},{10,12},{12,14},{14,16},{16,18},{18... | collective-permute-start | bytes 1572872 | tf_op jit(solution)/shard_map/ppermute | solution.py:287
  42.9 1.9 %collective-permute-start.3 = (bf16[64,4096]{1,0:T(8,128)(2,1)}, bf16[64,4096]{1,0:T(8,128)(2,1)S(1)}, u32[]{:S(2)}, u32[]{:S(2)}) collective-permute-start(bf16[64,4096]{1,0:T(8,128)(2,1)} %get-tuple-element.27.refs_2_), channel_id=1, source_target_pairs={{2,0},{4,2},{6,4},{8,6},{10,8},{12,10},{14,12},{16,14},{18,16},{20... | collective-permute-start | bytes 1572872 | tf_op jit(solution)/shard_map/ppermute | solution.py:292
  48.7 3.2 %collective-permute-done.7 = f32[64,64]{1,0:T(8,128)S(1)} collective-permute-done((f32[64,64]{1,0:T(8,128)S(1)}, f32[64,64]{1,0:T(8,128)S(1)}, u32[]{:S(2)}, u32[]{:S(2)}) %collective-permute-start.7) | collective-permute-done | bytes 16416 | tf_op jit(solution)/shard_map/ppermute | solution.py:296
  52.9 9.8 %collective-permute-start.8 = (f32[64,64]{1,0:T(8,128)S(1)}, f32[64,64]{1,0:T(8,128)S(1)}, u32[]{:S(2)}, u32[]{:S(2)}) collective-permute-start(f32[64,64]{1,0:T(8,128)S(1)} %convolution_add_fusion.7), channel_id=1, source_target_pairs={{0,32},{2,34},{4,36},{6,38},{8,40},{10,42},{12,44},{14,46},{16,48}... | collective-permute-start | bytes 49160 | tf_op jit(solution)/shard_map/ppermute | solution.py:296
  65.4 2.4 %collective-permute-start.9 = (f32[64,64]{1,0:T(8,128)S(1)}, f32[64,64]{1,0:T(8,128)S(1)}, u32[]{:S(2)}, u32[]{:S(2)}) collective-permute-start(f32[64,64]{1,0:T(8,128)S(1)} %convolution_add_fusion.6), channel_id=1, source_target_pairs={{0,96},{2,98},{4,100},{6,102},{8,104},{10,106},{12,108},{14,110},{... | collective-permute-start | bytes 49160 | tf_op jit(solution)/shard_map/ppermute | solution.py:296
  68.8 1.8 %collective-permute-done.9 = f32[64,64]{1,0:T(8,128)S(1)} collective-permute-done((f32[64,64]{1,0:T(8,128)S(1)}, f32[64,64]{1,0:T(8,128)S(1)}, u32[]{:S(2)}, u32[]{:S(2)}) %collective-permute-start.9) | collective-permute-done | bytes 16416 | tf_op jit(solution)/shard_map/ppermute | solution.py:296
  72.7 22.9 %tail.2 = (bf16[64,8192]{1,0:T(8,128)(2,1)}, bf16[64,4096]{1,0:T(8,128)(2,1)S(1)}, bf16[64,4096]{1,0:T(8,128)(2,1)S(1)}, bf16[64,2048]{1,0:T(8,128)(2,1)S(1)}, f32[64,64]{1,0:T(8,128)S(1)}) custom-call(s32[32,5]{1,0:T(8,128)S(1)} %copy.13.refs_0_, s32[32,4]{1,0:T(8,128)S(1)} %copy.14.refs_1_, bf16[64,4096]{1,0:T(8,128)(2,1)S(1)} %copy-done.3, ...), custom_call_target="tpu_custom_call" | custom-call | flops 1700000000 | bytes 30000000 | tf_op jit(solution)/shard_map/tail/pallas_call | solution.py:267
  95.6 3.9 %collective-permute-done.10 = f32[64,64]{1,0:T(8,128)S(1)} collective-permute-done((f32[64,64]{1,0:T(8,128)S(1)}, f32[64,64]{1,0:T(8,128)S(1)}, u32[]{:S(2)}, u32[]{:S(2)}) %collective-permute-start.10) | collective-permute-done | bytes 16416 | tf_op jit(solution)/shard_map/ppermute | solution.py:296
  100.1 4.9 %collective-permute-done.11 = f32[64,64]{1,0:T(8,128)S(1)} collective-permute-done((f32[64,64]{1,0:T(8,128)S(1)}, f32[64,64]{1,0:T(8,128)S(1)}, u32[]{:S(2)}, u32[]{:S(2)}) %collective-permute-start.11) | collective-permute-done | bytes 16416 | tf_op jit(solution)/shard_map/ppermute | solution.py:296
  105.5 1.9 %collective-permute-start.14 = (bf16[64,2048]{1,0:T(8,128)(2,1)S(1)}, bf16[64,2048]{1,0:T(8,128)(2,1)S(1)}, u32[]{:S(2)}, u32[]{:S(2)}) collective-permute-start(bf16[64,2048]{1,0:T(8,128)(2,1)S(1)} %get-tuple-element.38.refs_6_), channel_id=1, source_target_pairs={{0,2},{2,4},{4,6},{6,8},{8,10},{10,12},{12,14},{14,16},{16,18},{18... | collective-permute-start | bytes 786440 | tf_op jit(solution)/shard_map/ppermute | solution.py:287
  107.4 3.9 %collective-permute-start.15 = (bf16[64,2048]{1,0:T(8,128)(2,1)S(1)}, bf16[64,2048]{1,0:T(8,128)(2,1)S(1)}, u32[]{:S(2)}, u32[]{:S(2)}) collective-permute-start(bf16[64,2048]{1,0:T(8,128)(2,1)S(1)} %get-tuple-element.38.refs_6_), channel_id=1, source_target_pairs={{2,0},{4,2},{6,4},{8,6},{10,8},{12,10},{14,12},{16,14},{18,16},{20... | collective-permute-start | bytes 786440 | tf_op jit(solution)/shard_map/ppermute | solution.py:292
  111.4 6.1 %collective-permute-start.12 = (bf16[64,4096]{1,0:T(8,128)(2,1)S(1)}, bf16[64,4096]{1,0:T(8,128)(2,1)S(1)}, u32[]{:S(2)}, u32[]{:S(2)}) collective-permute-start(bf16[64,4096]{1,0:T(8,128)(2,1)S(1)} %get-tuple-element.36.refs_3_), channel_id=1, source_target_pairs={{0,2},{2,4},{4,6},{6,8},{8,10},{10,12},{12,14},{14,16},{16,18},{18... | collective-permute-start | bytes 1572872 | tf_op jit(solution)/shard_map/ppermute | solution.py:287
  117.5 1.9 %collective-permute-start.13 = (bf16[64,4096]{1,0:T(8,128)(2,1)S(1)}, bf16[64,4096]{1,0:T(8,128)(2,1)S(1)}, u32[]{:S(2)}, u32[]{:S(2)}) collective-permute-start(bf16[64,4096]{1,0:T(8,128)(2,1)S(1)} %get-tuple-element.37.refs_2_), channel_id=1, source_target_pairs={{2,0},{4,2},{6,4},{8,6},{10,8},{12,10},{14,12},{16,14},{18,16},{20... | collective-permute-start | bytes 1572872 | tf_op jit(solution)/shard_map/ppermute | solution.py:292
  120.3 4.8 %collective-permute-done.17 = f32[64,64]{1,0:T(8,128)S(1)} collective-permute-done((f32[64,64]{1,0:T(8,128)S(1)}, f32[64,64]{1,0:T(8,128)S(1)}, u32[]{:S(2)}, u32[]{:S(2)}) %collective-permute-start.17) | collective-permute-done | bytes 16416 | tf_op jit(solution)/shard_map/ppermute | solution.py:296
  125.2 9.1 %collective-permute-start.18 = (f32[64,64]{1,0:T(8,128)S(1)}, f32[64,64]{1,0:T(8,128)S(1)}, u32[]{:S(2)}, u32[]{:S(2)}) collective-permute-start(f32[64,64]{1,0:T(8,128)S(1)} %convolution_add_fusion.1), channel_id=1, source_target_pairs={{0,32},{2,34},{4,36},{6,38},{8,40},{10,42},{12,44},{14,46},{16,48}... | collective-permute-start | bytes 49160 | tf_op jit(solution)/shard_map/ppermute | solution.py:296
  136.7 4.9 %collective-permute-done.19 = f32[64,64]{1,0:T(8,128)S(1)} collective-permute-done((f32[64,64]{1,0:T(8,128)S(1)}, f32[64,64]{1,0:T(8,128)S(1)}, u32[]{:S(2)}, u32[]{:S(2)}) %collective-permute-start.19) | collective-permute-done | bytes 16416 | tf_op jit(solution)/shard_map/ppermute | solution.py:296
  142.0 20.3 %tail.3 = bf16[64,8192]{1,0:T(8,128)(2,1)} custom-call(s32[32,5]{1,0:T(8,128)S(1)} %copy.13.refs_0_, s32[32,4]{1,0:T(8,128)S(1)} %copy.14.refs_1_, bf16[64,4096]{1,0:T(8,128)(2,1)S(1)} %get-tuple-element.37.refs_2_, bf16[64,4096]{1,0:T(8,128)(2,1)S(1)} %get-tuple-element.36.refs_3_, bf16[64,4096]{1,0:T(8,128)(2,1)S(1)} %collective-permute-done.12.refs_4_, ...), custom_call_target="tpu_custom_call" | custom-call | flops 1700000000 | bytes 30000000 | tf_op jit(solution)/shard_map/tail/pallas_call | solution.py:267
  (82 shorter events, 22.9 us)
Async XLA Ops:
  6.0 13.0 %collective-permute-start = (f32[64,64]{1,0:T(8,128)}, f32[64,64]{1,0:T(8,128)S(1)}, u32[]{:S(2)}, u32[]{:S(2)}) collective-permute-start(f32[64,64]{1,0:T(8,128)} %get-tuple-element.24), channel_id=1, source_target_pairs={{0,2},{2,0},{4,6},{6,4},{8,10},{10,8},{12,14},{14,12},{16,18},{18,... | collective-permute-start | bytes 49160 | tf_op jit(solution)/shard_map/ppermute | solution.py:296
  15.0 57.6 %copy-start = (bf16[32,64,256]{2,1,0:T(8,128)(2,1)S(1)}, bf16[32,64,256]{2,1,0:T(8,128)(2,1)}, u32[]{:S(2)}) copy-start(bf16[32,64,256]{2,1,0:T(8,128)(2,1)} %refs_11_.3) | copy-start | bytes 3145732
  15.0 57.6 %copy-start.1 = (bf16[32,4,64,64]{3,2,1,0:T(8,128)(2,1)S(1)}, bf16[32,4,64,64]{3,2,1,0:T(8,128)(2,1)}, u32[]{:S(2)}) copy-start(bf16[32,4,64,64]{3,2,1,0:T(8,128)(2,1)} %refs_13_.3) | copy-start | bytes 3145732
  19.0 53.7 %copy-start.3 = (bf16[64,4096]{1,0:T(8,128)(2,1)S(1)}, bf16[64,4096]{1,0:T(8,128)(2,1)}, u32[]{:S(2)}) copy-start(bf16[64,4096]{1,0:T(8,128)(2,1)} %get-tuple-element.27.refs_2_) | copy-start | bytes 1572868
  19.0 53.7 %copy-start.4 = (bf16[64,4096]{1,0:T(8,128)(2,1)S(1)}, bf16[64,4096]{1,0:T(8,128)(2,1)}, u32[]{:S(2)}) copy-start(bf16[64,4096]{1,0:T(8,128)(2,1)} %get-tuple-element.26.refs_3_) | copy-start | bytes 1572868
  20.0 5.2 %collective-permute-start.1 = (f32[64,64]{1,0:T(8,128)S(1)}, f32[64,64]{1,0:T(8,128)S(1)}, u32[]{:S(2)}, u32[]{:S(2)}) collective-permute-start(f32[64,64]{1,0:T(8,128)S(1)} %convolution_add_fusion.11), channel_id=1, source_target_pairs={{0,6},{2,4},{4,2},{6,0},{8,14},{10,12},{12,10},{14,8},{16,22},{18,... | collective-permute-start | bytes 49160 | tf_op jit(solution)/shard_map/ppermute | solution.py:296
  26.2 19.6 %collective-permute-start.6 = (f32[64,64]{1,0:T(8,128)S(1)}, f32[64,64]{1,0:T(8,128)S(1)}, u32[]{:S(2)}, u32[]{:S(2)}) collective-permute-start(f32[64,64]{1,0:T(8,128)S(1)} %convolution_add_fusion.9), channel_id=1, source_target_pairs={{0,8},{2,10},{4,12},{6,14},{8,0},{10,2},{12,4},{14,6},{16,24},{18,... | collective-permute-start | bytes 49160 | tf_op jit(solution)/shard_map/ppermute | solution.py:296
  27.9 44.6 %collective-permute-start.4 = (bf16[64,2048]{1,0:T(8,128)(2,1)S(1)}, bf16[64,2048]{1,0:T(8,128)(2,1)S(1)}, u32[]{:S(2)}, u32[]{:S(2)}) collective-permute-start(bf16[64,2048]{1,0:T(8,128)(2,1)S(1)} %copy-done.5), channel_id=1, source_target_pairs={{0,2},{2,4},{4,6},{6,8},{8,10},{10,12},{12,14},{14,16},{16,18},{18... | collective-permute-start | bytes 786440 | tf_op jit(solution)/shard_map/ppermute | solution.py:287
  32.8 39.8 %collective-permute-start.5 = (bf16[64,2048]{1,0:T(8,128)(2,1)S(1)}, bf16[64,2048]{1,0:T(8,128)(2,1)S(1)}, u32[]{:S(2)}, u32[]{:S(2)}) collective-permute-start(bf16[64,2048]{1,0:T(8,128)(2,1)S(1)} %copy-done.5), channel_id=1, source_target_pairs={{2,0},{4,2},{6,4},{8,6},{10,8},{12,10},{14,12},{16,14},{18,16},{20... | collective-permute-start | bytes 786440 | tf_op jit(solution)/shard_map/ppermute | solution.py:292
  34.8 37.8 %collective-permute-start.2 = (bf16[64,4096]{1,0:T(8,128)(2,1)}, bf16[64,4096]{1,0:T(8,128)(2,1)S(1)}, u32[]{:S(2)}, u32[]{:S(2)}) collective-permute-start(bf16[64,4096]{1,0:T(8,128)(2,1)} %get-tuple-element.26.refs_3_), channel_id=1, source_target_pairs={{0,2},{2,4},{4,6},{6,8},{8,10},{10,12},{12,14},{14,16},{16,18},{18... | collective-permute-start | bytes 1572872 | tf_op jit(solution)/shard_map/ppermute | solution.py:287
  42.9 29.7 %collective-permute-start.3 = (bf16[64,4096]{1,0:T(8,128)(2,1)}, bf16[64,4096]{1,0:T(8,128)(2,1)S(1)}, u32[]{:S(2)}, u32[]{:S(2)}) collective-permute-start(bf16[64,4096]{1,0:T(8,128)(2,1)} %get-tuple-element.27.refs_2_), channel_id=1, source_target_pairs={{2,0},{4,2},{6,4},{8,6},{10,8},{12,10},{14,12},{16,14},{18,16},{20... | collective-permute-start | bytes 1572872 | tf_op jit(solution)/shard_map/ppermute | solution.py:292
  46.7 5.2 %collective-permute-start.7 = (f32[64,64]{1,0:T(8,128)S(1)}, f32[64,64]{1,0:T(8,128)S(1)}, u32[]{:S(2)}, u32[]{:S(2)}) collective-permute-start(f32[64,64]{1,0:T(8,128)S(1)} %convolution_add_fusion.8), channel_id=1, source_target_pairs={{0,24},{2,26},{4,28},{6,30},{8,16},{10,18},{12,20},{14,22},{16,8},... | collective-permute-start | bytes 49160 | tf_op jit(solution)/shard_map/ppermute | solution.py:296
  52.9 11.7 %collective-permute-start.8 = (f32[64,64]{1,0:T(8,128)S(1)}, f32[64,64]{1,0:T(8,128)S(1)}, u32[]{:S(2)}, u32[]{:S(2)}) collective-permute-start(f32[64,64]{1,0:T(8,128)S(1)} %convolution_add_fusion.7), channel_id=1, source_target_pairs={{0,32},{2,34},{4,36},{6,38},{8,40},{10,42},{12,44},{14,46},{16,48}... | collective-permute-start | bytes 49160 | tf_op jit(solution)/shard_map/ppermute | solution.py:296
  65.4 5.2 %collective-permute-start.9 = (f32[64,64]{1,0:T(8,128)S(1)}, f32[64,64]{1,0:T(8,128)S(1)}, u32[]{:S(2)}, u32[]{:S(2)}) collective-permute-start(f32[64,64]{1,0:T(8,128)S(1)} %convolution_add_fusion.6), channel_id=1, source_target_pairs={{0,96},{2,98},{4,100},{6,102},{8,104},{10,106},{12,108},{14,110},{... | collective-permute-start | bytes 49160 | tf_op jit(solution)/shard_map/ppermute | solution.py:296
  95.5 4.0 %collective-permute-start.10 = (f32[64,64]{1,0:T(8,128)S(1)}, f32[64,64]{1,0:T(8,128)S(1)}, u32[]{:S(2)}, u32[]{:S(2)}) collective-permute-start(f32[64,64]{1,0:T(8,128)S(1)} %get-tuple-element.35), channel_id=1, source_target_pairs={{0,2},{2,0},{4,6},{6,4},{8,10},{10,8},{12,14},{14,12},{16,18},{18,... | collective-permute-start | bytes 49160 | tf_op jit(solution)/shard_map/ppermute | solution.py:296
  99.9 5.2 %collective-permute-start.11 = (f32[64,64]{1,0:T(8,128)S(1)}, f32[64,64]{1,0:T(8,128)S(1)}, u32[]{:S(2)}, u32[]{:S(2)}) collective-permute-start(f32[64,64]{1,0:T(8,128)S(1)} %convolution_add_fusion.5), channel_id=1, source_target_pairs={{0,6},{2,4},{4,2},{6,0},{8,14},{10,12},{12,10},{14,8},{16,22},{18,... | collective-permute-start | bytes 49160 | tf_op jit(solution)/shard_map/ppermute | solution.py:296
  105.2 14.4 %collective-permute-start.16 = (f32[64,64]{1,0:T(8,128)S(1)}, f32[64,64]{1,0:T(8,128)S(1)}, u32[]{:S(2)}, u32[]{:S(2)}) collective-permute-start(f32[64,64]{1,0:T(8,128)S(1)} %convolution_add_fusion.3), channel_id=1, source_target_pairs={{0,8},{2,10},{4,12},{6,14},{8,0},{10,2},{12,4},{14,6},{16,24},{18,... | collective-permute-start | bytes 49160 | tf_op jit(solution)/shard_map/ppermute | solution.py:296
  105.5 36.5 %collective-permute-start.14 = (bf16[64,2048]{1,0:T(8,128)(2,1)S(1)}, bf16[64,2048]{1,0:T(8,128)(2,1)S(1)}, u32[]{:S(2)}, u32[]{:S(2)}) collective-permute-start(bf16[64,2048]{1,0:T(8,128)(2,1)S(1)} %get-tuple-element.38.refs_6_), channel_id=1, source_target_pairs={{0,2},{2,4},{4,6},{6,8},{8,10},{10,12},{12,14},{14,16},{16,18},{18... | collective-permute-start | bytes 786440 | tf_op jit(solution)/shard_map/ppermute | solution.py:287
  107.4 34.6 %collective-permute-start.15 = (bf16[64,2048]{1,0:T(8,128)(2,1)S(1)}, bf16[64,2048]{1,0:T(8,128)(2,1)S(1)}, u32[]{:S(2)}, u32[]{:S(2)}) collective-permute-start(bf16[64,2048]{1,0:T(8,128)(2,1)S(1)} %get-tuple-element.38.refs_6_), channel_id=1, source_target_pairs={{2,0},{4,2},{6,4},{8,6},{10,8},{12,10},{14,12},{16,14},{18,16},{20... | collective-permute-start | bytes 786440 | tf_op jit(solution)/shard_map/ppermute | solution.py:292
  111.4 30.7 %collective-permute-start.12 = (bf16[64,4096]{1,0:T(8,128)(2,1)S(1)}, bf16[64,4096]{1,0:T(8,128)(2,1)S(1)}, u32[]{:S(2)}, u32[]{:S(2)}) collective-permute-start(bf16[64,4096]{1,0:T(8,128)(2,1)S(1)} %get-tuple-element.36.refs_3_), channel_id=1, source_target_pairs={{0,2},{2,4},{4,6},{6,8},{8,10},{10,12},{12,14},{14,16},{16,18},{18... | collective-permute-start | bytes 1572872 | tf_op jit(solution)/shard_map/ppermute | solution.py:287
  117.5 24.5 %collective-permute-start.13 = (bf16[64,4096]{1,0:T(8,128)(2,1)S(1)}, bf16[64,4096]{1,0:T(8,128)(2,1)S(1)}, u32[]{:S(2)}, u32[]{:S(2)}) collective-permute-start(bf16[64,4096]{1,0:T(8,128)(2,1)S(1)} %get-tuple-element.37.refs_2_), channel_id=1, source_target_pairs={{2,0},{4,2},{6,4},{8,6},{10,8},{12,10},{14,12},{16,14},{18,16},{20... | collective-permute-start | bytes 1572872 | tf_op jit(solution)/shard_map/ppermute | solution.py:292
  119.8 5.2 %collective-permute-start.17 = (f32[64,64]{1,0:T(8,128)S(1)}, f32[64,64]{1,0:T(8,128)S(1)}, u32[]{:S(2)}, u32[]{:S(2)}) collective-permute-start(f32[64,64]{1,0:T(8,128)S(1)} %convolution_add_fusion.2), channel_id=1, source_target_pairs={{0,24},{2,26},{4,28},{6,30},{8,16},{10,18},{12,20},{14,22},{16,8},... | collective-permute-start | bytes 49160 | tf_op jit(solution)/shard_map/ppermute | solution.py:296
  125.2 11.0 %collective-permute-start.18 = (f32[64,64]{1,0:T(8,128)S(1)}, f32[64,64]{1,0:T(8,128)S(1)}, u32[]{:S(2)}, u32[]{:S(2)}) collective-permute-start(f32[64,64]{1,0:T(8,128)S(1)} %convolution_add_fusion.1), channel_id=1, source_target_pairs={{0,32},{2,34},{4,36},{6,38},{8,40},{10,42},{12,44},{14,46},{16,48}... | collective-permute-start | bytes 49160 | tf_op jit(solution)/shard_map/ppermute | solution.py:296
  136.4 5.2 %collective-permute-start.19 = (f32[64,64]{1,0:T(8,128)S(1)}, f32[64,64]{1,0:T(8,128)S(1)}, u32[]{:S(2)}, u32[]{:S(2)}) collective-permute-start(f32[64,64]{1,0:T(8,128)S(1)} %convolution_add_fusion), channel_id=1, source_target_pairs={{0,96},{2,98},{4,100},{6,102},{8,104},{10,106},{12,108},{14,110},{... | collective-permute-start | bytes 49160 | tf_op jit(solution)/shard_map/ppermute | solution.py:296
  (9 other events, 162.3 us)

commit v2 on v0

v2 whole, which is shorter than its diff:
```python
import jax
import jax.numpy as jnp
from jax import lax
from jax.experimental import pallas as pl
from jax.experimental.pallas import tpu as pltpu
from jax.sharding import PartitionSpec as P


REACH = 16
FARR = 32
PIECES = 4
BF = jnp.bfloat16
F32 = jnp.float32
NT = (((1,), (1,)), ((), ()))
NN = (((1,), (0,)), ((), ()))
HBM = pl.BlockSpec(memory_space=pltpu.HBM)
VMEM = pl.BlockSpec(memory_space=pltpu.VMEM)


def mm(a, b, dims=NN):
    return lax.dot_general(a, b, dims, preferred_element_type=F32)


def exact(a, b, dims=NN):
    return lax.dot_general(
        a, b, dims, precision=lax.Precision.HIGHEST, preferred_element_type=F32
    )


def params(mib):
    return pltpu.CompilerParams(vmem_limit_bytes=mib * 2**20)


def cost(flops, moved):
    return pl.CostEstimate(flops=flops, bytes_accessed=moved, transcendentals=0)


def is_even():
    return (lax.axis_index("leaf") & 1) == 0


def columns_of(start, width):
    return pl.ds(pl.multiple_of(start, width), width)


def head_body(v, basis_hbm, trans_hbm, a, b, node, basis, trans, sems):
    leaves, rank, points = basis.shape
    half = v.shape[1] // 2
    first_a = jnp.where(is_even(), leaves // 2, 0)
    sides = ((a, first_a), (b, leaves // 2 - first_a))
    copies = [
        pltpu.make_async_copy(
            v.at[:, columns_of(first * points, half)], msg.at[:, :half], sems.at[i]
        )
        for i, (msg, first) in enumerate(sides)
    ]
    copies.append(pltpu.make_async_copy(basis_hbm, basis, sems.at[2]))
    copies.append(pltpu.make_async_copy(trans_hbm, trans, sems.at[3]))
    for i in (2, 0, 3, 1):
        copies[i].start()
    copies[2].wait()
    total = None
    for side, (msg, first) in enumerate(sides):
        copies[side].wait()
        if side == 0:
            copies[3].wait()
        for pair in range(leaves // 4):
            parts = [
                mm(msg[:, leaf * points : (leaf + 1) * points], basis[first + leaf], NT)
                for leaf in (2 * pair, 2 * pair + 1)
            ]
            both = jnp.concatenate(parts, axis=1).astype(BF)
            start = (first // 2 + pair) * 2 * rank
            a[:, columns_of(half + start, 2 * rank)] = both
            b[:, columns_of(half + start, 2 * rank)] = both
            term = mm(both, trans[columns_of(start, 2 * rank), :])
            total = term if total is None else total + term
    node[...] = total


def head(vectors, basis_t, trans2):
    columns, own = vectors.shape
    leaves, rank, _ = basis_t.shape
    message = jax.ShapeDtypeStruct((columns, own // 2 + leaves * rank), BF)
    return pl.pallas_call(
        head_body,
        in_specs=[HBM] * 3,
        out_specs=[VMEM] * 3,
        out_shape=[message, message, jax.ShapeDtypeStruct((columns, rank), F32)],
        scratch_shapes=[
            pltpu.VMEM(basis_t.shape, BF),
            pltpu.VMEM(trans2.shape, BF),
            pltpu.SemaphoreType.DMA((4,)),
        ],
        compiler_params=params(10),
        cost_estimate=cost(200_000_000, 6_000_000),
        name="head",
    )(*(pltpu.with_memory_space_constraint(x, pltpu.HBM) for x in (vectors, basis_t, trans2)))


def table_body(levels, trans, couple, up, down, own, pair):
    device = lax.axis_index("leaf")
    count, rows, nodes = 8, trans.shape[0], trans.shape[2]
    row = lax.broadcasted_iota(jnp.int32, (count, nodes), 0)
    node = lax.broadcasted_iota(jnp.int32, (count, nodes), 1)
    offset = (2 << levels) - lax.shift_right_logical(jnp.full_like(row, 2 << levels), row)
    here = offset + lax.shift_right_logical(jnp.zeros_like(row) + device, row)
    there = jnp.bitwise_xor(here, 1)
    wanted = row < levels
    pick_here = jnp.where(wanted & (node == here), 1.0, 0.0).astype(BF)
    pick_there = jnp.where(wanted & (node == there), 1.0, 0.0).astype(BF)
    both = jnp.concatenate([pick_here, pick_there], axis=0)
    for k in range(rows):
        own[:, k, :] = mm(both, trans[k], NT)
        pair[:, k, :] = mm(pick_here, couple[k], NT)
    for t in range(levels):
        up[t, 0] = own[t]
        up[t, 1] = own[count + t]
    down[0] = pair[0]
    path = own[0]
    for t in range(1, levels):
        down[t] = exact(path, pair[t])
        if t + 1 < levels:
            path = exact(path, own[t])


def table(top_transfer, top_couple):
    rank = top_transfer.shape[1]
    levels = lax.axis_size("leaf").bit_length() - 1
    return pl.pallas_call(
        lambda *refs: table_body(levels, *refs),
        in_specs=[VMEM] * 2,
        out_specs=[VMEM] * 2,
        out_shape=[
            jax.ShapeDtypeStruct((levels, 2, rank, rank), F32),
            jax.ShapeDtypeStruct((levels, rank, rank), F32),
        ],
        scratch_shapes=[pltpu.VMEM((16, rank, rank), F32), pltpu.VMEM((8, rank, rank), F32)],
        compiler_params=params(10),
        cost_estimate=cost(10_000_000, 3_000_000),
        name="table",
    )(jnp.transpose(top_transfer, (1, 2, 0)), jnp.transpose(top_couple, (1, 2, 0)))


def near_body(piece, load, near_list, v, near, *refs):
    if load:
        total, kept, sems = refs
    else:
        (total,) = refs
        kept = near
    some, kn, points, _ = kept.shape
    leaves = v.shape[1] // points
    first = lax.axis_index("leaf") * leaves
    group = 4
    copies = []
    if load:
        for g in range(some // group):
            here = pl.ds(piece * some + g * group, group)
            copies.append(
                pltpu.make_async_copy(near.at[here], kept.at[pl.ds(g * group, group)], sems.at[g])
            )
            copies[-1].start()
    for i in range(some):
        if load and i % group == 0:
            copies[i // group].wait()
        out = None
        for s in range(kn):
            source = near_list[piece * some + i, s] - first
            inside = (source >= 0) & (source < leaves)
            rows = v[:, columns_of(jnp.clip(source, 0, leaves - 1) * points, points)]
            term = mm(jnp.where(inside, rows, jnp.zeros_like(rows)), kept[i, s], NT)
            out = term if out is None else out + term
        total[:, i * points : (i + 1) * points] = out


def near_piece(piece, near_list, v, near_blocks, kept):
    columns = v.shape[0]
    load = kept is None
    shape = near_blocks.shape
    some = shape[0] // PIECES
    out_shape = [jax.ShapeDtypeStruct((columns, some * shape[2]), F32)]
    scratch = []
    if load:
        out_shape.append(jax.ShapeDtypeStruct((some, *shape[1:]), BF))
        scratch.append(pltpu.SemaphoreType.DMA((some // 4,)))
    out = pl.pallas_call(
        lambda *refs: near_body(piece, load, *refs),
        grid_spec=pltpu.PrefetchScalarGridSpec(
            num_scalar_prefetch=1,
            in_specs=[VMEM, HBM if load else VMEM],
            out_specs=[VMEM] * len(out_shape),
            scratch_shapes=scratch,
        ),
        out_shape=out_shape,
        compiler_params=params(10),
        cost_estimate=cost(350_000_000, 6_000_000),
    )(near_list, v, pltpu.with_memory_space_constraint(near_blocks, pltpu.HBM) if load else kept)
    return out[0], (out[1] if load else kept)


def halo_plan(near_list):
    leaves, kn = near_list.shape
    first = lax.axis_index("leaf") * leaves
    source = [near_list[:, s] - first for s in range(kn)]
    outside = [(j < 0) | (j >= leaves) for j in source]
    code = [
        jnp.where(j < 0, j + REACH, j - leaves + REACH) + 64 * s for s, j in enumerate(source)
    ]
    place = []
    count = jnp.zeros_like(source[0])
    for out in outside:
        place.append(count)
        count = count + out.astype(jnp.int32)
    rows = []
    for j in range(kn - 1):
        row = jnp.full_like(count, -1)
        for s in range(kn):
            row = jnp.where(outside[s] & (place[s] == j), code[s], row)
        rows.append(row)
    most = jnp.max(count.reshape(PIECES, -1), axis=1)
    rows.append(jnp.pad(most, (0, leaves - PIECES)))
    return jnp.stack(rows)


def tail_body(more, plan, couple_list, got_a, got_b, sent_a, top, basis, trans, couple, *refs):
    kept, partial, refs = refs[:PIECES], refs[PIECES : 2 * PIECES], refs[2 * PIECES :]
    if more:
        image, a, b, node, table_ref, acc, total_ref = refs
    else:
        image, table_ref, acc, staged, sems = refs
    leaves, rank, points = basis.shape
    some = leaves // PIECES
    half = leaves // 2 * points
    even = is_even()
    first = lax.axis_index("leaf") * leaves
    base_a = jnp.where(even, 2 * leaves, 0)
    for ref, base in ((got_a, base_a), (sent_a, leaves), (got_b, 2 * leaves - base_a)):
        for pair in range(leaves // 2):
            start = half + 2 * rank * pair
            both = ref[:, start : start + 2 * rank]
            table_ref[base + 2 * pair] = both[:, :rank]
            table_ref[base + 2 * pair + 1] = both[:, rank:]
    high = top[...].astype(BF)
    low = (top[...] - high.astype(F32)).astype(BF)
    if more:
        total_ref[...] = jnp.zeros_like(total_ref)
    writes = []
    for piece in range(PIECES):
        near, own = kept[piece], partial[piece]
        acc[...] = own[...]

        def add(j, carry, near=near, piece=piece):
            for i in range(some):
                code = plan[j, piece * some + i]
                there = code >= 0
                code = jnp.maximum(code, 0)
                place = code & 31
                at = columns_of((place & 15) * points, points)
                in_a = (place >= REACH) == even
                rows = jnp.where(in_a, got_a[:, at], got_b[:, at])
                rows = jnp.where(there, rows, jnp.zeros_like(rows))
                here = slice(i * points, (i + 1) * points)
                acc[:, here] += mm(rows, near[i, lax.shift_right_logical(code, 6)], NT)
            return carry

        lax.fori_loop(0, plan[4, piece], add, 0)
        results = []
        for i in range(some):
            leaf = piece * some + i
            moved = trans[leaf * rank : (leaf + 1) * rank, :]
            local = mm(high, moved, NT) + mm(low, moved, NT)
            for s in range(couple.shape[1]):
                local += mm(table_ref[couple_list[leaf, s] - first + FARR], couple[leaf, s], NT)
            here = slice(i * points, (i + 1) * points)
            value = (acc[:, here] + mm(local.astype(BF), basis[leaf])).astype(BF)
            results.append(value)
            if more:
                image[:, leaf * points : (leaf + 1) * points] = value
            else:
                staged[:, leaf * points : (leaf + 1) * points] = value
        if not more:
            here = pl.ds(piece * some * points, some * points)
            writes.append(pltpu.make_async_copy(staged.at[:, here], image.at[:, here], sems.at[piece]))
            writes[-1].start()
            continue
        for pair in range(some // 2):
            leaf = piece * some + 2 * pair
            parts = [mm(results[2 * pair + i], basis[leaf + i], NT) for i in range(2)]
            both = jnp.concatenate(parts, axis=1).astype(BF)
            a[:, half + leaf * rank : half + (leaf + 2) * rank] = both
            b[:, half + leaf * rank : half + (leaf + 2) * rank] = both
            total_ref[...] += mm(both, trans[leaf * rank : (leaf + 2) * rank, :])
        in_right = piece >= PIECES // 2
        start = piece % (PIECES // 2) * some * points

        def put(message, results=results, start=start):
            for i, value in enumerate(results):
                message[:, start + i * points : start + (i + 1) * points] = value

        @pl.when(even == in_right)
        def _():
            put(a)

        @pl.when(even != in_right)
        def _():
            put(b)

    for write in writes:
        write.wait()
    if more:
        node[...] = total_ref[...]


def tail(more, lists, got, sent_a, top, kept, partial, basis_t, trans2, leaf_couple):
    columns, wide = sent_a.shape
    leaves, rank, points = basis_t.shape
    own = leaves * points
    image = jax.ShapeDtypeStruct((columns, own), BF)
    scratch = [
        pltpu.VMEM((3 * leaves, columns, rank), BF),
        pltpu.VMEM((columns, own // PIECES), F32),
    ]
    if more:
        message = jax.ShapeDtypeStruct((columns, wide), BF)
        out_shape = [image, message, message, jax.ShapeDtypeStruct((columns, rank), F32)]
        out_specs = [VMEM] * 4
        scratch.append(pltpu.VMEM((columns, rank), F32))
    else:
        out_shape, out_specs = [image], [HBM]
        scratch += [pltpu.VMEM((columns, own), BF), pltpu.SemaphoreType.DMA((PIECES,))]
    return pl.pallas_call(
        lambda *refs: tail_body(more, *refs),
        grid_spec=pltpu.PrefetchScalarGridSpec(
            num_scalar_prefetch=2,
            in_specs=[VMEM] * (7 + 2 * PIECES),
            out_specs=out_specs,
            scratch_shapes=scratch,
        ),
        out_shape=out_shape,
        compiler_params=params(16),
        cost_estimate=cost(1_000_000_000, 10_000_000),
        name="tail",
    )(*lists, *got, sent_a, top, basis_t, trans2, leaf_couple, *kept, *partial)


def swapped(value, mask):
    return lax.ppermute(value, "leaf", [(i, i ^ mask) for i in range(lax.axis_size("leaf"))])


def swapped_odd(value):
    size = lax.axis_size("leaf")
    pairs = [(i, i + 1) for i in range(1, size - 1, 2)]
    return lax.ppermute(value, "leaf", pairs + [(j, i) for i, j in pairs])


def one_product(more, v, a, b, node, up, down, kept, plan, near_list, couple_list, near_blocks, *fixed):
    levels = up.shape[0]
    top = jnp.zeros_like(node)
    got_a = got_b = None
    partial, held = [], []
    for t in range(levels):
        mask = (1 << t) if t % 2 == 0 else 3 << (t - 1)
        other = swapped(node, mask)
        if t >= 2:
            piece = t - 2
            own, block = near_piece(piece, near_list, v, near_blocks, kept[piece] if kept else None)
            partial.append(own)
            held.append(block)
        if t == 0:
            a, other = lax.optimization_barrier((a, other))
            got_a = swapped(a, 1)
        if t == 1:
            b, other = lax.optimization_barrier((b, other))
            got_b = swapped_odd(b)
        if t + 1 < levels:
            node = exact(node, up[t, 0]) + exact(other, up[t, 1])
        top += exact(other, down[t], NT)
    out = tail(more, (plan, couple_list), (got_a, got_b), a, top, held, partial, *fixed)
    return out, held


def on_device(
    rhs_block,
    basis_t,
    near_blocks,
    near_list,
    leaf_transfer,
    couple_list,
    leaf_couple,
    top_transfer,
    top_couple,
):
    leaves, rank, _ = leaf_transfer.shape
    trans2 = leaf_transfer.reshape(leaves * rank, rank)
    a, b, node = head(rhs_block, basis_t, trans2)
    up, down = table(top_transfer, top_couple)
    plan = halo_plan(near_list)
    lists = (plan, near_list, couple_list, near_blocks, basis_t, trans2, leaf_couple)
    (first_image, a, b, node), kept = one_product(
        True, rhs_block, a, b, node, up, down, None, *lists
    )
    (second_image,), _ = one_product(
        False, first_image, a, b, node, up, down, kept, *lists
    )
    return (first_image, second_image)


def solution(mesh):
    in_specs = (
        P("rhs", "leaf"),
        P("leaf", None, None),
        P("leaf", None, None, None),
        P("leaf", None),
        P("leaf", None, None),
        P("leaf", None),
        P("leaf", None, None, None),
        P(),
        P(),
    )
    out_specs = (P("rhs", "leaf"), P("rhs", "leaf"))
    return jax.shard_map(
        on_device, mesh=mesh, in_specs=in_specs, out_specs=out_specs, check_vma=False
    )
```

time: 244 us -> 192 us (0.79)
  the two profiles are of different devices: /device:TPU:96 before, /device:TPU:6 now
where the time goes in v2:
time: 192 us
  Pallas kernels  66.8 us (35%)
  starting transfers between devices  42.6 us (22%)
  waiting for transfers between devices  36.6 us (19%)
  local copies, waits for them, and re-layouts  35.9 us (19%)
  matrix products  5.45 us (3%)
  other arithmetic  2.79 us (1%)
    ppermute x14, waiting for transfers between devices, swapped(): lax.ppermute(value, 'leaf', [(i, i ^ mask) for i in range(lax.axis_size('...  36.6 us
    ppermute x14, starting transfers between devices, swapped(): lax.ppermute(value, 'leaf', [(i, i ^ mask) for i in range(lax.axis_size('...  36 us
    unnamed x72, local copies, waits for them, and re-layouts  35.8 us
    pallas_call x2, Pallas kernels, tail(): pl.pallas_call(lambda *refs: tail_body(more, *refs), grid_spec=pltpu.Pref...  31.8 us
    pallas_call x8, Pallas kernels, near_piece(): pl.pallas_call(lambda *refs: near_body(piece, load, *refs), grid_spec=plt...  27.5 us
    ppermute x2, starting transfers between devices, swapped_odd(): return lax.ppermute(value, 'leaf', pairs + [(j, i) for i, j in pairs])  6.58 us
    dot_general x32, matrix products, exact(): lax.dot_general(a, b, dims, precision=lax.Precision.HIGHEST, preferred_el...  5.45 us
    pallas_call x1, Pallas kernels, head(): pl.pallas_call(head_body, in_specs=[HBM] * 3, out_specs=[VMEM] * 3, out_s...  5.22 us
  transfers between devices with their start and end apart: 16, of which 10 were waited for; matrix products, arithmetic and copies ran while one was open for 5% of the time, Pallas kernels for 12%

profile of v2, /device:TPU:6, one launch (start us, length us, event | category | flops | bytes accessed | tf_op | source)
XLA Modules:
  0.0 191.6 jit_solution(15608198854349712462)
XLA Ops:
  0.6 5.2 %head.1 = (bf16[64,6144]{1,0:T(8,128)(2,1)S(1)}, bf16[64,6144]{1,0:T(8,128)(2,1)S(1)}, f32[64,64]{1,0:T(8,128)S(1)}) custom-call(bf16[64,8192]{1,0:T(8,128)(2,1)} %refs_1_.9, bf16[32,64,256]{2,1,0:T(8,128)(2,1)} %refs_6_.3, bf16[2048,64]{1,0:T(8,128)(2,1)} %bitcast.294), custom_call_target="tpu_custom_call" | custom-call | flops 200000000 | bytes 6000000 | tf_op jit(solution)/shard_map/head/pallas_call | solution.py:85
  13.1 4.4 %shard_map.107 = (f32[64,2048]{1,0:T(8,128)S(1)}, bf16[8,5,256,256]{3,2,1,0:T(8,128)(2,1)S(1)}) custom-call(s32[32,5]{1,0:T(8,128)S(1)} %copy.11.refs_0_, bf16[64,8192]{1,0:T(8,128)(2,1)S(1)} %copy-done.8, bf16[32,5,256,256]{3,2,1,0:T(8,128)(2,1)} %refs_2_.7), custom_call_target="tpu_custom_call" | custom-call | flops 350000000 | bytes 6000000 | tf_op jit(solution)/shard_map/pallas_call | solution.py:186
  20.6 4.4 %shard_map.106 = (f32[64,2048]{1,0:T(8,128)S(1)}, bf16[8,5,256,256]{3,2,1,0:T(8,128)(2,1)S(1)}) custom-call(s32[32,5]{1,0:T(8,128)S(1)} %copy.11.refs_0_, bf16[64,8192]{1,0:T(8,128)(2,1)S(1)} %copy-done.8, bf16[32,5,256,256]{3,2,1,0:T(8,128)(2,1)} %refs_2_.7), custom_call_target="tpu_custom_call" | custom-call | flops 350000000 | bytes 6000000 | tf_op jit(solution)/shard_map/pallas_call | solution.py:186
  28.2 4.4 %shard_map.105 = (f32[64,2048]{1,0:T(8,128)S(1)}, bf16[8,5,256,256]{3,2,1,0:T(8,128)(2,1)S(1)}) custom-call(s32[32,5]{1,0:T(8,128)S(1)} %copy.11.refs_0_, bf16[64,8192]{1,0:T(8,128)(2,1)S(1)} %copy-done.8, bf16[32,5,256,256]{3,2,1,0:T(8,128)(2,1)} %refs_2_.7), custom_call_target="tpu_custom_call" | custom-call | flops 350000000 | bytes 6000000 | tf_op jit(solution)/shard_map/pallas_call | solution.py:186
  39.6 4.4 %shard_map.104 = (f32[64,2048]{1,0:T(8,128)S(1)}, bf16[8,5,256,256]{3,2,1,0:T(8,128)(2,1)S(1)}) custom-call(s32[32,5]{1,0:T(8,128)S(1)} %copy.11.refs_0_, bf16[64,8192]{1,0:T(8,128)(2,1)S(1)} %copy-done.9, bf16[32,5,256,256]{3,2,1,0:T(8,128)(2,1)} %refs_2_.7), custom_call_target="tpu_custom_call" | custom-call | flops 350000000 | bytes 6000000 | tf_op jit(solution)/shard_map/pallas_call | solution.py:186
  49.0 3.7 %collective-permute-done.2 = f32[64,64]{1,0:T(8,128)S(1)} collective-permute-done((f32[64,64]{1,0:T(8,128)S(1)}, f32[64,64]{1,0:T(8,128)S(1)}, u32[]{:S(2)}, u32[]{:S(2)}) %collective-permute-start.2) | collective-permute-done | bytes 16416 | tf_op jit(solution)/shard_map/ppermute | solution.py:347
  54.8 2.9 %collective-permute-start.3 = (bf16[64,6144]{1,0:T(8,128)(2,1)}, bf16[64,6144]{1,0:T(8,128)(2,1)S(1)}, u32[]{:S(2)}, u32[]{:S(2)}) collective-permute-start(bf16[64,6144]{1,0:T(8,128)(2,1)} %copy-done.27), channel_id=1, source_target_pairs={{2,4},{6,8},{10,12},{14,16},{18,20},{22,24},{26,28},{30,32},{34,36... | collective-permute-start | bytes 2359304 | tf_op jit(solution)/shard_map/ppermute | solution.py:353
  58.1 4.2 %collective-permute-start.5 = (f32[64,64]{1,0:T(8,128)S(1)}, f32[64,64]{1,0:T(8,128)S(1)}, u32[]{:S(2)}, u32[]{:S(2)}) collective-permute-start(f32[64,64]{1,0:T(8,128)S(1)} %convolution_add_fusion.8), channel_id=1, source_target_pairs={{0,24},{2,26},{4,28},{6,30},{8,16},{10,18},{12,20},{14,22},{16,8},... | collective-permute-start | bytes 49160 | tf_op jit(solution)/shard_map/ppermute | solution.py:347
  64.6 14.3 %collective-permute-start.6 = (f32[64,64]{1,0:T(8,128)S(1)}, f32[64,64]{1,0:T(8,128)S(1)}, u32[]{:S(2)}, u32[]{:S(2)}) collective-permute-start(f32[64,64]{1,0:T(8,128)S(1)} %convolution_add_fusion.7), channel_id=1, source_target_pairs={{0,32},{2,34},{4,36},{6,38},{8,40},{10,42},{12,44},{14,46},{16,48}... | collective-permute-start | bytes 49160 | tf_op jit(solution)/shard_map/ppermute | solution.py:347
  81.0 4.1 %collective-permute-start.7 = (f32[64,64]{1,0:T(8,128)S(1)}, f32[64,64]{1,0:T(8,128)S(1)}, u32[]{:S(2)}, u32[]{:S(2)}) collective-permute-start(f32[64,64]{1,0:T(8,128)S(1)} %convolution_add_fusion.6), channel_id=1, source_target_pairs={{0,96},{2,98},{4,100},{6,102},{8,104},{10,106},{12,108},{14,110},{... | collective-permute-start | bytes 49160 | tf_op jit(solution)/shard_map/ppermute | solution.py:347
  89.9 2.5 %copy-done.3 = bf16[8,5,256,256]{3,2,1,0:T(8,128)(2,1)S(1)} copy-done((bf16[8,5,256,256]{3,2,1,0:T(8,128)(2,1)S(1)}, bf16[8,5,256,256]{3,2,1,0:T(8,128)(2,1)}, u32[]{:S(2)}) %copy-start.3) | copy-done | bytes 5242904
  92.4 2.5 %copy-done.5 = bf16[8,5,256,256]{3,2,1,0:T(8,128)(2,1)S(1)} copy-done((bf16[8,5,256,256]{3,2,1,0:T(8,128)(2,1)S(1)}, bf16[8,5,256,256]{3,2,1,0:T(8,128)(2,1)}, u32[]{:S(2)}) %copy-start.5) | copy-done | bytes 5242904
  104.3 17.7 %tail.2 = (bf16[64,8192]{1,0:T(8,128)(2,1)}, bf16[64,6144]{1,0:T(8,128)(2,1)S(1)}, bf16[64,6144]{1,0:T(8,128)(2,1)S(1)}, f32[64,64]{1,0:T(8,128)S(1)}) custom-call(s32[5,32]{1,0:T(8,128)S(1)} %stack.5.refs_0_, s32[32,4]{1,0:T(8,128)S(1)} %copy.15.refs_1_, bf16[64,6144]{1,0:T(8,128)(2,1)S(1)} %collective-permute-done.1.refs_2_, ...), custom_call_target="tpu_custom_call" | custom-call | flops 1000000000 | bytes 10000000 | tf_op jit(solution)/shard_map/tail/pallas_call | solution.py:331
  123.4 2.5 %shard_map.111.refs_16_ = f32[64,2048]{1,0:T(8,128)S(1)} custom-call(s32[32,5]{1,0:T(8,128)S(1)} %copy.11.refs_0_, bf16[64,8192]{1,0:T(8,128)(2,1)S(1)} %copy-done.10, bf16[8,5,256,256]{3,2,1,0:T(8,128)(2,1)S(1)} %copy-done.1), custom_call_target="tpu_custom_call" | custom-call | flops 350000000 | bytes 6000000 | tf_op jit(solution)/shard_map/pallas_call | solution.py:186
  125.9 2.5 %shard_map.110.refs_15_ = f32[64,2048]{1,0:T(8,128)S(1)} custom-call(s32[32,5]{1,0:T(8,128)S(1)} %copy.11.refs_0_, bf16[64,8192]{1,0:T(8,128)(2,1)S(1)} %copy-done.10, bf16[8,5,256,256]{3,2,1,0:T(8,128)(2,1)S(1)} %copy-done.3), custom_call_target="tpu_custom_call" | custom-call | flops 350000000 | bytes 6000000 | tf_op jit(solution)/shard_map/pallas_call | solution.py:186
  128.4 2.5 %shard_map.109.refs_14_ = f32[64,2048]{1,0:T(8,128)S(1)} custom-call(s32[32,5]{1,0:T(8,128)S(1)} %copy.11.refs_0_, bf16[64,8192]{1,0:T(8,128)(2,1)S(1)} %copy-done.10, bf16[8,5,256,256]{3,2,1,0:T(8,128)(2,1)S(1)} %bitcast.293), custom_call_target="tpu_custom_call" | custom-call | flops 350000000 | bytes 6000000 | tf_op jit(solution)/shard_map/pallas_call | solution.py:186
  131.0 2.5 %shard_map.108.refs_13_ = f32[64,2048]{1,0:T(8,128)S(1)} custom-call(s32[32,5]{1,0:T(8,128)S(1)} %copy.11.refs_0_, bf16[64,8192]{1,0:T(8,128)(2,1)S(1)} %copy-done.10, bf16[8,5,256,256]{3,2,1,0:T(8,128)(2,1)S(1)} %copy-done.7), custom_call_target="tpu_custom_call" | custom-call | flops 350000000 | bytes 6000000 | tf_op jit(solution)/shard_map/pallas_call | solution.py:186
  136.7 3.8 %collective-permute-done.10 = f32[64,64]{1,0:T(8,128)S(1)} collective-permute-done((f32[64,64]{1,0:T(8,128)S(1)}, f32[64,64]{1,0:T(8,128)S(1)}, u32[]{:S(2)}, u32[]{:S(2)}) %collective-permute-start.10) | collective-permute-done | bytes 16416 | tf_op jit(solution)/shard_map/ppermute | solution.py:347
  141.9 3.6 %collective-permute-start.11 = (bf16[64,6144]{1,0:T(8,128)(2,1)S(1)}, bf16[64,6144]{1,0:T(8,128)(2,1)S(1)}, u32[]{:S(2)}, u32[]{:S(2)}) collective-permute-start(bf16[64,6144]{1,0:T(8,128)(2,1)S(1)} %get-tuple-element.50), channel_id=1, source_target_pairs={{2,4},{6,8},{10,12},{14,16},{18,20},{22,24},{26,28},{30,32},{34,36... | collective-permute-start | bytes 2359304 | tf_op jit(solution)/shard_map/ppermute | solution.py:353
  145.6 15.6 %collective-permute-done.12 = f32[64,64]{1,0:T(8,128)S(1)} collective-permute-done((f32[64,64]{1,0:T(8,128)S(1)}, f32[64,64]{1,0:T(8,128)S(1)}, u32[]{:S(2)}, u32[]{:S(2)}) %collective-permute-start.12) | collective-permute-done | bytes 16416 | tf_op jit(solution)/shard_map/ppermute | solution.py:347
  161.5 2.6 %collective-permute-start.13 = (f32[64,64]{1,0:T(8,128)S(1)}, f32[64,64]{1,0:T(8,128)S(1)}, u32[]{:S(2)}, u32[]{:S(2)}) collective-permute-start(f32[64,64]{1,0:T(8,128)S(1)} %convolution_add_fusion.2), channel_id=1, source_target_pairs={{0,24},{2,26},{4,28},{6,30},{8,16},{10,18},{12,20},{14,22},{16,8},... | collective-permute-start | bytes 49160 | tf_op jit(solution)/shard_map/ppermute | solution.py:347
  168.1 2.9 %collective-permute-done.14 = f32[64,64]{1,0:T(8,128)S(1)} collective-permute-done((f32[64,64]{1,0:T(8,128)S(1)}, f32[64,64]{1,0:T(8,128)S(1)}, u32[]{:S(2)}, u32[]{:S(2)}) %collective-permute-start.14) | collective-permute-done | bytes 16416 | tf_op jit(solution)/shard_map/ppermute | solution.py:347
  171.2 3.7 %collective-permute-start.15 = (f32[64,64]{1,0:T(8,128)S(1)}, f32[64,64]{1,0:T(8,128)S(1)}, u32[]{:S(2)}, u32[]{:S(2)}) collective-permute-start(f32[64,64]{1,0:T(8,128)S(1)} %convolution_add_fusion), channel_id=1, source_target_pairs={{0,96},{2,98},{4,100},{6,102},{8,104},{10,106},{12,108},{14,110},{... | collective-permute-start | bytes 49160 | tf_op jit(solution)/shard_map/ppermute | solution.py:347
  177.3 14.1 %tail.3 = bf16[64,8192]{1,0:T(8,128)(2,1)} custom-call(s32[5,32]{1,0:T(8,128)S(1)} %stack.5.refs_0_, s32[32,4]{1,0:T(8,128)S(1)} %copy.15.refs_1_, bf16[64,6144]{1,0:T(8,128)(2,1)S(1)} %collective-permute-done.9.refs_2_, bf16[64,6144]{1,0:T(8,128)(2,1)S(1)} %collective-permute-done.11.refs_3_, bf16[64,6144]{1,0:T(8,128)(2,1)S(1)} %get-tuple-element.47.refs_4_, ...), custom_call_target="tpu_custom_call" | custom-call | flops 1000000000 | bytes 10000000 | tf_op jit(solution)/shard_map/tail/pallas_call | solution.py:331
  (134 shorter events, 59.1 us)
Async XLA Ops:
  7.6 39.6 %collective-permute-start = (f32[64,64]{1,0:T(8,128)S(1)}, f32[64,64]{1,0:T(8,128)S(1)}, u32[]{:S(2)}, u32[]{:S(2)}) collective-permute-start(f32[64,64]{1,0:T(8,128)S(1)} %get-tuple-element.28), channel_id=1, source_target_pairs={{0,2},{2,0},{4,6},{6,4},{8,10},{10,8},{12,14},{14,12},{16,18},{18,... | collective-permute-start | bytes 49160 | tf_op jit(solution)/shard_map/ppermute | solution.py:347
  28.2 11.4 %copy-start.9 = (bf16[64,8192]{1,0:T(8,128)(2,1)S(1)}, bf16[64,8192]{1,0:T(8,128)(2,1)}, u32[]{:S(2)}) copy-start(bf16[64,8192]{1,0:T(8,128)(2,1)} %refs_1_.9) | copy-start | bytes 3145732
  39.6 47.8 %copy-start.11 = (bf16[32,64,256]{2,1,0:T(8,128)(2,1)S(1)}, bf16[32,64,256]{2,1,0:T(8,128)(2,1)}, u32[]{:S(2)}) copy-start(bf16[32,64,256]{2,1,0:T(8,128)(2,1)} %refs_6_.3) | copy-start | bytes 3145732
  39.6 47.8 %copy-start.14 = (bf16[32,64,64]{2,1,0:T(8,128)(2,1)S(1)}, bf16[32,64,64]{2,1,0:T(8,128)(2,1)}, u32[]{:S(2)}) copy-start(bf16[32,64,64]{2,1,0:T(8,128)(2,1)} %param.13) | copy-start | bytes 786436
  47.4 5.2 %collective-permute-start.2 = (f32[64,64]{1,0:T(8,128)S(1)}, f32[64,64]{1,0:T(8,128)S(1)}, u32[]{:S(2)}, u32[]{:S(2)}) collective-permute-start(f32[64,64]{1,0:T(8,128)S(1)} %convolution_add_fusion.11), channel_id=1, source_target_pairs={{0,6},{2,4},{4,2},{6,0},{8,14},{10,12},{12,10},{14,8},{16,22},{18,... | collective-permute-start | bytes 49160 | tf_op jit(solution)/shard_map/ppermute | solution.py:347
  48.8 38.6 %collective-permute-start.1 = (bf16[64,6144]{1,0:T(8,128)(2,1)}, bf16[64,6144]{1,0:T(8,128)(2,1)S(1)}, u32[]{:S(2)}, u32[]{:S(2)}) collective-permute-start(bf16[64,6144]{1,0:T(8,128)(2,1)} %copy-done.17), channel_id=1, source_target_pairs={{0,2},{2,0},{4,6},{6,4},{8,10},{10,8},{12,14},{14,12},{16,18},{18,... | collective-permute-start | bytes 2359304 | tf_op jit(solution)/shard_map/ppermute | solution.py:347
  53.0 4.8 %collective-permute-start.4 = (f32[64,64]{1,0:T(8,128)S(1)}, f32[64,64]{1,0:T(8,128)S(1)}, u32[]{:S(2)}, u32[]{:S(2)}) collective-permute-start(f32[64,64]{1,0:T(8,128)S(1)} %convolution_add_fusion.9), channel_id=1, source_target_pairs={{0,8},{2,10},{4,12},{6,14},{8,0},{10,2},{12,4},{14,6},{16,24},{18,... | collective-permute-start | bytes 49160 | tf_op jit(solution)/shard_map/ppermute | solution.py:347
  54.8 32.6 %collective-permute-start.3 = (bf16[64,6144]{1,0:T(8,128)(2,1)}, bf16[64,6144]{1,0:T(8,128)(2,1)S(1)}, u32[]{:S(2)}, u32[]{:S(2)}) collective-permute-start(bf16[64,6144]{1,0:T(8,128)(2,1)} %copy-done.27), channel_id=1, source_target_pairs={{2,4},{6,8},{10,12},{14,16},{18,20},{22,24},{26,28},{30,32},{34,36... | collective-permute-start | bytes 2359304 | tf_op jit(solution)/shard_map/ppermute | solution.py:353
  58.1 6.1 %collective-permute-start.5 = (f32[64,64]{1,0:T(8,128)S(1)}, f32[64,64]{1,0:T(8,128)S(1)}, u32[]{:S(2)}, u32[]{:S(2)}) collective-permute-start(f32[64,64]{1,0:T(8,128)S(1)} %convolution_add_fusion.8), channel_id=1, source_target_pairs={{0,24},{2,26},{4,28},{6,30},{8,16},{10,18},{12,20},{14,22},{16,8},... | collective-permute-start | bytes 49160 | tf_op jit(solution)/shard_map/ppermute | solution.py:347
  64.6 16.2 %collective-permute-start.6 = (f32[64,64]{1,0:T(8,128)S(1)}, f32[64,64]{1,0:T(8,128)S(1)}, u32[]{:S(2)}, u32[]{:S(2)}) collective-permute-start(f32[64,64]{1,0:T(8,128)S(1)} %convolution_add_fusion.7), channel_id=1, source_target_pairs={{0,32},{2,34},{4,36},{6,38},{8,40},{10,42},{12,44},{14,46},{16,48}... | collective-permute-start | bytes 49160 | tf_op jit(solution)/shard_map/ppermute | solution.py:347
  81.0 6.0 %collective-permute-start.7 = (f32[64,64]{1,0:T(8,128)S(1)}, f32[64,64]{1,0:T(8,128)S(1)}, u32[]{:S(2)}, u32[]{:S(2)}) collective-permute-start(f32[64,64]{1,0:T(8,128)S(1)} %convolution_add_fusion.6), channel_id=1, source_target_pairs={{0,96},{2,98},{4,100},{6,102},{8,104},{10,106},{12,108},{14,110},{... | collective-permute-start | bytes 49160 | tf_op jit(solution)/shard_map/ppermute | solution.py:347
  128.4 48.8 %slice-start = ((s8[5242880]{0:T(1024)(128)(4,1)}), s8[4194304]{0:T(1024)(128)(4,1)S(1)}, s32[]{:S(2)}) async-start(s8[5242880]{0:T(1024)(128)(4,1)} %bitcast.288), calls=%async_computation | async-start | bytes 8388608
  128.4 48.8 %slice-start.2 = ((s8[5242880]{0:T(1024)(128)(4,1)}), s8[4194304]{0:T(1024)(128)(4,1)S(1)}, s32[]{:S(2)}) async-start(s8[5242880]{0:T(1024)(128)(4,1)} %bitcast.290), calls=%async_computation.2 | async-start | bytes 8388608
  130.9 46.3 %copy-start.13 = (bf16[32,4,64,64]{3,2,1,0:T(8,128)(2,1)S(1)}, bf16[32,4,64,64]{3,2,1,0:T(8,128)(2,1)}, u32[]{:S(2)}) copy-start(bf16[32,4,64,64]{3,2,1,0:T(8,128)(2,1)} %refs_8_.3) | copy-start | bytes 3145732
  130.9 46.3 %slice-start.1 = ((s8[5242880]{0:T(1024)(128)(4,1)}), s8[1048576]{0:T(1024)(128)(4,1)S(1)}, s32[]{:S(2)}) async-start(s8[5242880]{0:T(1024)(128)(4,1)} %bitcast.288), calls=%async_computation.1 | async-start | bytes 2097152
  130.9 46.3 %slice-start.3 = ((s8[5242880]{0:T(1024)(128)(4,1)}), s8[1048576]{0:T(1024)(128)(4,1)S(1)}, s32[]{:S(2)}) async-start(s8[5242880]{0:T(1024)(128)(4,1)} %bitcast.290), calls=%async_computation.3 | async-start | bytes 2097152
  131.0 4.0 %collective-permute-start.8 = (f32[64,64]{1,0:T(8,128)S(1)}, f32[64,64]{1,0:T(8,128)S(1)}, u32[]{:S(2)}, u32[]{:S(2)}) collective-permute-start(f32[64,64]{1,0:T(8,128)S(1)} %get-tuple-element.46), channel_id=1, source_target_pairs={{0,2},{2,0},{4,6},{6,4},{8,10},{10,8},{12,14},{14,12},{16,18},{18,... | collective-permute-start | bytes 49160 | tf_op jit(solution)/shard_map/ppermute | solution.py:347
  135.3 5.2 %collective-permute-start.10 = (f32[64,64]{1,0:T(8,128)S(1)}, f32[64,64]{1,0:T(8,128)S(1)}, u32[]{:S(2)}, u32[]{:S(2)}) collective-permute-start(f32[64,64]{1,0:T(8,128)S(1)} %convolution_add_fusion.5), channel_id=1, source_target_pairs={{0,6},{2,4},{4,2},{6,0},{8,14},{10,12},{12,10},{14,8},{16,22},{18,... | collective-permute-start | bytes 49160 | tf_op jit(solution)/shard_map/ppermute | solution.py:347
  136.6 40.6 %collective-permute-start.9 = (bf16[64,6144]{1,0:T(8,128)(2,1)S(1)}, bf16[64,6144]{1,0:T(8,128)(2,1)S(1)}, u32[]{:S(2)}, u32[]{:S(2)}) collective-permute-start(bf16[64,6144]{1,0:T(8,128)(2,1)S(1)} %get-tuple-element.47.refs_4_), channel_id=1, source_target_pairs={{0,2},{2,0},{4,6},{6,4},{8,10},{10,8},{12,14},{14,12},{16,18},{18,... | collective-permute-start | bytes 2359304 | tf_op jit(solution)/shard_map/ppermute | solution.py:347
  140.9 20.3 %collective-permute-start.12 = (f32[64,64]{1,0:T(8,128)S(1)}, f32[64,64]{1,0:T(8,128)S(1)}, u32[]{:S(2)}, u32[]{:S(2)}) collective-permute-start(f32[64,64]{1,0:T(8,128)S(1)} %convolution_add_fusion.3), channel_id=1, source_target_pairs={{0,8},{2,10},{4,12},{6,14},{8,0},{10,2},{12,4},{14,6},{16,24},{18,... | collective-permute-start | bytes 49160 | tf_op jit(solution)/shard_map/ppermute | solution.py:347
  141.9 35.3 %collective-permute-start.11 = (bf16[64,6144]{1,0:T(8,128)(2,1)S(1)}, bf16[64,6144]{1,0:T(8,128)(2,1)S(1)}, u32[]{:S(2)}, u32[]{:S(2)}) collective-permute-start(bf16[64,6144]{1,0:T(8,128)(2,1)S(1)} %get-tuple-element.50), channel_id=1, source_target_pairs={{2,4},{6,8},{10,12},{14,16},{18,20},{22,24},{26,28},{30,32},{34,36... | collective-permute-start | bytes 2359304 | tf_op jit(solution)/shard_map/ppermute | solution.py:353
  161.5 5.2 %collective-permute-start.13 = (f32[64,64]{1,0:T(8,128)S(1)}, f32[64,64]{1,0:T(8,128)S(1)}, u32[]{:S(2)}, u32[]{:S(2)}) collective-permute-start(f32[64,64]{1,0:T(8,128)S(1)} %convolution_add_fusion.2), channel_id=1, source_target_pairs={{0,24},{2,26},{4,28},{6,30},{8,16},{10,18},{12,20},{14,22},{16,8},... | collective-permute-start | bytes 49160 | tf_op jit(solution)/shard_map/ppermute | solution.py:347
  167.0 4.0 %collective-permute-start.14 = (f32[64,64]{1,0:T(8,128)S(1)}, f32[64,64]{1,0:T(8,128)S(1)}, u32[]{:S(2)}, u32[]{:S(2)}) collective-permute-start(f32[64,64]{1,0:T(8,128)S(1)} %convolution_add_fusion.1), channel_id=1, source_target_pairs={{0,32},{2,34},{4,36},{6,38},{8,40},{10,42},{12,44},{14,46},{16,48}... | collective-permute-start | bytes 49160 | tf_op jit(solution)/shard_map/ppermute | solution.py:347
  171.2 5.6 %collective-permute-start.15 = (f32[64,64]{1,0:T(8,128)S(1)}, f32[64,64]{1,0:T(8,128)S(1)}, u32[]{:S(2)}, u32[]{:S(2)}) collective-permute-start(f32[64,64]{1,0:T(8,128)S(1)} %convolution_add_fusion), channel_id=1, source_target_pairs={{0,96},{2,98},{4,100},{6,102},{8,104},{10,106},{12,108},{14,110},{... | collective-permute-start | bytes 49160 | tf_op jit(solution)/shard_map/ppermute | solution.py:347
  (27 other events, 61.5 us)

commit v3 on v2

v3 whole, which is shorter than its diff:
```python
import jax
import jax.numpy as jnp
from jax import lax
from jax.experimental import pallas as pl
from jax.experimental.pallas import tpu as pltpu
from jax.sharding import PartitionSpec as P


REACH = 16
FARR = 32
PIECES = 4
TOGETHER = 4
STRIDE = 40
BF = jnp.bfloat16
F32 = jnp.float32
NT = (((1,), (1,)), ((), ()))
NN = (((1,), (0,)), ((), ()))
HBM = pl.BlockSpec(memory_space=pltpu.HBM)
VMEM = pl.BlockSpec(memory_space=pltpu.VMEM)


def mm(a, b, dims=NN):
    return lax.dot_general(a, b, dims, preferred_element_type=F32)


def exact(a, b, dims=NN):
    return lax.dot_general(
        a, b, dims, precision=lax.Precision.HIGHEST, preferred_element_type=F32
    )


def params(mib):
    return pltpu.CompilerParams(vmem_limit_bytes=mib * 2**20)


def cost(flops, moved):
    return pl.CostEstimate(flops=flops, bytes_accessed=moved, transcendentals=0)


def is_even():
    return (lax.axis_index("leaf") & 1) == 0


def columns_of(start, width):
    return pl.ds(pl.multiple_of(start, width), width)


def split_body(v, va, vb, sems):
    half = va.shape[1]
    start_a = jnp.where(is_even(), half, 0)
    copies = [
        pltpu.make_async_copy(v.at[:, columns_of(start, half)], out, sems.at[i])
        for i, (out, start) in enumerate(((va, start_a), (vb, half - start_a)))
    ]
    for copy in copies:
        copy.start()
    for copy in copies:
        copy.wait()


def split(vectors):
    columns, own = vectors.shape
    return pl.pallas_call(
        split_body,
        in_specs=[HBM],
        out_specs=[VMEM] * 2,
        out_shape=[jax.ShapeDtypeStruct((columns, own // 2), BF)] * 2,
        scratch_shapes=[pltpu.SemaphoreType.DMA((2,))],
        compiler_params=params(4),
        cost_estimate=cost(0, 2_000_000),
        name="split",
    )(pltpu.with_memory_space_constraint(vectors, pltpu.HBM))


def head_body(va, vb, basis_hbm, trans_hbm, coef, node, basis, trans, sems):
    leaves, rank, points = basis.shape
    first_a = jnp.where(is_even(), leaves // 2, 0)
    copies = [
        pltpu.make_async_copy(basis_hbm, basis, sems.at[0]),
        pltpu.make_async_copy(trans_hbm, trans, sems.at[1]),
    ]
    for copy in copies:
        copy.start()
    for copy in copies:
        copy.wait()
    total = None
    for v, first in ((va, first_a), (vb, leaves // 2 - first_a)):
        for pair in range(leaves // 4):
            parts = [
                mm(v[:, leaf * points : (leaf + 1) * points], basis[first + leaf], NT)
                for leaf in (2 * pair, 2 * pair + 1)
            ]
            both = jnp.concatenate(parts, axis=1).astype(BF)
            at = columns_of((first // 2 + pair) * 2 * rank, 2 * rank)
            coef[:, at] = both
            term = mm(both, trans[at, :])
            total = term if total is None else total + term
    node[...] = total


def head(va, vb, basis_t, trans2):
    columns = va.shape[0]
    leaves, rank, _ = basis_t.shape
    hbm = (pltpu.with_memory_space_constraint(x, pltpu.HBM) for x in (basis_t, trans2))
    return pl.pallas_call(
        head_body,
        in_specs=[VMEM] * 2 + [HBM] * 2,
        out_specs=[VMEM] * 2,
        out_shape=[
            jax.ShapeDtypeStruct((columns, leaves * rank), BF),
            jax.ShapeDtypeStruct((columns, rank), F32),
        ],
        scratch_shapes=[
            pltpu.VMEM(basis_t.shape, BF),
            pltpu.VMEM(trans2.shape, BF),
            pltpu.SemaphoreType.DMA((2,)),
        ],
        compiler_params=params(6),
        cost_estimate=cost(200_000_000, 6_000_000),
        name="head",
    )(va, vb, *hbm)


def table_body(levels, near_list, trans_hbm, couple_hbm, near, up, down, plan, kept, *scratch):
    trans, couple, own, pair, sems = scratch
    copies = [
        pltpu.make_async_copy(trans_hbm, trans, sems.at[0]),
        pltpu.make_async_copy(couple_hbm, couple, sems.at[1]),
        pltpu.make_async_copy(near.at[pl.ds(0, kept.shape[0])], kept, sems.at[2]),
    ]
    for copy in copies:
        copy.start()
    device = lax.axis_index("leaf")
    kn, leaves = near_list.shape
    some = leaves // PIECES
    first = device * leaves

    for piece in range(PIECES):

        def scan(i, n, piece=piece):
            leaf = piece * some + i
            for s in range(kn):
                source = near_list[s, leaf] - first
                left = source < 0
                place = source + jnp.where(left, REACH, REACH - leaves)
                plan[piece * STRIDE + n] = (leaf * 8 + s) * 32 + place
                n = n + jnp.where(left | (source >= leaves), 1, 0)
            return n

        count = lax.fori_loop(0, some, scan, 0)
        for i in range(TOGETHER):
            plan[piece * STRIDE + count + i] = (leaves * 8) * 32
        plan[PIECES * STRIDE + piece] = lax.div(count + TOGETHER - 1, TOGETHER)

    count, rows, nodes = 8, trans.shape[0], trans.shape[2]
    row = lax.broadcasted_iota(jnp.int32, (count, nodes), 0)
    node = lax.broadcasted_iota(jnp.int32, (count, nodes), 1)
    offset = (2 << levels) - lax.shift_right_logical(jnp.full_like(row, 2 << levels), row)
    here = offset + lax.shift_right_logical(jnp.zeros_like(row) + device, row)
    there = jnp.bitwise_xor(here, 1)
    wanted = row < levels
    pick_here = jnp.where(wanted & (node == here), 1.0, 0.0).astype(BF)
    pick_there = jnp.where(wanted & (node == there), 1.0, 0.0).astype(BF)
    both = jnp.concatenate([pick_here, pick_there], axis=0)
    copies[0].wait()
    copies[1].wait()
    for k in range(rows):
        own[:, k, :] = mm(both, trans[k], NT)
        pair[:, k, :] = mm(pick_here, couple[k], NT)
    for t in range(levels):
        up[t, 0] = own[t]
        up[t, 1] = own[count + t]
    down[0] = pair[0]
    path = own[0]
    for t in range(1, levels):
        down[t] = exact(path, pair[t])
        if t + 1 < levels:
            path = exact(path, own[t])
    copies[2].wait()


def table(top_transfer, top_couple, near_list_t, near_blocks):
    nodes, rank, _ = top_transfer.shape
    levels = lax.axis_size("leaf").bit_length() - 1
    shape = near_blocks.shape
    hbm = (
        jnp.transpose(top_transfer, (1, 2, 0)),
        jnp.transpose(top_couple, (1, 2, 0)),
        near_blocks,
    )
    return pl.pallas_call(
        lambda *refs: table_body(levels, *refs),
        grid_spec=pltpu.PrefetchScalarGridSpec(
            num_scalar_prefetch=1,
            in_specs=[HBM] * 3,
            out_specs=[VMEM, VMEM, pl.BlockSpec(memory_space=pltpu.SMEM), VMEM],
            scratch_shapes=[
                pltpu.VMEM((rank, rank, nodes), BF),
                pltpu.VMEM((rank, rank, nodes), BF),
                pltpu.VMEM((16, rank, rank), F32),
                pltpu.VMEM((8, rank, rank), F32),
                pltpu.SemaphoreType.DMA((3,)),
            ],
        ),
        out_shape=[
            jax.ShapeDtypeStruct((levels, 2, rank, rank), F32),
            jax.ShapeDtypeStruct((levels, rank, rank), F32),
            jax.ShapeDtypeStruct((PIECES * STRIDE + 8,), jnp.int32),
            jax.ShapeDtypeStruct((shape[0] // PIECES, *shape[1:]), BF),
        ],
        compiler_params=params(6),
        cost_estimate=cost(10_000_000, 8_000_000),
        name="table",
    )(near_list_t, *(pltpu.with_memory_space_constraint(x, pltpu.HBM) for x in hbm))


def near_body(piece, load, near_list, v, kept, *refs):
    if load:
        near, total, later, sem = refs
        here = pl.ds((piece + 1) * later.shape[0], later.shape[0])
        copy = pltpu.make_async_copy(near.at[here], later, sem)
        copy.start()
    else:
        (total,) = refs
    some, kn, points, _ = kept.shape
    leaves = v.shape[1] // points
    first = lax.axis_index("leaf") * leaves
    for i in range(some):
        out = None
        for s in range(kn):
            source = near_list[s, piece * some + i] - first
            inside = (source >= 0) & (source < leaves)
            rows = v[:, columns_of(jnp.clip(source, 0, leaves - 1) * points, points)]
            term = mm(jnp.where(inside, rows, jnp.zeros_like(rows)), kept[i, s], NT)
            out = term if out is None else out + term
        total[:, i * points : (i + 1) * points] = out
    if load:
        copy.wait()


def near_piece(piece, near_list_t, v, near_blocks, kept, load):
    columns = v.shape[0]
    some, _, points, _ = kept.shape
    in_specs = [VMEM, VMEM]
    args = [v, kept]
    out_shape = [jax.ShapeDtypeStruct((columns, some * points), F32)]
    scratch = []
    if load:
        in_specs.append(HBM)
        args.append(pltpu.with_memory_space_constraint(near_blocks, pltpu.HBM))
        out_shape.append(jax.ShapeDtypeStruct(kept.shape, BF))
        scratch.append(pltpu.SemaphoreType.DMA)
    return pl.pallas_call(
        lambda *refs: near_body(piece, load, *refs),
        grid_spec=pltpu.PrefetchScalarGridSpec(
            num_scalar_prefetch=1,
            in_specs=in_specs,
            out_specs=[VMEM] * len(out_shape),
            scratch_shapes=scratch,
        ),
        out_shape=out_shape,
        compiler_params=params(4),
        cost_estimate=cost(350_000_000, 6_000_000),
    )(near_list_t, *args)


def tail_body(more, plan, couple_list, *refs):
    got_va, got_vb, got_ca, got_cb, sent_c, top, basis, trans, couple = refs[:9]
    refs = refs[9:]
    kept, partial, refs = refs[:PIECES], refs[PIECES : 2 * PIECES], refs[2 * PIECES :]
    if more:
        image, own_v, va, vb, coef, node, table_ref, wide, acc, total_ref, sems = refs
    else:
        image, own_v, table_ref, wide, acc, sems = refs
    leaves, rank, points = basis.shape
    some = leaves // PIECES
    half = leaves // 2 * points
    even = is_even()
    first = lax.axis_index("leaf") * leaves
    start_a = jnp.where(even, half, 0)
    copies = [
        pltpu.make_async_copy(ref, wide.at[:, columns_of(start, half)], sems.at[i])
        for i, (ref, start) in enumerate(((got_va, start_a), (got_vb, half - start_a)))
    ]
    for copy in copies:
        copy.start()
    base_a = jnp.where(even, 2 * leaves, 0)
    for ref, base in ((got_ca, base_a), (sent_c, leaves), (got_cb, 2 * leaves - base_a)):
        for pair in range(leaves // 2):
            both = ref[:, 2 * rank * pair : 2 * rank * (pair + 1)]
            table_ref[base + 2 * pair] = both[:, :rank]
            table_ref[base + 2 * pair + 1] = both[:, rank:]
    high = top[...].astype(BF)
    low = (top[...] - high.astype(F32)).astype(BF)
    if more:
        total_ref[...] = jnp.zeros_like(total_ref)
    for piece in range(PIECES):
        width = some * points
        acc[:, piece * width : (piece + 1) * width] = partial[piece][...]
    for copy in copies:
        copy.wait()
    writes = []
    for piece in range(PIECES):
        near = kept[piece]

        def add(j, carry, near=near, piece=piece):
            terms = []
            for i in range(TOGETHER):
                code = plan[piece * STRIDE + j * TOGETHER + i]
                block = lax.shift_right_logical(code, 5)
                leaf = lax.shift_right_logical(code, 8)
                rows = wide[:, columns_of((code & 31) * points, points)]
                term = mm(rows, near[leaf & (some - 1), block & 7], NT)
                terms.append((columns_of(leaf * points, points), term))
            for here, term in terms:
                acc[:, here] += term
            return carry

        lax.fori_loop(0, plan[PIECES * STRIDE + piece], add, 0)
        results = []
        for i in range(some):
            leaf = piece * some + i
            moved = trans[leaf * rank : (leaf + 1) * rank, :]
            local = mm(high, moved, NT) + mm(low, moved, NT)
            for s in range(couple.shape[1]):
                local += mm(table_ref[couple_list[s, leaf] - first + FARR], couple[leaf, s], NT)
            here = slice(leaf * points, (leaf + 1) * points)
            value = (acc[:, here] + mm(local.astype(BF), basis[leaf])).astype(BF)
            results.append(value)
            own_v[:, here] = value
        here = pl.ds(piece * some * points, some * points)
        writes.append(pltpu.make_async_copy(own_v.at[:, here], image.at[:, here], sems.at[2 + piece]))
        writes[-1].start()
        if not more:
            continue
        for pair in range(some // 2):
            leaf = piece * some + 2 * pair
            parts = [mm(results[2 * pair + i], basis[leaf + i], NT) for i in range(2)]
            both = jnp.concatenate(parts, axis=1).astype(BF)
            coef[:, leaf * rank : (leaf + 2) * rank] = both
            total_ref[...] += mm(both, trans[leaf * rank : (leaf + 2) * rank, :])
        in_right = piece >= PIECES // 2
        start = piece % (PIECES // 2) * some * points

        def put(message, results=results, start=start):
            for i, value in enumerate(results):
                message[:, start + i * points : start + (i + 1) * points] = value

        @pl.when(even == in_right)
        def _():
            put(va)

        @pl.when(even != in_right)
        def _():
            put(vb)

    if more:
        node[...] = total_ref[...]
    for write in writes:
        write.wait()


def tail(more, lists, got, sent_c, top, kept, partial, basis_t, trans2, leaf_couple):
    columns = sent_c.shape[0]
    leaves, rank, points = basis_t.shape
    own = leaves * points
    image = jax.ShapeDtypeStruct((columns, own), BF)
    out_shape, out_specs = [image], [HBM]
    scratch = [
        pltpu.VMEM((3 * leaves, columns, rank), BF),
        pltpu.VMEM((columns, own), BF),
        pltpu.VMEM((columns, own + points), F32),
    ]
    if more:
        half = jax.ShapeDtypeStruct((columns, own // 2), BF)
        out_shape += [
            image,
            half,
            half,
            jax.ShapeDtypeStruct((columns, leaves * rank), BF),
            jax.ShapeDtypeStruct((columns, rank), F32),
        ]
        out_specs += [VMEM] * 5
        scratch.append(pltpu.VMEM((columns, rank), F32))
    else:
        scratch.insert(0, pltpu.VMEM((columns, own), BF))
    scratch.append(pltpu.SemaphoreType.DMA((2 + PIECES,)))
    return pl.pallas_call(
        lambda *refs: tail_body(more, *refs),
        grid_spec=pltpu.PrefetchScalarGridSpec(
            num_scalar_prefetch=2,
            in_specs=[VMEM] * (9 + 2 * PIECES),
            out_specs=out_specs,
            scratch_shapes=scratch,
        ),
        out_shape=out_shape,
        compiler_params=params(12),
        cost_estimate=cost(1_000_000_000, 10_000_000),
        name="tail",
    )(*lists, *got, sent_c, top, basis_t, trans2, leaf_couple, *kept, *partial)


def swapped(value, mask):
    return lax.ppermute(value, "leaf", [(i, i ^ mask) for i in range(lax.axis_size("leaf"))])


def swapped_odd(value):
    size = lax.axis_size("leaf")
    pairs = [(i, i + 1) for i in range(1, size - 1, 2)]
    return lax.ppermute(value, "leaf", pairs + [(j, i) for i, j in pairs])


def one_product(node, va, vb, coef, got_va, got_vb, fill, tables):
    levels = lax.axis_size("leaf").bit_length() - 1
    top = jnp.zeros_like(node)
    got_ca = got_cb = None
    for t in range(levels):
        mask = (1 << t) if t % 2 == 0 else 3 << (t - 1)
        other = swapped(node, mask)
        fill(t)
        up, down = tables()
        if t == 0:
            va, coef, other = lax.optimization_barrier((va, coef, other))
            if got_va is None:
                got_va = swapped(va, 1)
            got_ca = swapped(coef, 1)
        if t == 3:
            vb, later, other = lax.optimization_barrier((vb, coef, other))
            if got_vb is None:
                got_vb = swapped_odd(vb)
            got_cb = swapped_odd(later)
        if t + 1 < levels:
            node = exact(node, up[t, 0]) + exact(other, up[t, 1])
        top += exact(other, down[t], NT)
    return top, (got_va, got_vb, got_ca, got_cb)


def on_device(
    rhs_block,
    basis_t,
    near_blocks,
    near_list,
    leaf_transfer,
    couple_list,
    leaf_couple,
    top_transfer,
    top_couple,
):
    leaves, rank, _ = leaf_transfer.shape
    trans2 = leaf_transfer.reshape(leaves * rank, rank)
    near_list_t, couple_list_t = near_list.T, couple_list.T
    made = {}
    kept, partial = [], []

    def fill_first(t):
        if t == 0:
            made["up"], made["down"], made["plan"], block = table(
                top_transfer, top_couple, near_list_t, near_blocks
            )
            kept.append(block)
        elif t <= PIECES:
            piece = t - 1
            out = near_piece(
                piece, near_list_t, rhs_block, near_blocks, kept[piece], piece + 1 < PIECES
            )
            partial.append(out[0])
            kept.extend(out[1:])

    def tables():
        return made["up"], made["down"]

    va, vb = split(rhs_block)
    got_va = swapped(va, 1)
    got_vb = swapped_odd(vb)
    coef, node = head(va, vb, basis_t, trans2)
    top, got = one_product(node, va, vb, coef, got_va, got_vb, fill_first, tables)
    lists = (made["plan"], couple_list_t)
    first_image, own_v, va, vb, coef_next, node = tail(
        True, lists, got, coef, top, kept, partial, basis_t, trans2, leaf_couple
    )
    again = []

    def fill_second(t):
        if t < PIECES:
            (out,) = near_piece(t, near_list_t, own_v, near_blocks, kept[t], False)
            again.append(out)

    top, got = one_product(node, va, vb, coef_next, None, None, fill_second, tables)
    (second_image,) = tail(
        False, lists, got, coef_next, top, kept, again, basis_t, trans2, leaf_couple
    )
    return (first_image, second_image)


def solution(mesh):
    in_specs = (
        P("rhs", "leaf"),
        P("leaf", None, None),
        P("leaf", None, None, None),
        P("leaf", None),
        P("leaf", None, None),
        P("leaf", None),
        P("leaf", None, None, None),
        P(),
        P(),
    )
    out_specs = (P("rhs", "leaf"), P("rhs", "leaf"))
    return jax.shard_map(
        on_device, mesh=mesh, in_specs=in_specs, out_specs=out_specs, check_vma=False
    )
```

time: 192 us -> 149 us (0.78)
  the two profiles are of different devices: /device:TPU:6 before, /device:TPU:96 now
where the time goes in v3:
time: 149 us; the launch traced here: 148 us
  Pallas kernels  62.8 us (42%)
  starting transfers between devices  39.5 us (27%)
  waiting for transfers between devices  37.8 us (25%)
  matrix products  5.45 us (4%)
    ppermute x16, waiting for transfers between devices, swapped(): lax.ppermute(value, 'leaf', [(i, i ^ mask) for i in range(lax.axis_size('...  33.5 us
    pallas_call x2, Pallas kernels, tail(): pl.pallas_call(lambda *refs: tail_body(more, *refs), grid_spec=pltpu.Pref...  27.9 us
    pallas_call x8, Pallas kernels, near_piece(): pl.pallas_call(lambda *refs: near_body(piece, load, *refs), grid_spec=plt...  25.2 us
    ppermute x4, starting transfers between devices, swapped_odd(): return lax.ppermute(value, 'leaf', pairs + [(j, i) for i, j in pairs])  21 us
    ppermute x16, starting transfers between devices, swapped(): lax.ppermute(value, 'leaf', [(i, i ^ mask) for i in range(lax.axis_size('...  18.5 us
    dot_general x32, matrix products, exact(): lax.dot_general(a, b, dims, precision=lax.Precision.HIGHEST, preferred_el...  5.45 us
    pallas_call x1, Pallas kernels, table(): pl.pallas_call(lambda *refs: table_body(levels, *refs), grid_spec=pltpu.P...  5.03 us
    ppermute x4, waiting for transfers between devices, swapped_odd(): return lax.ppermute(value, 'leaf', pairs + [(j, i) for i, j in pairs])  4.29 us
  transfers between devices with their start and end apart: 20, of which 11 were waited for; matrix products, arithmetic and copies ran while one was open for 3% of the time, Pallas kernels for 18%

profile of v3, /device:TPU:96, one launch (start us, length us, event | category | flops | bytes accessed | tf_op | source)
XLA Modules:
  0.0 147.5 jit_solution(1642097555162132391)
XLA Ops:
  3.4 6.3 %collective-permute-start.1 = (bf16[64,4096]{1,0:T(8,128)(2,1)S(1)}, bf16[64,4096]{1,0:T(8,128)(2,1)S(1)}, u32[]{:S(2)}, u32[]{:S(2)}) collective-permute-start(bf16[64,4096]{1,0:T(8,128)(2,1)S(1)} %get-tuple-element.34.vb), channel_id=1, source_target_pairs={{2,4},{6,8},{10,12},{14,16},{18,20},{22,24},{26,28},{30,32},{34,36... | collective-permute-start | bytes 1572872 | tf_op jit(solution)/shard_map/ppermute | solution.py:410
  9.7 3.4 %head.1 = (bf16[64,2048]{1,0:T(8,128)(2,1)S(1)}, f32[64,64]{1,0:T(8,128)S(1)}) custom-call(bf16[64,4096]{1,0:T(8,128)(2,1)S(1)} %get-tuple-element.33.va, bf16[64,4096]{1,0:T(8,128)(2,1)S(1)} %get-tuple-element.34.vb, bf16[32,64,256]{2,1,0:T(8,128)(2,1)} %refs_8_.3, bf16[2048,64]{1,0:T(8,128)(2,1)} %bitcast.117), custom_call_target="tpu_custom_call" | custom-call | flops 200000000 | bytes 6000000 | tf_op jit(solution)/shard_map/head/pallas_call | solution.py:105
  13.9 5.0 %table.1 = (f32[6,2,64,64]{3,2,1,0:T(8,128)S(1)}, f32[6,64,64]{2,1,0:T(8,128)S(1)}, s32[168]{0:T(256)S(1)}, bf16[8,5,256,256]{3,2,1,0:T(8,128)(2,1)S(1)}) custom-call(s32[5,32]{1,0:T(8,128)S(1)} %bitcast.120, bf16[64,64,126]{2,1,0:T(8,128)(2,1)} %bitcast.131, bf16[64,64,126]{2,1,0:T(8,128)(2,1)} %bitcast.132, bf16[32,5,256,256]{3,2,1,0:T(8,128)(2,1)} %refs_3_.7), custom_call_target="tpu_custom_call" | custom-call | flops 10000000 | bytes 8000000 | tf_op jit(solution)/shard_map/table/pallas_call | solution.py:191
  19.1 4.6 %shard_map.104 = (f32[64,2048]{1,0:T(8,128)S(1)}, bf16[8,5,256,256]{3,2,1,0:T(8,128)(2,1)S(1)}) custom-call(s32[5,32]{1,0:T(8,128)S(1)} %bitcast.121, bf16[64,8192]{1,0:T(8,128)(2,1)S(1)} %copy-done, bf16[8,5,256,256]{3,2,1,0:T(8,128)(2,1)S(1)} %get-tuple-element.43.refs_2_.refs_11_, bf16[32,5,256,256]{3,2,1,0:T(8,128)(2,1)} %refs_3_.7), custom_call_target="tpu_custom_call" | custom-call | flops 350000000 | bytes 6000000 | tf_op jit(solution)/shard_map/pallas_call | solution.py:253
  23.7 4.6 %shard_map.105 = (f32[64,2048]{1,0:T(8,128)S(1)}, bf16[8,5,256,256]{3,2,1,0:T(8,128)(2,1)S(1)}) custom-call(s32[5,32]{1,0:T(8,128)S(1)} %bitcast.122, bf16[64,8192]{1,0:T(8,128)(2,1)S(1)} %copy-done, bf16[8,5,256,256]{3,2,1,0:T(8,128)(2,1)S(1)} %get-tuple-element.44.refs_2_.refs_12_, bf16[32,5,256,256]{3,2,1,0:T(8,128)(2,1)} %refs_3_.7), custom_call_target="tpu_custom_call" | custom-call | flops 350000000 | bytes 6000000 | tf_op jit(solution)/shard_map/pallas_call | solution.py:253
  28.3 4.6 %shard_map.106 = (f32[64,2048]{1,0:T(8,128)S(1)}, bf16[8,5,256,256]{3,2,1,0:T(8,128)(2,1)S(1)}) custom-call(s32[5,32]{1,0:T(8,128)S(1)} %bitcast.123, bf16[64,8192]{1,0:T(8,128)(2,1)S(1)} %copy-done, bf16[8,5,256,256]{3,2,1,0:T(8,128)(2,1)S(1)} %get-tuple-element.45.refs_2_.refs_13_, bf16[32,5,256,256]{3,2,1,0:T(8,128)(2,1)} %refs_3_.7), custom_call_target="tpu_custom_call" | custom-call | flops 350000000 | bytes 6000000 | tf_op jit(solution)/shard_map/pallas_call | solution.py:253
  32.9 2.3 %shard_map.107.refs_18_ = f32[64,2048]{1,0:T(8,128)S(1)} custom-call(s32[5,32]{1,0:T(8,128)S(1)} %bitcast.124, bf16[64,8192]{1,0:T(8,128)(2,1)S(1)} %copy-done, bf16[8,5,256,256]{3,2,1,0:T(8,128)(2,1)S(1)} %get-tuple-element.46.refs_2_.refs_14_), custom_call_target="tpu_custom_call" | custom-call | flops 350000000 | bytes 6000000 | tf_op jit(solution)/shard_map/pallas_call | solution.py:253
  37.7 2.9 %collective-permute-done.4 = f32[64,64]{1,0:T(8,128)S(1)} collective-permute-done((f32[64,64]{1,0:T(8,128)S(1)}, f32[64,64]{1,0:T(8,128)S(1)}, u32[]{:S(2)}, u32[]{:S(2)}) %collective-permute-start.4) | collective-permute-done | bytes 16416 | tf_op jit(solution)/shard_map/ppermute | solution.py:404
  41.2 3.7 %collective-permute-done.5 = f32[64,64]{1,0:T(8,128)S(1)} collective-permute-done((f32[64,64]{1,0:T(8,128)S(1)}, f32[64,64]{1,0:T(8,128)S(1)}, u32[]{:S(2)}, u32[]{:S(2)}) %collective-permute-start.5) | collective-permute-done | bytes 16416 | tf_op jit(solution)/shard_map/ppermute | solution.py:404
  46.8 3.6 %collective-permute-done.6 = f32[64,64]{1,0:T(8,128)S(1)} collective-permute-done((f32[64,64]{1,0:T(8,128)S(1)}, f32[64,64]{1,0:T(8,128)S(1)}, u32[]{:S(2)}, u32[]{:S(2)}) %collective-permute-start.6) | collective-permute-done | bytes 16416 | tf_op jit(solution)/shard_map/ppermute | solution.py:404
  51.2 4.6 %collective-permute-start.7 = (bf16[64,2048]{1,0:T(8,128)(2,1)S(1)}, bf16[64,2048]{1,0:T(8,128)(2,1)S(1)}, u32[]{:S(2)}, u32[]{:S(2)}) collective-permute-start(bf16[64,2048]{1,0:T(8,128)(2,1)S(1)} %get-tuple-element.40.refs_6_), channel_id=1, source_target_pairs={{2,4},{6,8},{10,12},{14,16},{18,20},{22,24},{26,28},{30,32},{34,36... | collective-permute-start | bytes 786440 | tf_op jit(solution)/shard_map/ppermute | solution.py:410
  56.3 4.9 %collective-permute-done.9 = f32[64,64]{1,0:T(8,128)S(1)} collective-permute-done((f32[64,64]{1,0:T(8,128)S(1)}, f32[64,64]{1,0:T(8,128)S(1)}, u32[]{:S(2)}, u32[]{:S(2)}) %collective-permute-start.9) | collective-permute-done | bytes 16416 | tf_op jit(solution)/shard_map/ppermute | solution.py:404
  63.7 15.3 %tail.2 = (bf16[64,8192]{1,0:T(8,128)(2,1)}, bf16[64,8192]{1,0:T(8,128)(2,1)S(1)}, bf16[64,4096]{1,0:T(8,128)(2,1)S(1)}, bf16[64,4096]{1,0:T(8,128)(2,1)S(1)}, b...) custom-call(s32[168]{0:T(256)S(1)} %get-tuple-element.32.refs_0_, s32[4,32]{1,0:T(4,128)S(1)} %bitcast.129, ...), custom_call_target="tpu_custom_call" | custom-call | flops 1000000000 | bytes 10000000 | tf_op jit(solution)/shard_map/tail/pallas_call | solution.py:388
  79.0 2.3 %shard_map.111.refs_18_ = f32[64,2048]{1,0:T(8,128)S(1)} custom-call(s32[5,32]{1,0:T(8,128)S(1)} %bitcast.125, bf16[64,8192]{1,0:T(8,128)(2,1)S(1)} %get-tuple-element.61.refs_1_, bf16[8,5,256,256]{3,2,1,0:T(8,128)(2,1)S(1)} %get-tuple-element.46.refs_2_.refs_14_), custom_call_target="tpu_custom_call" | custom-call | flops 350000000 | bytes 6000000 | tf_op jit(solution)/shard_map/pallas_call | solution.py:253
  81.3 2.3 %shard_map.110.refs_17_ = f32[64,2048]{1,0:T(8,128)S(1)} custom-call(s32[5,32]{1,0:T(8,128)S(1)} %bitcast.126, bf16[64,8192]{1,0:T(8,128)(2,1)S(1)} %get-tuple-element.61.refs_1_, bf16[8,5,256,256]{3,2,1,0:T(8,128)(2,1)S(1)} %get-tuple-element.45.refs_2_.refs_13_), custom_call_target="tpu_custom_call" | custom-call | flops 350000000 | bytes 6000000 | tf_op jit(solution)/shard_map/pallas_call | solution.py:253
  83.6 2.3 %shard_map.109.refs_16_ = f32[64,2048]{1,0:T(8,128)S(1)} custom-call(s32[5,32]{1,0:T(8,128)S(1)} %bitcast.127, bf16[64,8192]{1,0:T(8,128)(2,1)S(1)} %get-tuple-element.61.refs_1_, bf16[8,5,256,256]{3,2,1,0:T(8,128)(2,1)S(1)} %get-tuple-element.44.refs_2_.refs_12_), custom_call_target="tpu_custom_call" | custom-call | flops 350000000 | bytes 6000000 | tf_op jit(solution)/shard_map/pallas_call | solution.py:253
  86.0 2.3 %shard_map.108.refs_15_ = f32[64,2048]{1,0:T(8,128)S(1)} custom-call(s32[5,32]{1,0:T(8,128)S(1)} %bitcast.128, bf16[64,8192]{1,0:T(8,128)(2,1)S(1)} %get-tuple-element.61.refs_1_, bf16[8,5,256,256]{3,2,1,0:T(8,128)(2,1)S(1)} %get-tuple-element.43.refs_2_.refs_11_), custom_call_target="tpu_custom_call" | custom-call | flops 350000000 | bytes 6000000 | tf_op jit(solution)/shard_map/pallas_call | solution.py:253
  93.0 2.8 %collective-permute-done.12 = f32[64,64]{1,0:T(8,128)S(1)} collective-permute-done((f32[64,64]{1,0:T(8,128)S(1)}, f32[64,64]{1,0:T(8,128)S(1)}, u32[]{:S(2)}, u32[]{:S(2)}) %collective-permute-start.12) | collective-permute-done | bytes 16416 | tf_op jit(solution)/shard_map/ppermute | solution.py:404
  96.4 3.7 %collective-permute-done.13 = f32[64,64]{1,0:T(8,128)S(1)} collective-permute-done((f32[64,64]{1,0:T(8,128)S(1)}, f32[64,64]{1,0:T(8,128)S(1)}, u32[]{:S(2)}, u32[]{:S(2)}) %collective-permute-start.13) | collective-permute-done | bytes 16416 | tf_op jit(solution)/shard_map/ppermute | solution.py:404
  100.8 4.9 %collective-permute-done.14 = f32[64,64]{1,0:T(8,128)S(1)} collective-permute-done((f32[64,64]{1,0:T(8,128)S(1)}, f32[64,64]{1,0:T(8,128)S(1)}, u32[]{:S(2)}, u32[]{:S(2)}) %collective-permute-start.14) | collective-permute-done | bytes 16416 | tf_op jit(solution)/shard_map/ppermute | solution.py:404
  106.0 10.4 %collective-permute-start.18 = (f32[64,64]{1,0:T(8,128)S(1)}, f32[64,64]{1,0:T(8,128)S(1)}, u32[]{:S(2)}, u32[]{:S(2)}) collective-permute-start(f32[64,64]{1,0:T(8,128)S(1)} %convolution_add_fusion.1), channel_id=1, source_target_pairs={{0,32},{2,34},{4,36},{6,38},{8,40},{10,42},{12,44},{14,46},{16,48}... | collective-permute-start | bytes 49160 | tf_op jit(solution)/shard_map/ppermute | solution.py:404
  118.6 8.1 %collective-permute-start.15 = (bf16[64,4096]{1,0:T(8,128)(2,1)S(1)}, bf16[64,4096]{1,0:T(8,128)(2,1)S(1)}, u32[]{:S(2)}, u32[]{:S(2)}) collective-permute-start(bf16[64,4096]{1,0:T(8,128)(2,1)S(1)} %get-tuple-element.58), channel_id=1, source_target_pairs={{2,4},{6,8},{10,12},{14,16},{18,20},{22,24},{26,28},{30,32},{34,36... | collective-permute-start | bytes 1572872 | tf_op jit(solution)/shard_map/ppermute | solution.py:410
  127.2 4.9 %collective-permute-done.19 = f32[64,64]{1,0:T(8,128)S(1)} collective-permute-done((f32[64,64]{1,0:T(8,128)S(1)}, f32[64,64]{1,0:T(8,128)S(1)}, u32[]{:S(2)}, u32[]{:S(2)}) %collective-permute-start.19) | collective-permute-done | bytes 16416 | tf_op jit(solution)/shard_map/ppermute | solution.py:404
  134.7 12.6 %tail.3 = bf16[64,8192]{1,0:T(8,128)(2,1)} custom-call(s32[168]{0:T(256)S(1)} %get-tuple-element.32.refs_0_, s32[4,32]{1,0:T(4,128)S(1)} %bitcast.130, bf16[64,4096]{1,0:T(8,128)(2,1)S(1)} %collective-permute-done.11.refs_2_, bf16[64,4096]{1,0:T(8,128)(2,1)S(1)} %collective-permute-done.15.refs_3_, bf16[64,2048]{1,0:T(8,128)(2,1)S(1)} %collective-permute-done.16.refs_4_, ...), custom_call_target="tpu_custom_call" | custom-call | flops 1000000000 | bytes 10000000 | tf_op jit(solution)/shard_map/tail/pallas_call | solution.py:388
  (75 shorter events, 23.7 us)
Async XLA Ops:
  1.9 61.8 %collective-permute-start = (bf16[64,4096]{1,0:T(8,128)(2,1)S(1)}, bf16[64,4096]{1,0:T(8,128)(2,1)S(1)}, u32[]{:S(2)}, u32[]{:S(2)}) collective-permute-start(bf16[64,4096]{1,0:T(8,128)(2,1)S(1)} %get-tuple-element.33.va), channel_id=1, source_target_pairs={{0,2},{2,0},{4,6},{6,4},{8,10},{10,8},{12,14},{14,12},{16,18},{18,... | collective-permute-start | bytes 1572872 | tf_op jit(solution)/shard_map/ppermute | solution.py:404
  3.4 60.3 %collective-permute-start.1 = (bf16[64,4096]{1,0:T(8,128)(2,1)S(1)}, bf16[64,4096]{1,0:T(8,128)(2,1)S(1)}, u32[]{:S(2)}, u32[]{:S(2)}) collective-permute-start(bf16[64,4096]{1,0:T(8,128)(2,1)S(1)} %get-tuple-element.34.vb), channel_id=1, source_target_pairs={{2,4},{6,8},{10,12},{14,16},{18,20},{22,24},{26,28},{30,32},{34,36... | collective-permute-start | bytes 1572872 | tf_op jit(solution)/shard_map/ppermute | solution.py:410
  13.1 22.1 %collective-permute-start.2 = (f32[64,64]{1,0:T(8,128)S(1)}, f32[64,64]{1,0:T(8,128)S(1)}, u32[]{:S(2)}, u32[]{:S(2)}) collective-permute-start(f32[64,64]{1,0:T(8,128)S(1)} %get-tuple-element.36), channel_id=1, source_target_pairs={{0,2},{2,0},{4,6},{6,4},{8,10},{10,8},{12,14},{14,12},{16,18},{18,... | collective-permute-start | bytes 49160 | tf_op jit(solution)/shard_map/ppermute | solution.py:404
  32.9 30.8 %copy-start.1 = (bf16[32,64,256]{2,1,0:T(8,128)(2,1)S(1)}, bf16[32,64,256]{2,1,0:T(8,128)(2,1)}, u32[]{:S(2)}) copy-start(bf16[32,64,256]{2,1,0:T(8,128)(2,1)} %refs_8_.3) | copy-start | bytes 3145732
  32.9 30.8 %copy-start.2 = (bf16[32,4,64,64]{3,2,1,0:T(8,128)(2,1)S(1)}, bf16[32,4,64,64]{3,2,1,0:T(8,128)(2,1)}, u32[]{:S(2)}) copy-start(bf16[32,4,64,64]{3,2,1,0:T(8,128)(2,1)} %refs_10_.3) | copy-start | bytes 3145732
  32.9 30.8 %copy-start.3 = (bf16[32,64,64]{2,1,0:T(8,128)(2,1)S(1)}, bf16[32,64,64]{2,1,0:T(8,128)(2,1)}, u32[]{:S(2)}) copy-start(bf16[32,64,64]{2,1,0:T(8,128)(2,1)} %param.13) | copy-start | bytes 786436
  32.9 30.8 %copy-start.6 = (s32[32,4]{0,1:T(4,128)S(1)}, s32[32,4]{0,1:T(4,128)}, u32[]{:S(2)}) copy-start(s32[32,4]{0,1:T(4,128)} %param.14) | copy-start | bytes 1540
  35.4 5.2 %collective-permute-start.4 = (f32[64,64]{1,0:T(8,128)S(1)}, f32[64,64]{1,0:T(8,128)S(1)}, u32[]{:S(2)}, u32[]{:S(2)}) collective-permute-start(f32[64,64]{1,0:T(8,128)S(1)} %convolution_add_fusion.11), channel_id=1, source_target_pairs={{0,6},{2,4},{4,2},{6,0},{8,14},{10,12},{12,10},{14,8},{16,22},{18,... | collective-permute-start | bytes 49160 | tf_op jit(solution)/shard_map/ppermute | solution.py:404
  35.7 26.0 %collective-permute-start.3 = (bf16[64,2048]{1,0:T(8,128)(2,1)S(1)}, bf16[64,2048]{1,0:T(8,128)(2,1)S(1)}, u32[]{:S(2)}, u32[]{:S(2)}) collective-permute-start(bf16[64,2048]{1,0:T(8,128)(2,1)S(1)} %get-tuple-element.40.refs_6_), channel_id=1, source_target_pairs={{0,2},{2,0},{4,6},{6,4},{8,10},{10,8},{12,14},{14,12},{16,18},{18,... | collective-permute-start | bytes 786440 | tf_op jit(solution)/shard_map/ppermute | solution.py:404
  40.9 4.0 %collective-permute-start.5 = (f32[64,64]{1,0:T(8,128)S(1)}, f32[64,64]{1,0:T(8,128)S(1)}, u32[]{:S(2)}, u32[]{:S(2)}) collective-permute-start(f32[64,64]{1,0:T(8,128)S(1)} %convolution_add_fusion.10), channel_id=1, source_target_pairs={{0,8},{2,10},{4,12},{6,14},{8,0},{10,2},{12,4},{14,6},{16,24},{18,... | collective-permute-start | bytes 49160 | tf_op jit(solution)/shard_map/ppermute | solution.py:404
  45.3 5.2 %collective-permute-start.6 = (f32[64,64]{1,0:T(8,128)S(1)}, f32[64,64]{1,0:T(8,128)S(1)}, u32[]{:S(2)}, u32[]{:S(2)}) collective-permute-start(f32[64,64]{1,0:T(8,128)S(1)} %convolution_add_fusion.9), channel_id=1, source_target_pairs={{0,24},{2,26},{4,28},{6,30},{8,16},{10,18},{12,20},{14,22},{16,8},... | collective-permute-start | bytes 49160 | tf_op jit(solution)/shard_map/ppermute | solution.py:404
  50.8 5.0 %collective-permute-start.8 = (f32[64,64]{1,0:T(8,128)S(1)}, f32[64,64]{1,0:T(8,128)S(1)}, u32[]{:S(2)}, u32[]{:S(2)}) collective-permute-start(f32[64,64]{1,0:T(8,128)S(1)} %convolution_add_fusion.7), channel_id=1, source_target_pairs={{0,32},{2,34},{4,36},{6,38},{8,40},{10,42},{12,44},{14,46},{16,48}... | collective-permute-start | bytes 49160 | tf_op jit(solution)/shard_map/ppermute | solution.py:404
  51.2 12.5 %collective-permute-start.7 = (bf16[64,2048]{1,0:T(8,128)(2,1)S(1)}, bf16[64,2048]{1,0:T(8,128)(2,1)S(1)}, u32[]{:S(2)}, u32[]{:S(2)}) collective-permute-start(bf16[64,2048]{1,0:T(8,128)(2,1)S(1)} %get-tuple-element.40.refs_6_), channel_id=1, source_target_pairs={{2,4},{6,8},{10,12},{14,16},{18,20},{22,24},{26,28},{30,32},{34,36... | collective-permute-start | bytes 786440 | tf_op jit(solution)/shard_map/ppermute | solution.py:410
  56.0 5.2 %collective-permute-start.9 = (f32[64,64]{1,0:T(8,128)S(1)}, f32[64,64]{1,0:T(8,128)S(1)}, u32[]{:S(2)}, u32[]{:S(2)}) collective-permute-start(f32[64,64]{1,0:T(8,128)S(1)} %convolution_add_fusion.6), channel_id=1, source_target_pairs={{0,96},{2,98},{4,100},{6,102},{8,104},{10,106},{12,108},{14,110},{... | collective-permute-start | bytes 49160 | tf_op jit(solution)/shard_map/ppermute | solution.py:404
  85.9 4.3 %collective-permute-start.10 = (f32[64,64]{1,0:T(8,128)S(1)}, f32[64,64]{1,0:T(8,128)S(1)}, u32[]{:S(2)}, u32[]{:S(2)}) collective-permute-start(f32[64,64]{1,0:T(8,128)S(1)} %get-tuple-element.53), channel_id=1, source_target_pairs={{0,2},{2,0},{4,6},{6,4},{8,10},{10,8},{12,14},{14,12},{16,18},{18,... | collective-permute-start | bytes 49160 | tf_op jit(solution)/shard_map/ppermute | solution.py:404
  90.6 5.2 %collective-permute-start.12 = (f32[64,64]{1,0:T(8,128)S(1)}, f32[64,64]{1,0:T(8,128)S(1)}, u32[]{:S(2)}, u32[]{:S(2)}) collective-permute-start(f32[64,64]{1,0:T(8,128)S(1)} %convolution_add_fusion.5), channel_id=1, source_target_pairs={{0,6},{2,4},{4,2},{6,0},{8,14},{10,12},{12,10},{14,8},{16,22},{18,... | collective-permute-start | bytes 49160 | tf_op jit(solution)/shard_map/ppermute | solution.py:404
  90.9 41.6 %collective-permute-start.16 = (bf16[64,2048]{1,0:T(8,128)(2,1)S(1)}, bf16[64,2048]{1,0:T(8,128)(2,1)S(1)}, u32[]{:S(2)}, u32[]{:S(2)}) collective-permute-start(bf16[64,2048]{1,0:T(8,128)(2,1)S(1)} %get-tuple-element.59.refs_6_), channel_id=1, source_target_pairs={{0,2},{2,0},{4,6},{6,4},{8,10},{10,8},{12,14},{14,12},{16,18},{18,... | collective-permute-start | bytes 786440 | tf_op jit(solution)/shard_map/ppermute | solution.py:404
  91.0 41.5 %collective-permute-start.11 = (bf16[64,4096]{1,0:T(8,128)(2,1)S(1)}, bf16[64,4096]{1,0:T(8,128)(2,1)S(1)}, u32[]{:S(2)}, u32[]{:S(2)}) collective-permute-start(bf16[64,4096]{1,0:T(8,128)(2,1)S(1)} %get-tuple-element.54), channel_id=1, source_target_pairs={{0,2},{2,0},{4,6},{6,4},{8,10},{10,8},{12,14},{14,12},{16,18},{18,... | collective-permute-start | bytes 1572872 | tf_op jit(solution)/shard_map/ppermute | solution.py:404
  96.2 4.0 %collective-permute-start.13 = (f32[64,64]{1,0:T(8,128)S(1)}, f32[64,64]{1,0:T(8,128)S(1)}, u32[]{:S(2)}, u32[]{:S(2)}) collective-permute-start(f32[64,64]{1,0:T(8,128)S(1)} %convolution_add_fusion.4), channel_id=1, source_target_pairs={{0,8},{2,10},{4,12},{6,14},{8,0},{10,2},{12,4},{14,6},{16,24},{18,... | collective-permute-start | bytes 49160 | tf_op jit(solution)/shard_map/ppermute | solution.py:404
  100.5 5.2 %collective-permute-start.14 = (f32[64,64]{1,0:T(8,128)S(1)}, f32[64,64]{1,0:T(8,128)S(1)}, u32[]{:S(2)}, u32[]{:S(2)}) collective-permute-start(f32[64,64]{1,0:T(8,128)S(1)} %convolution_add_fusion.3), channel_id=1, source_target_pairs={{0,24},{2,26},{4,28},{6,30},{8,16},{10,18},{12,20},{14,22},{16,8},... | collective-permute-start | bytes 49160 | tf_op jit(solution)/shard_map/ppermute | solution.py:404
  106.0 20.7 %collective-permute-start.18 = (f32[64,64]{1,0:T(8,128)S(1)}, f32[64,64]{1,0:T(8,128)S(1)}, u32[]{:S(2)}, u32[]{:S(2)}) collective-permute-start(f32[64,64]{1,0:T(8,128)S(1)} %convolution_add_fusion.1), channel_id=1, source_target_pairs={{0,32},{2,34},{4,36},{6,38},{8,40},{10,42},{12,44},{14,46},{16,48}... | collective-permute-start | bytes 49160 | tf_op jit(solution)/shard_map/ppermute | solution.py:404
  116.6 15.9 %collective-permute-start.17 = (bf16[64,2048]{1,0:T(8,128)(2,1)S(1)}, bf16[64,2048]{1,0:T(8,128)(2,1)S(1)}, u32[]{:S(2)}, u32[]{:S(2)}) collective-permute-start(bf16[64,2048]{1,0:T(8,128)(2,1)S(1)} %get-tuple-element.59.refs_6_), channel_id=1, source_target_pairs={{2,4},{6,8},{10,12},{14,16},{18,20},{22,24},{26,28},{30,32},{34,36... | collective-permute-start | bytes 786440 | tf_op jit(solution)/shard_map/ppermute | solution.py:410
  118.6 16.2 %collective-permute-start.15 = (bf16[64,4096]{1,0:T(8,128)(2,1)S(1)}, bf16[64,4096]{1,0:T(8,128)(2,1)S(1)}, u32[]{:S(2)}, u32[]{:S(2)}) collective-permute-start(bf16[64,4096]{1,0:T(8,128)(2,1)S(1)} %get-tuple-element.58), channel_id=1, source_target_pairs={{2,4},{6,8},{10,12},{14,16},{18,20},{22,24},{26,28},{30,32},{34,36... | collective-permute-start | bytes 1572872 | tf_op jit(solution)/shard_map/ppermute | solution.py:410
  126.9 5.2 %collective-permute-start.19 = (f32[64,64]{1,0:T(8,128)S(1)}, f32[64,64]{1,0:T(8,128)S(1)}, u32[]{:S(2)}, u32[]{:S(2)}) collective-permute-start(f32[64,64]{1,0:T(8,128)S(1)} %convolution_add_fusion), channel_id=1, source_target_pairs={{0,96},{2,98},{4,100},{6,102},{8,104},{10,106},{12,108},{14,110},{... | collective-permute-start | bytes 49160 | tf_op jit(solution)/shard_map/ppermute | solution.py:404
  (3 other events, 11.1 us)

commit v4 on v3

--- a/solution.py
+++ b/solution.py
@@ -9,8 +9,8 @@
 REACH = 16
 FARR = 32
 PIECES = 4
-TOGETHER = 4
-STRIDE = 40
+TOGETHER = 8
+COUNT = 144
 BF = jnp.bfloat16
 F32 = jnp.float32
 NT = (((1,), (1,)), ((), ()))
@@ -35,6 +35,18 @@
 
 def cost(flops, moved):
     return pl.CostEstimate(flops=flops, bytes_accessed=moved, transcendentals=0)
+
+
+def paired_coef(v, even_basis, odd_basis):
+    zero = jnp.zeros_like(even_basis)
+    blocks = jnp.concatenate(
+        [
+            jnp.concatenate([even_basis, zero], axis=1),
+            jnp.concatenate([zero, odd_basis], axis=1),
+        ],
+        axis=0,
+    )
+    return mm(v, blocks, NT).astype(BF)
 
 
 def is_even():
@@ -86,11 +98,9 @@
     total = None
     for v, first in ((va, first_a), (vb, leaves // 2 - first_a)):
         for pair in range(leaves // 4):
-            parts = [
-                mm(v[:, leaf * points : (leaf + 1) * points], basis[first + leaf], NT)
-                for leaf in (2 * pair, 2 * pair + 1)
-            ]
-            both = jnp.concatenate(parts, axis=1).astype(BF)
+            leaf = first + 2 * pair
+            rows = v[:, 2 * pair * points : 2 * (pair + 1) * points]
+            both = paired_coef(rows, basis[leaf], basis[leaf + 1])
             at = columns_of((first // 2 + pair) * 2 * rank, 2 * rank)
             coef[:, at] = both
             term = mm(both, trans[at, :])
@@ -121,37 +131,40 @@
     )(va, vb, *hbm)
 
 
-def table_body(levels, near_list, trans_hbm, couple_hbm, near, up, down, plan, kept, *scratch):
-    trans, couple, own, pair, sems = scratch
+def load_piece(near, kept, piece, sems):
+    some = kept.shape[0] // PIECES
+    return [
+        pltpu.make_async_copy(near.at[piece * some + i], kept.at[piece * some + i], sems.at[i])
+        for i in range(some)
+    ]
+
+
+def table_body(levels, near_list, trans_hbm, couple_hbm, near, up, pair, plan, kept, *scratch):
+    trans, couple, sems = scratch
     copies = [
-        pltpu.make_async_copy(trans_hbm, trans, sems.at[0]),
-        pltpu.make_async_copy(couple_hbm, couple, sems.at[1]),
-        pltpu.make_async_copy(near.at[pl.ds(0, kept.shape[0])], kept, sems.at[2]),
+        pltpu.make_async_copy(trans_hbm, trans, sems.at[8]),
+        pltpu.make_async_copy(couple_hbm, couple, sems.at[9]),
     ]
+    copies += load_piece(near, kept, 0, sems)
     for copy in copies:
         copy.start()
     device = lax.axis_index("leaf")
     kn, leaves = near_list.shape
-    some = leaves // PIECES
     first = device * leaves
 
-    for piece in range(PIECES):
-
-        def scan(i, n, piece=piece):
-            leaf = piece * some + i
-            for s in range(kn):
-                source = near_list[s, leaf] - first
-                left = source < 0
-                place = source + jnp.where(left, REACH, REACH - leaves)
-                plan[piece * STRIDE + n] = (leaf * 8 + s) * 32 + place
-                n = n + jnp.where(left | (source >= leaves), 1, 0)
-            return n
-
-        count = lax.fori_loop(0, some, scan, 0)
-        for i in range(TOGETHER):
-            plan[piece * STRIDE + count + i] = (leaves * 8) * 32
-        plan[PIECES * STRIDE + piece] = lax.div(count + TOGETHER - 1, TOGETHER)
-
+    def scan(leaf, n):
+        for slot in range(kn):
+            source = near_list[slot, leaf] - first
+            left = source < 0
+            place = source + jnp.where(left, REACH, REACH - leaves)
+            plan[n] = (leaf * 8 + slot) * 32 + place
+            n = n + jnp.where(left | (source >= leaves), 1, 0)
+        return n
+
+    total = lax.fori_loop(0, leaves, scan, 0)
+    for i in range(TOGETHER):
+        plan[total + i] = (leaves * 8) * 32
+    plan[COUNT] = lax.div(total + TOGETHER - 1, TOGETHER)
     count, rows, nodes = 8, trans.shape[0], trans.shape[2]
     row = lax.broadcasted_iota(jnp.int32, (count, nodes), 0)
     node = lax.broadcasted_iota(jnp.int32, (count, nodes), 1)
@@ -165,18 +178,34 @@
     copies[0].wait()
     copies[1].wait()
     for k in range(rows):
-        own[:, k, :] = mm(both, trans[k], NT)
-        pair[:, k, :] = mm(pick_here, couple[k], NT)
-    for t in range(levels):
-        up[t, 0] = own[t]
-        up[t, 1] = own[count + t]
+        picked = mm(both, trans[k], NT)
+        up[0, :, k, :] = picked[:levels]
+        up[1, :, k, :] = picked[count : count + levels]
+        pair[:, k, :] = mm(pick_here, couple[k], NT)[:levels]
+    for copy in copies[2:]:
+        copy.wait()
+
+
+def chain_body(up, pair, down):
+    levels = pair.shape[0]
     down[0] = pair[0]
-    path = own[0]
+    path = up[0, 0]
     for t in range(1, levels):
         down[t] = exact(path, pair[t])
         if t + 1 < levels:
-            path = exact(path, own[t])
-    copies[2].wait()
+            path = exact(path, up[0, t])
+
+
+def chain(up, pair):
+    return pl.pallas_call(
+        chain_body,
+        in_specs=[VMEM] * 2,
+        out_specs=VMEM,
+        out_shape=jax.ShapeDtypeStruct(pair.shape, F32),
+        compiler_params=params(4),
+        cost_estimate=cost(10_000_000, 1_000_000),
+        name="chain",
+    )(up, pair)
 
 
 def table(top_transfer, top_couple, near_list_t, near_blocks):
@@ -197,16 +226,14 @@
             scratch_shapes=[
                 pltpu.VMEM((rank, rank, nodes), BF),
                 pltpu.VMEM((rank, rank, nodes), BF),
-                pltpu.VMEM((16, rank, rank), F32),
-                pltpu.VMEM((8, rank, rank), F32),
-                pltpu.SemaphoreType.DMA((3,)),
+                pltpu.SemaphoreType.DMA((shape[0] // PIECES + 2,)),
             ],
         ),
         out_shape=[
-            jax.ShapeDtypeStruct((levels, 2, rank, rank), F32),
+            jax.ShapeDtypeStruct((2, levels, rank, rank), F32),
             jax.ShapeDtypeStruct((levels, rank, rank), F32),
-            jax.ShapeDtypeStruct((PIECES * STRIDE + 8,), jnp.int32),
-            jax.ShapeDtypeStruct((shape[0] // PIECES, *shape[1:]), BF),
+            jax.ShapeDtypeStruct((COUNT + 8,), jnp.int32),
+            jax.ShapeDtypeStruct(shape, BF),
         ],
         compiler_params=params(6),
         cost_estimate=cost(10_000_000, 8_000_000),
@@ -215,32 +242,35 @@
 
 
 def near_body(piece, load, near_list, v, kept, *refs):
+    copies = []
     if load:
-        near, total, later, sem = refs
-        here = pl.ds((piece + 1) * later.shape[0], later.shape[0])
-        copy = pltpu.make_async_copy(near.at[here], later, sem)
-        copy.start()
+        near, total, kept, sems = refs
+        copies = load_piece(near, kept, piece + 1, sems)
+        for copy in copies:
+            copy.start()
     else:
         (total,) = refs
-    some, kn, points, _ = kept.shape
-    leaves = v.shape[1] // points
+    leaves, kn, points, _ = kept.shape
+    some = leaves // PIECES
     first = lax.axis_index("leaf") * leaves
     for i in range(some):
         out = None
+        leaf = piece * some + i
         for s in range(kn):
-            source = near_list[s, piece * some + i] - first
+            source = near_list[s, leaf] - first
             inside = (source >= 0) & (source < leaves)
             rows = v[:, columns_of(jnp.clip(source, 0, leaves - 1) * points, points)]
-            term = mm(jnp.where(inside, rows, jnp.zeros_like(rows)), kept[i, s], NT)
+            term = mm(jnp.where(inside, rows, jnp.zeros_like(rows)), kept[leaf, s], NT)
             out = term if out is None else out + term
         total[:, i * points : (i + 1) * points] = out
-    if load:
+    for copy in copies:
         copy.wait()
 
 
 def near_piece(piece, near_list_t, v, near_blocks, kept, load):
     columns = v.shape[0]
-    some, _, points, _ = kept.shape
+    leaves, _, points, _ = kept.shape
+    some = leaves // PIECES
     in_specs = [VMEM, VMEM]
     args = [v, kept]
     out_shape = [jax.ShapeDtypeStruct((columns, some * points), F32)]
@@ -249,7 +279,7 @@
         in_specs.append(HBM)
         args.append(pltpu.with_memory_space_constraint(near_blocks, pltpu.HBM))
         out_shape.append(jax.ShapeDtypeStruct(kept.shape, BF))
-        scratch.append(pltpu.SemaphoreType.DMA)
+        scratch.append(pltpu.SemaphoreType.DMA((some,)))
     return pl.pallas_call(
         lambda *refs: near_body(piece, load, *refs),
         grid_spec=pltpu.PrefetchScalarGridSpec(
@@ -259,6 +289,7 @@
             scratch_shapes=scratch,
         ),
         out_shape=out_shape,
+        input_output_aliases={2: 1} if load else {},
         compiler_params=params(4),
         cost_estimate=cost(350_000_000, 6_000_000),
     )(near_list_t, *args)
@@ -267,7 +298,7 @@
 def tail_body(more, plan, couple_list, *refs):
     got_va, got_vb, got_ca, got_cb, sent_c, top, basis, trans, couple = refs[:9]
     refs = refs[9:]
-    kept, partial, refs = refs[:PIECES], refs[PIECES : 2 * PIECES], refs[2 * PIECES :]
+    near, partial, refs = refs[0], refs[1 : 1 + PIECES], refs[1 + PIECES :]
     if more:
         image, own_v, va, vb, coef, node, table_ref, wide, acc, total_ref, sems = refs
     else:
@@ -284,14 +315,16 @@
     ]
     for copy in copies:
         copy.start()
+    row = lax.broadcasted_iota(jnp.int32, (2 * rank, 2 * rank), 0)
+    lane = lax.broadcasted_iota(jnp.int32, (2 * rank, 2 * rank), 1)
+    swap = jnp.where(jnp.bitwise_xor(row, rank) == lane, 1.0, 0.0).astype(BF)
     base_a = jnp.where(even, 2 * leaves, 0)
     for ref, base in ((got_ca, base_a), (sent_c, leaves), (got_cb, 2 * leaves - base_a)):
         for pair in range(leaves // 2):
             both = ref[:, 2 * rank * pair : 2 * rank * (pair + 1)]
-            table_ref[base + 2 * pair] = both[:, :rank]
-            table_ref[base + 2 * pair + 1] = both[:, rank:]
-    high = top[...].astype(BF)
-    low = (top[...] - high.astype(F32)).astype(BF)
+            table_ref[base + 2 * pair] = both
+            table_ref[base + 2 * pair + 1] = mm(both, swap).astype(BF)
+    descent = top[...].astype(BF)
     if more:
         total_ref[...] = jnp.zeros_like(total_ref)
     for piece in range(PIECES):
@@ -299,31 +332,31 @@
         acc[:, piece * width : (piece + 1) * width] = partial[piece][...]
     for copy in copies:
         copy.wait()
+
+    def add(j, carry):
+        terms = []
+        for i in range(TOGETHER):
+            code = plan[j * TOGETHER + i]
+            leaf = lax.shift_right_logical(code, 8)
+            slot = lax.shift_right_logical(code, 5) & 7
+            rows = wide[:, columns_of((code & 31) * points, points)]
+            term = mm(rows, near[leaf & (leaves - 1), slot], NT)
+            terms.append((columns_of(leaf * points, points), term))
+        for here, term in terms:
+            acc[:, here] += term
+        return carry
+
+    lax.fori_loop(0, plan[COUNT], add, 0)
     writes = []
     for piece in range(PIECES):
-        near = kept[piece]
-
-        def add(j, carry, near=near, piece=piece):
-            terms = []
-            for i in range(TOGETHER):
-                code = plan[piece * STRIDE + j * TOGETHER + i]
-                block = lax.shift_right_logical(code, 5)
-                leaf = lax.shift_right_logical(code, 8)
-                rows = wide[:, columns_of((code & 31) * points, points)]
-                term = mm(rows, near[leaf & (some - 1), block & 7], NT)
-                terms.append((columns_of(leaf * points, points), term))
-            for here, term in terms:
-                acc[:, here] += term
-            return carry
-
-        lax.fori_loop(0, plan[PIECES * STRIDE + piece], add, 0)
         results = []
         for i in range(some):
             leaf = piece * some + i
             moved = trans[leaf * rank : (leaf + 1) * rank, :]
-            local = mm(high, moved, NT) + mm(low, moved, NT)
+            local = mm(descent, moved, NT)
             for s in range(couple.shape[1]):
-                local += mm(table_ref[couple_list[s, leaf] - first + FARR], couple[leaf, s], NT)
+                source = couple_list[s, leaf] - first + FARR
+                local += mm(table_ref[source, :, :rank], couple[leaf, s], NT)
             here = slice(leaf * points, (leaf + 1) * points)
             value = (acc[:, here] + mm(local.astype(BF), basis[leaf])).astype(BF)
             results.append(value)
@@ -335,8 +368,8 @@
             continue
         for pair in range(some // 2):
             leaf = piece * some + 2 * pair
-            parts = [mm(results[2 * pair + i], basis[leaf + i], NT) for i in range(2)]
-            both = jnp.concatenate(parts, axis=1).astype(BF)
+            rows = jnp.concatenate(results[2 * pair : 2 * pair + 2], axis=1)
+            both = paired_coef(rows, basis[leaf], basis[leaf + 1])
             coef[:, leaf * rank : (leaf + 2) * rank] = both
             total_ref[...] += mm(both, trans[leaf * rank : (leaf + 2) * rank, :])
         in_right = piece >= PIECES // 2
@@ -367,7 +400,7 @@
     image = jax.ShapeDtypeStruct((columns, own), BF)
     out_shape, out_specs = [image], [HBM]
     scratch = [
-        pltpu.VMEM((3 * leaves, columns, rank), BF),
+        pltpu.VMEM((3 * leaves, columns, 2 * rank), BF),
         pltpu.VMEM((columns, own), BF),
         pltpu.VMEM((columns, own + points), F32),
     ]
@@ -389,7 +422,7 @@
         lambda *refs: tail_body(more, *refs),
         grid_spec=pltpu.PrefetchScalarGridSpec(
             num_scalar_prefetch=2,
-            in_specs=[VMEM] * (9 + 2 * PIECES),
+            in_specs=[VMEM] * (10 + PIECES),
             out_specs=out_specs,
             scratch_shapes=scratch,
         ),
@@ -397,7 +430,7 @@
         compiler_params=params(12),
         cost_estimate=cost(1_000_000_000, 10_000_000),
         name="tail",
-    )(*lists, *got, sent_c, top, basis_t, trans2, leaf_couple, *kept, *partial)
+    )(*lists, *got, sent_c, top, basis_t, trans2, leaf_couple, kept, *partial)
 
 
 def swapped(value, mask):
@@ -414,11 +447,12 @@
     levels = lax.axis_size("leaf").bit_length() - 1
     top = jnp.zeros_like(node)
     got_ca = got_cb = None
+    others = []
     for t in range(levels):
         mask = (1 << t) if t % 2 == 0 else 3 << (t - 1)
         other = swapped(node, mask)
         fill(t)
-        up, down = tables()
+        up, down = tables(t)
         if t == 0:
             va, coef, other = lax.optimization_barrier((va, coef, other))
             if got_va is None:
@@ -430,7 +464,9 @@
                 got_vb = swapped_odd(vb)
             got_cb = swapped_odd(later)
         if t + 1 < levels:
-            node = exact(node, up[t, 0]) + exact(other, up[t, 1])
+            node = exact(node, up[0, t]) + exact(other, up[1, t])
+        others.append(other)
+    for t, other in enumerate(others):
         top += exact(other, down[t], NT)
     return top, (got_va, got_vb, got_ca, got_cb)
 
@@ -450,24 +486,24 @@
     trans2 = leaf_transfer.reshape(leaves * rank, rank)
     near_list_t, couple_list_t = near_list.T, couple_list.T
     made = {}
-    kept, partial = [], []
+    partial = []
 
     def fill_first(t):
         if t == 0:
-            made["up"], made["down"], made["plan"], block = table(
+            made["up"], made["pair"], made["plan"], made["kept"] = table(
                 top_transfer, top_couple, near_list_t, near_blocks
             )
-            kept.append(block)
         elif t <= PIECES:
-            piece = t - 1
-            out = near_piece(
-                piece, near_list_t, rhs_block, near_blocks, kept[piece], piece + 1 < PIECES
-            )
+            load = t < PIECES
+            out = near_piece(t - 1, near_list_t, rhs_block, near_blocks, made["kept"], load)
             partial.append(out[0])
-            kept.extend(out[1:])
-
-    def tables():
-        return made["up"], made["down"]
+            if load:
+                made["kept"] = out[1]
+
+    def tables(t):
+        if t == 4 and "down" not in made:
+            made["down"] = chain(made["up"], made["pair"])
+        return made["up"], made.get("down")
 
     va, vb = split(rhs_block)
     got_va = swapped(va, 1)
@@ -476,18 +512,19 @@
     top, got = one_product(node, va, vb, coef, got_va, got_vb, fill_first, tables)
     lists = (made["plan"], couple_list_t)
     first_image, own_v, va, vb, coef_next, node = tail(
-        True, lists, got, coef, top, kept, partial, basis_t, trans2, leaf_couple
+        True, lists, got, coef, top, made["kept"], partial, basis_t, trans2, leaf_couple
     )
     again = []
 
     def fill_second(t):
-        if t < PIECES:
-            (out,) = near_piece(t, near_list_t, own_v, near_blocks, kept[t], False)
-            again.append(out)
+        if t == 4:
+            for piece in range(PIECES):
+                (out,) = near_piece(piece, near_list_t, own_v, near_blocks, made["kept"], False)
+                again.append(out)
 
     top, got = one_product(node, va, vb, coef_next, None, None, fill_second, tables)
     (second_image,) = tail(
-        False, lists, got, coef_next, top, kept, again, basis_t, trans2, leaf_couple
+        False, lists, got, coef_next, top, made["kept"], again, basis_t, trans2, leaf_couple
     )
     return (first_image, second_image)
 

time: 149 us -> 139 us (0.933)
  Pallas kernels: 62.8 us -> 54.7 us
    pallas_call x8, Pallas kernels: 25.2 us -> 20.9 us  [near_piece(): pl.pallas_call(lambda *refs: near_body(piece, load, *refs), grid_spec=plt...]
    pallas_call x2, Pallas kernels: 27.9 us -> 24.4 us  [tail(): pl.pallas_call(lambda *refs: tail_body(more, *refs), grid_spec=pltpu.Pref...]
  transfers between devices with their start and end apart: 20 -> 20, of which waited for: 11 -> 11; matrix products, arithmetic and copies ran while one was open for 3% -> 4% of each run, Pallas kernels for 18% -> 16%
where the time goes in v4:
time: 139 us
  Pallas kernels  54.7 us (39%)
  starting transfers between devices  39.3 us (28%)
  waiting for transfers between devices  37.1 us (27%)
  matrix products  5.45 us (4%)
    ppermute x16, waiting for transfers between devices, swapped(): lax.ppermute(value, 'leaf', [(i, i ^ mask) for i in range(lax.axis_size('...  32.8 us
    pallas_call x2, Pallas kernels, tail(): pl.pallas_call(lambda *refs: tail_body(more, *refs), grid_spec=pltpu.Pref...  24.4 us
    ppermute x4, starting transfers between devices, swapped_odd(): return lax.ppermute(value, 'leaf', pairs + [(j, i) for i, j in pairs])  21 us
    pallas_call x8, Pallas kernels, near_piece(): pl.pallas_call(lambda *refs: near_body(piece, load, *refs), grid_spec=plt...  20.9 us
    ppermute x16, starting transfers between devices, swapped(): lax.ppermute(value, 'leaf', [(i, i ^ mask) for i in range(lax.axis_size('...  18.3 us
    dot_general x32, matrix products, exact(): lax.dot_general(a, b, dims, precision=lax.Precision.HIGHEST, preferred_el...  5.45 us
    pallas_call x1, Pallas kernels, table(): pl.pallas_call(lambda *refs: table_body(levels, *refs), grid_spec=pltpu.P...  4.36 us
    ppermute x4, waiting for transfers between devices, swapped_odd(): return lax.ppermute(value, 'leaf', pairs + [(j, i) for i, j in pairs])  4.31 us
  transfers between devices with their start and end apart: 20, of which 11 were waited for; matrix products, arithmetic and copies ran while one was open for 4% of the time, Pallas kernels for 16%

profile of v4, /device:TPU:96, one launch (start us, length us, event | category | flops | bytes accessed | tf_op | source)
XLA Modules:
  0.0 138.6 jit_solution(18037748595094984207)
XLA Ops:
  3.5 6.3 %collective-permute-start.1 = (bf16[64,4096]{1,0:T(8,128)(2,1)S(1)}, bf16[64,4096]{1,0:T(8,128)(2,1)S(1)}, u32[]{:S(2)}, u32[]{:S(2)}) collective-permute-start(bf16[64,4096]{1,0:T(8,128)(2,1)S(1)} %get-tuple-element.34.vb), channel_id=1, source_target_pairs={{2,4},{6,8},{10,12},{14,16},{18,20},{22,24},{26,28},{30,32},{34,36... | collective-permute-start | bytes 1572872 | tf_op jit(solution)/shard_map/ppermute | solution.py:443
  9.8 2.8 %head.1 = (bf16[64,2048]{1,0:T(8,128)(2,1)S(1)}, f32[64,64]{1,0:T(8,128)S(1)}) custom-call(bf16[64,4096]{1,0:T(8,128)(2,1)S(1)} %get-tuple-element.33.va, bf16[64,4096]{1,0:T(8,128)(2,1)S(1)} %get-tuple-element.34.vb, bf16[32,64,256]{2,1,0:T(8,128)(2,1)} %refs_8_.3, bf16[2048,64]{1,0:T(8,128)(2,1)} %bitcast.111), custom_call_target="tpu_custom_call" | custom-call | flops 200000000 | bytes 6000000 | tf_op jit(solution)/shard_map/head/pallas_call | solution.py:115
  13.4 4.4 %table.1 = (f32[2,6,64,64]{3,2,1,0:T(8,128)S(1)}, f32[6,64,64]{2,1,0:T(8,128)S(1)}, s32[152]{0:T(256)S(1)}, bf16[32,5,256,256]{3,2,1,0:T(8,128)(2,1)S(1)}) custom-call(s32[5,32]{1,0:T(8,128)S(1)} %bitcast.114, bf16[64,64,126]{2,1,0:T(8,128)(2,1)} %bitcast.125, bf16[64,64,126]{2,1,0:T(8,128)(2,1)} %bitcast.126, bf16[32,5,256,256]{3,2,1,0:T(8,128)(2,1)} %refs_3_.7), custom_call_target="tpu_custom_call" | custom-call | flops 10000000 | bytes 8000000 | tf_op jit(solution)/shard_map/table/pallas_call | solution.py:220
  18.0 3.1 %shard_map.104 = (f32[64,2048]{1,0:T(8,128)S(1)}, bf16[32,5,256,256]{3,2,1,0:T(8,128)(2,1)S(1)}) custom-call(s32[5,32]{1,0:T(8,128)S(1)} %bitcast.115, bf16[64,8192]{1,0:T(8,128)(2,1)S(1)} %copy-done, bf16[32,5,256,256]{3,2,1,0:T(8,128)(2,1)S(1)} %get-tuple-element.43.refs_2_, bf16[32,5,256,256]{3,2,1,0:T(8,128)(2,1)} %refs_3_.7), custom_call_target="tpu_custom_call", output_to_operand_aliasing={{1}: (2, {})} | custom-call | flops 350000000 | bytes 6000000 | tf_op jit(solution)/shard_map/pallas_call | solution.py:283
  21.1 3.1 %shard_map.105 = (f32[64,2048]{1,0:T(8,128)S(1)}, bf16[32,5,256,256]{3,2,1,0:T(8,128)(2,1)S(1)}) custom-call(s32[5,32]{1,0:T(8,128)S(1)} %bitcast.116, bf16[64,8192]{1,0:T(8,128)(2,1)S(1)} %copy-done, bf16[32,5,256,256]{3,2,1,0:T(8,128)(2,1)S(1)} %get-tuple-element.44.refs_2_, bf16[32,5,256,256]{3,2,1,0:T(8,128)(2,1)} %refs_3_.7), custom_call_target="tpu_custom_call", output_to_operand_aliasing={{1}: (2, {})} | custom-call | flops 350000000 | bytes 6000000 | tf_op jit(solution)/shard_map/pallas_call | solution.py:283
  24.3 3.1 %shard_map.106 = (f32[64,2048]{1,0:T(8,128)S(1)}, bf16[32,5,256,256]{3,2,1,0:T(8,128)(2,1)S(1)}) custom-call(s32[5,32]{1,0:T(8,128)S(1)} %bitcast.117, bf16[64,8192]{1,0:T(8,128)(2,1)S(1)} %copy-done, bf16[32,5,256,256]{3,2,1,0:T(8,128)(2,1)S(1)} %get-tuple-element.45.refs_2_, bf16[32,5,256,256]{3,2,1,0:T(8,128)(2,1)} %refs_3_.7), custom_call_target="tpu_custom_call", output_to_operand_aliasing={{1}: (2, {})} | custom-call | flops 350000000 | bytes 6000000 | tf_op jit(solution)/shard_map/pallas_call | solution.py:283
  33.2 2.9 %collective-permute-done.4 = f32[64,64]{1,0:T(8,128)S(1)} collective-permute-done((f32[64,64]{1,0:T(8,128)S(1)}, f32[64,64]{1,0:T(8,128)S(1)}, u32[]{:S(2)}, u32[]{:S(2)}) %collective-permute-start.4) | collective-permute-done | bytes 16416 | tf_op jit(solution)/shard_map/ppermute | solution.py:437
  36.7 3.5 %collective-permute-done.5 = f32[64,64]{1,0:T(8,128)S(1)} collective-permute-done((f32[64,64]{1,0:T(8,128)S(1)}, f32[64,64]{1,0:T(8,128)S(1)}, u32[]{:S(2)}, u32[]{:S(2)}) %collective-permute-start.5) | collective-permute-done | bytes 16416 | tf_op jit(solution)/shard_map/ppermute | solution.py:437
  42.1 3.5 %collective-permute-done.6 = f32[64,64]{1,0:T(8,128)S(1)} collective-permute-done((f32[64,64]{1,0:T(8,128)S(1)}, f32[64,64]{1,0:T(8,128)S(1)}, u32[]{:S(2)}, u32[]{:S(2)}) %collective-permute-start.6) | collective-permute-done | bytes 16416 | tf_op jit(solution)/shard_map/ppermute | solution.py:437
  46.3 4.6 %collective-permute-start.7 = (bf16[64,2048]{1,0:T(8,128)(2,1)S(1)}, bf16[64,2048]{1,0:T(8,128)(2,1)S(1)}, u32[]{:S(2)}, u32[]{:S(2)}) collective-permute-start(bf16[64,2048]{1,0:T(8,128)(2,1)S(1)} %get-tuple-element.40.refs_6_), channel_id=1, source_target_pairs={{2,4},{6,8},{10,12},{14,16},{18,20},{22,24},{26,28},{30,32},{34,36... | collective-permute-start | bytes 786440 | tf_op jit(solution)/shard_map/ppermute | solution.py:443
  51.4 4.9 %collective-permute-done.9 = f32[64,64]{1,0:T(8,128)S(1)} collective-permute-done((f32[64,64]{1,0:T(8,128)S(1)}, f32[64,64]{1,0:T(8,128)S(1)}, u32[]{:S(2)}, u32[]{:S(2)}) %collective-permute-start.9) | collective-permute-done | bytes 16416 | tf_op jit(solution)/shard_map/ppermute | solution.py:437
  58.8 13.5 %tail.2 = (bf16[64,8192]{1,0:T(8,128)(2,1)}, bf16[64,8192]{1,0:T(8,128)(2,1)S(1)}, bf16[64,4096]{1,0:T(8,128)(2,1)S(1)}, bf16[64,4096]{1,0:T(8,128)(2,1)S(1)}, b...) custom-call(s32[152]{0:T(256)S(1)} %get-tuple-element.32.refs_0_, s32[4,32]{1,0:T(4,128)S(1)} %bitcast.123, ...), custom_call_target="tpu_custom_call" | custom-call | flops 1000000000 | bytes 10000000 | tf_op jit(solution)/shard_map/tail/pallas_call | solution.py:421
  72.4 2.3 %shard_map.111.refs_15_ = f32[64,2048]{1,0:T(8,128)S(1)} custom-call(s32[5,32]{1,0:T(8,128)S(1)} %bitcast.119, bf16[64,8192]{1,0:T(8,128)(2,1)S(1)} %get-tuple-element.61.refs_1_, bf16[32,5,256,256]{3,2,1,0:T(8,128)(2,1)S(1)} %get-tuple-element.46.refs_2_.refs_11_), custom_call_target="tpu_custom_call" | custom-call | flops 350000000 | bytes 6000000 | tf_op jit(solution)/shard_map/pallas_call | solution.py:283
  74.7 2.3 %shard_map.110.refs_14_ = f32[64,2048]{1,0:T(8,128)S(1)} custom-call(s32[5,32]{1,0:T(8,128)S(1)} %bitcast.120, bf16[64,8192]{1,0:T(8,128)(2,1)S(1)} %get-tuple-element.61.refs_1_, bf16[32,5,256,256]{3,2,1,0:T(8,128)(2,1)S(1)} %get-tuple-element.46.refs_2_.refs_11_), custom_call_target="tpu_custom_call" | custom-call | flops 350000000 | bytes 6000000 | tf_op jit(solution)/shard_map/pallas_call | solution.py:283
  77.0 2.3 %shard_map.109.refs_13_ = f32[64,2048]{1,0:T(8,128)S(1)} custom-call(s32[5,32]{1,0:T(8,128)S(1)} %bitcast.121, bf16[64,8192]{1,0:T(8,128)(2,1)S(1)} %get-tuple-element.61.refs_1_, bf16[32,5,256,256]{3,2,1,0:T(8,128)(2,1)S(1)} %get-tuple-element.46.refs_2_.refs_11_), custom_call_target="tpu_custom_call" | custom-call | flops 350000000 | bytes 6000000 | tf_op jit(solution)/shard_map/pallas_call | solution.py:283
  79.4 2.3 %shard_map.108.refs_12_ = f32[64,2048]{1,0:T(8,128)S(1)} custom-call(s32[5,32]{1,0:T(8,128)S(1)} %bitcast.122, bf16[64,8192]{1,0:T(8,128)(2,1)S(1)} %get-tuple-element.61.refs_1_, bf16[32,5,256,256]{3,2,1,0:T(8,128)(2,1)S(1)} %get-tuple-element.46.refs_2_.refs_11_), custom_call_target="tpu_custom_call" | custom-call | flops 350000000 | bytes 6000000 | tf_op jit(solution)/shard_map/pallas_call | solution.py:283
  86.3 2.8 %collective-permute-done.12 = f32[64,64]{1,0:T(8,128)S(1)} collective-permute-done((f32[64,64]{1,0:T(8,128)S(1)}, f32[64,64]{1,0:T(8,128)S(1)}, u32[]{:S(2)}, u32[]{:S(2)}) %collective-permute-start.12) | collective-permute-done | bytes 16416 | tf_op jit(solution)/shard_map/ppermute | solution.py:437
  89.8 3.5 %collective-permute-done.13 = f32[64,64]{1,0:T(8,128)S(1)} collective-permute-done((f32[64,64]{1,0:T(8,128)S(1)}, f32[64,64]{1,0:T(8,128)S(1)}, u32[]{:S(2)}, u32[]{:S(2)}) %collective-permute-start.13) | collective-permute-done | bytes 16416 | tf_op jit(solution)/shard_map/ppermute | solution.py:437
  94.0 4.8 %collective-permute-done.14 = f32[64,64]{1,0:T(8,128)S(1)} collective-permute-done((f32[64,64]{1,0:T(8,128)S(1)}, f32[64,64]{1,0:T(8,128)S(1)}, u32[]{:S(2)}, u32[]{:S(2)}) %collective-permute-start.14) | collective-permute-done | bytes 16416 | tf_op jit(solution)/shard_map/ppermute | solution.py:437
  99.1 10.2 %collective-permute-start.18 = (f32[64,64]{1,0:T(8,128)S(1)}, f32[64,64]{1,0:T(8,128)S(1)}, u32[]{:S(2)}, u32[]{:S(2)}) collective-permute-start(f32[64,64]{1,0:T(8,128)S(1)} %convolution_add_fusion.1), channel_id=1, source_target_pairs={{0,32},{2,34},{4,36},{6,38},{8,40},{10,42},{12,44},{14,46},{16,48}... | collective-permute-start | bytes 49160 | tf_op jit(solution)/shard_map/ppermute | solution.py:437
  109.5 2.5 %collective-permute-start.15 = (bf16[64,4096]{1,0:T(8,128)(2,1)S(1)}, bf16[64,4096]{1,0:T(8,128)(2,1)S(1)}, u32[]{:S(2)}, u32[]{:S(2)}) collective-permute-start(bf16[64,4096]{1,0:T(8,128)(2,1)S(1)} %get-tuple-element.58), channel_id=1, source_target_pairs={{2,4},{6,8},{10,12},{14,16},{18,20},{22,24},{26,28},{30,32},{34,36... | collective-permute-start | bytes 1572872 | tf_op jit(solution)/shard_map/ppermute | solution.py:443
  112.0 7.6 %collective-permute-start.17 = (bf16[64,2048]{1,0:T(8,128)(2,1)S(1)}, bf16[64,2048]{1,0:T(8,128)(2,1)S(1)}, u32[]{:S(2)}, u32[]{:S(2)}) collective-permute-start(bf16[64,2048]{1,0:T(8,128)(2,1)S(1)} %get-tuple-element.59.refs_6_), channel_id=1, source_target_pairs={{2,4},{6,8},{10,12},{14,16},{18,20},{22,24},{26,28},{30,32},{34,36... | collective-permute-start | bytes 786440 | tf_op jit(solution)/shard_map/ppermute | solution.py:443
  120.0 4.9 %collective-permute-done.19 = f32[64,64]{1,0:T(8,128)S(1)} collective-permute-done((f32[64,64]{1,0:T(8,128)S(1)}, f32[64,64]{1,0:T(8,128)S(1)}, u32[]{:S(2)}, u32[]{:S(2)}) %collective-permute-start.19) | collective-permute-done | bytes 16416 | tf_op jit(solution)/shard_map/ppermute | solution.py:437
  127.6 10.9 %tail.3 = bf16[64,8192]{1,0:T(8,128)(2,1)} custom-call(s32[152]{0:T(256)S(1)} %get-tuple-element.32.refs_0_, s32[4,32]{1,0:T(4,128)S(1)} %bitcast.124, bf16[64,4096]{1,0:T(8,128)(2,1)S(1)} %collective-permute-done.11.refs_2_, bf16[64,4096]{1,0:T(8,128)(2,1)S(1)} %collective-permute-done.15.refs_3_, bf16[64,2048]{1,0:T(8,128)(2,1)S(1)} %collective-permute-done.16.refs_4_, ...), custom_call_target="tpu_custom_call" | custom-call | flops 1000000000 | bytes 10000000 | tf_op jit(solution)/shard_map/tail/pallas_call | solution.py:421
  (76 shorter events, 25.1 us)
Async XLA Ops:
  2.0 56.8 %collective-permute-start = (bf16[64,4096]{1,0:T(8,128)(2,1)S(1)}, bf16[64,4096]{1,0:T(8,128)(2,1)S(1)}, u32[]{:S(2)}, u32[]{:S(2)}) collective-permute-start(bf16[64,4096]{1,0:T(8,128)(2,1)S(1)} %get-tuple-element.33.va), channel_id=1, source_target_pairs={{0,2},{2,0},{4,6},{6,4},{8,10},{10,8},{12,14},{14,12},{16,18},{18,... | collective-permute-start | bytes 1572872 | tf_op jit(solution)/shard_map/ppermute | solution.py:437
  3.5 55.3 %collective-permute-start.1 = (bf16[64,4096]{1,0:T(8,128)(2,1)S(1)}, bf16[64,4096]{1,0:T(8,128)(2,1)S(1)}, u32[]{:S(2)}, u32[]{:S(2)}) collective-permute-start(bf16[64,4096]{1,0:T(8,128)(2,1)S(1)} %get-tuple-element.34.vb), channel_id=1, source_target_pairs={{2,4},{6,8},{10,12},{14,16},{18,20},{22,24},{26,28},{30,32},{34,36... | collective-permute-start | bytes 1572872 | tf_op jit(solution)/shard_map/ppermute | solution.py:443
  12.6 18.0 %collective-permute-start.2 = (f32[64,64]{1,0:T(8,128)S(1)}, f32[64,64]{1,0:T(8,128)S(1)}, u32[]{:S(2)}, u32[]{:S(2)}) collective-permute-start(f32[64,64]{1,0:T(8,128)S(1)} %get-tuple-element.36), channel_id=1, source_target_pairs={{0,2},{2,0},{4,6},{6,4},{8,10},{10,8},{12,14},{14,12},{16,18},{18,... | collective-permute-start | bytes 49160 | tf_op jit(solution)/shard_map/ppermute | solution.py:437
  27.4 31.4 %copy-start.1 = (bf16[32,64,256]{2,1,0:T(8,128)(2,1)S(1)}, bf16[32,64,256]{2,1,0:T(8,128)(2,1)}, u32[]{:S(2)}) copy-start(bf16[32,64,256]{2,1,0:T(8,128)(2,1)} %refs_8_.3) | copy-start | bytes 3145732
  27.4 31.4 %copy-start.2 = (bf16[32,4,64,64]{3,2,1,0:T(8,128)(2,1)S(1)}, bf16[32,4,64,64]{3,2,1,0:T(8,128)(2,1)}, u32[]{:S(2)}) copy-start(bf16[32,4,64,64]{3,2,1,0:T(8,128)(2,1)} %refs_10_.3) | copy-start | bytes 3145732
  27.4 31.4 %copy-start.3 = (bf16[32,64,64]{2,1,0:T(8,128)(2,1)S(1)}, bf16[32,64,64]{2,1,0:T(8,128)(2,1)}, u32[]{:S(2)}) copy-start(bf16[32,64,64]{2,1,0:T(8,128)(2,1)} %param.13) | copy-start | bytes 786436
  29.7 42.6 %copy-start.5 = (s32[32,5]{0,1:T(8,128)S(1)}, s32[32,5]{0,1:T(8,128)}, u32[]{:S(2)}) copy-start(s32[32,5]{0,1:T(8,128)} %param.12) | copy-start | bytes 1924
  30.9 5.2 %collective-permute-start.4 = (f32[64,64]{1,0:T(8,128)S(1)}, f32[64,64]{1,0:T(8,128)S(1)}, u32[]{:S(2)}, u32[]{:S(2)}) collective-permute-start(f32[64,64]{1,0:T(8,128)S(1)} %convolution_add_fusion.11), channel_id=1, source_target_pairs={{0,6},{2,4},{4,2},{6,0},{8,14},{10,12},{12,10},{14,8},{16,22},{18,... | collective-permute-start | bytes 49160 | tf_op jit(solution)/shard_map/ppermute | solution.py:437
  31.1 25.6 %collective-permute-start.3 = (bf16[64,2048]{1,0:T(8,128)(2,1)S(1)}, bf16[64,2048]{1,0:T(8,128)(2,1)S(1)}, u32[]{:S(2)}, u32[]{:S(2)}) collective-permute-start(bf16[64,2048]{1,0:T(8,128)(2,1)S(1)} %get-tuple-element.40.refs_6_), channel_id=1, source_target_pairs={{0,2},{2,0},{4,6},{6,4},{8,10},{10,8},{12,14},{14,12},{16,18},{18,... | collective-permute-start | bytes 786440 | tf_op jit(solution)/shard_map/ppermute | solution.py:437
  36.2 4.0 %collective-permute-start.5 = (f32[64,64]{1,0:T(8,128)S(1)}, f32[64,64]{1,0:T(8,128)S(1)}, u32[]{:S(2)}, u32[]{:S(2)}) collective-permute-start(f32[64,64]{1,0:T(8,128)S(1)} %convolution_add_fusion.10), channel_id=1, source_target_pairs={{0,8},{2,10},{4,12},{6,14},{8,0},{10,2},{12,4},{14,6},{16,24},{18,... | collective-permute-start | bytes 49160 | tf_op jit(solution)/shard_map/ppermute | solution.py:437
  40.4 5.2 %collective-permute-start.6 = (f32[64,64]{1,0:T(8,128)S(1)}, f32[64,64]{1,0:T(8,128)S(1)}, u32[]{:S(2)}, u32[]{:S(2)}) collective-permute-start(f32[64,64]{1,0:T(8,128)S(1)} %convolution_add_fusion.9), channel_id=1, source_target_pairs={{0,24},{2,26},{4,28},{6,30},{8,16},{10,18},{12,20},{14,22},{16,8},... | collective-permute-start | bytes 49160 | tf_op jit(solution)/shard_map/ppermute | solution.py:437
  46.0 5.0 %collective-permute-start.8 = (f32[64,64]{1,0:T(8,128)S(1)}, f32[64,64]{1,0:T(8,128)S(1)}, u32[]{:S(2)}, u32[]{:S(2)}) collective-permute-start(f32[64,64]{1,0:T(8,128)S(1)} %convolution_add_fusion.7), channel_id=1, source_target_pairs={{0,32},{2,34},{4,36},{6,38},{8,40},{10,42},{12,44},{14,46},{16,48}... | collective-permute-start | bytes 49160 | tf_op jit(solution)/shard_map/ppermute | solution.py:437
  46.3 12.5 %collective-permute-start.7 = (bf16[64,2048]{1,0:T(8,128)(2,1)S(1)}, bf16[64,2048]{1,0:T(8,128)(2,1)S(1)}, u32[]{:S(2)}, u32[]{:S(2)}) collective-permute-start(bf16[64,2048]{1,0:T(8,128)(2,1)S(1)} %get-tuple-element.40.refs_6_), channel_id=1, source_target_pairs={{2,4},{6,8},{10,12},{14,16},{18,20},{22,24},{26,28},{30,32},{34,36... | collective-permute-start | bytes 786440 | tf_op jit(solution)/shard_map/ppermute | solution.py:443
  51.1 5.2 %collective-permute-start.9 = (f32[64,64]{1,0:T(8,128)S(1)}, f32[64,64]{1,0:T(8,128)S(1)}, u32[]{:S(2)}, u32[]{:S(2)}) collective-permute-start(f32[64,64]{1,0:T(8,128)S(1)} %convolution_add_fusion.6), channel_id=1, source_target_pairs={{0,96},{2,98},{4,100},{6,102},{8,104},{10,106},{12,108},{14,110},{... | collective-permute-start | bytes 49160 | tf_op jit(solution)/shard_map/ppermute | solution.py:437
  79.3 4.3 %collective-permute-start.10 = (f32[64,64]{1,0:T(8,128)S(1)}, f32[64,64]{1,0:T(8,128)S(1)}, u32[]{:S(2)}, u32[]{:S(2)}) collective-permute-start(f32[64,64]{1,0:T(8,128)S(1)} %get-tuple-element.53), channel_id=1, source_target_pairs={{0,2},{2,0},{4,6},{6,4},{8,10},{10,8},{12,14},{14,12},{16,18},{18,... | collective-permute-start | bytes 49160 | tf_op jit(solution)/shard_map/ppermute | solution.py:437
  84.0 5.2 %collective-permute-start.12 = (f32[64,64]{1,0:T(8,128)S(1)}, f32[64,64]{1,0:T(8,128)S(1)}, u32[]{:S(2)}, u32[]{:S(2)}) collective-permute-start(f32[64,64]{1,0:T(8,128)S(1)} %convolution_add_fusion.5), channel_id=1, source_target_pairs={{0,6},{2,4},{4,2},{6,0},{8,14},{10,12},{12,10},{14,8},{16,22},{18,... | collective-permute-start | bytes 49160 | tf_op jit(solution)/shard_map/ppermute | solution.py:437
  84.2 43.3 %collective-permute-start.11 = (bf16[64,4096]{1,0:T(8,128)(2,1)S(1)}, bf16[64,4096]{1,0:T(8,128)(2,1)S(1)}, u32[]{:S(2)}, u32[]{:S(2)}) collective-permute-start(bf16[64,4096]{1,0:T(8,128)(2,1)S(1)} %get-tuple-element.54), channel_id=1, source_target_pairs={{0,2},{2,0},{4,6},{6,4},{8,10},{10,8},{12,14},{14,12},{16,18},{18,... | collective-permute-start | bytes 1572872 | tf_op jit(solution)/shard_map/ppermute | solution.py:437
  84.4 40.9 %collective-permute-start.16 = (bf16[64,2048]{1,0:T(8,128)(2,1)S(1)}, bf16[64,2048]{1,0:T(8,128)(2,1)S(1)}, u32[]{:S(2)}, u32[]{:S(2)}) collective-permute-start(bf16[64,2048]{1,0:T(8,128)(2,1)S(1)} %get-tuple-element.59.refs_6_), channel_id=1, source_target_pairs={{0,2},{2,0},{4,6},{6,4},{8,10},{10,8},{12,14},{14,12},{16,18},{18,... | collective-permute-start | bytes 786440 | tf_op jit(solution)/shard_map/ppermute | solution.py:437
  89.3 4.0 %collective-permute-start.13 = (f32[64,64]{1,0:T(8,128)S(1)}, f32[64,64]{1,0:T(8,128)S(1)}, u32[]{:S(2)}, u32[]{:S(2)}) collective-permute-start(f32[64,64]{1,0:T(8,128)S(1)} %convolution_add_fusion.4), channel_id=1, source_target_pairs={{0,8},{2,10},{4,12},{6,14},{8,0},{10,2},{12,4},{14,6},{16,24},{18,... | collective-permute-start | bytes 49160 | tf_op jit(solution)/shard_map/ppermute | solution.py:437
  93.5 5.2 %collective-permute-start.14 = (f32[64,64]{1,0:T(8,128)S(1)}, f32[64,64]{1,0:T(8,128)S(1)}, u32[]{:S(2)}, u32[]{:S(2)}) collective-permute-start(f32[64,64]{1,0:T(8,128)S(1)} %convolution_add_fusion.3), channel_id=1, source_target_pairs={{0,24},{2,26},{4,28},{6,30},{8,16},{10,18},{12,20},{14,22},{16,8},... | collective-permute-start | bytes 49160 | tf_op jit(solution)/shard_map/ppermute | solution.py:437
  99.1 20.5 %collective-permute-start.18 = (f32[64,64]{1,0:T(8,128)S(1)}, f32[64,64]{1,0:T(8,128)S(1)}, u32[]{:S(2)}, u32[]{:S(2)}) collective-permute-start(f32[64,64]{1,0:T(8,128)S(1)} %convolution_add_fusion.1), channel_id=1, source_target_pairs={{0,32},{2,34},{4,36},{6,38},{8,40},{10,42},{12,44},{14,46},{16,48}... | collective-permute-start | bytes 49160 | tf_op jit(solution)/shard_map/ppermute | solution.py:437
  109.5 18.1 %collective-permute-start.15 = (bf16[64,4096]{1,0:T(8,128)(2,1)S(1)}, bf16[64,4096]{1,0:T(8,128)(2,1)S(1)}, u32[]{:S(2)}, u32[]{:S(2)}) collective-permute-start(bf16[64,4096]{1,0:T(8,128)(2,1)S(1)} %get-tuple-element.58), channel_id=1, source_target_pairs={{2,4},{6,8},{10,12},{14,16},{18,20},{22,24},{26,28},{30,32},{34,36... | collective-permute-start | bytes 1572872 | tf_op jit(solution)/shard_map/ppermute | solution.py:443
  112.0 15.6 %collective-permute-start.17 = (bf16[64,2048]{1,0:T(8,128)(2,1)S(1)}, bf16[64,2048]{1,0:T(8,128)(2,1)S(1)}, u32[]{:S(2)}, u32[]{:S(2)}) collective-permute-start(bf16[64,2048]{1,0:T(8,128)(2,1)S(1)} %get-tuple-element.59.refs_6_), channel_id=1, source_target_pairs={{2,4},{6,8},{10,12},{14,16},{18,20},{22,24},{26,28},{30,32},{34,36... | collective-permute-start | bytes 786440 | tf_op jit(solution)/shard_map/ppermute | solution.py:443
  119.7 5.2 %collective-permute-start.19 = (f32[64,64]{1,0:T(8,128)S(1)}, f32[64,64]{1,0:T(8,128)S(1)}, u32[]{:S(2)}, u32[]{:S(2)}) collective-permute-start(f32[64,64]{1,0:T(8,128)S(1)} %convolution_add_fusion), channel_id=1, source_target_pairs={{0,96},{2,98},{4,100},{6,102},{8,104},{10,106},{12,108},{14,110},{... | collective-permute-start | bytes 49160 | tf_op jit(solution)/shard_map/ppermute | solution.py:437
  (3 other events, 49.4 us)

commit v5 on v4

--- a/solution.py
+++ b/solution.py
@@ -10,7 +10,7 @@
 FARR = 32
 PIECES = 4
 TOGETHER = 8
-COUNT = 144
+LIST = 80
 BF = jnp.bfloat16
 F32 = jnp.float32
 NT = (((1,), (1,)), ((), ()))
@@ -151,20 +151,27 @@
     device = lax.axis_index("leaf")
     kn, leaves = near_list.shape
     first = device * leaves
-
-    def scan(leaf, n):
+    even = is_even()
+
+    def scan(leaf, found):
+        in_a, in_b = found
         for slot in range(kn):
             source = near_list[slot, leaf] - first
             left = source < 0
-            place = source + jnp.where(left, REACH, REACH - leaves)
-            plan[n] = (leaf * 8 + slot) * 32 + place
-            n = n + jnp.where(left | (source >= leaves), 1, 0)
-        return n
-
-    total = lax.fori_loop(0, leaves, scan, 0)
-    for i in range(TOGETHER):
-        plan[total + i] = (leaves * 8) * 32
-    plan[COUNT] = lax.div(total + TOGETHER - 1, TOGETHER)
+            outside = left | (source >= leaves)
+            to_a = left != even
+            code = (leaf * 8 + slot) * 16 + source + jnp.where(left, REACH, -leaves)
+            plan[in_a] = code
+            plan[LIST + in_b] = code
+            in_a = in_a + jnp.where(outside & to_a, 1, 0)
+            in_b = in_b + jnp.where(outside & jnp.logical_not(to_a), 1, 0)
+        return in_a, in_b
+
+    found = lax.fori_loop(0, leaves, scan, (jnp.int32(0), jnp.int32(0)))
+    for side, total in enumerate(found):
+        for i in range(TOGETHER):
+            plan[side * LIST + total + i] = (leaves * 8) * 16
+        plan[2 * LIST + side] = lax.div(total + TOGETHER - 1, TOGETHER)
     count, rows, nodes = 8, trans.shape[0], trans.shape[2]
     row = lax.broadcasted_iota(jnp.int32, (count, nodes), 0)
     node = lax.broadcasted_iota(jnp.int32, (count, nodes), 1)
@@ -232,7 +239,7 @@
         out_shape=[
             jax.ShapeDtypeStruct((2, levels, rank, rank), F32),
             jax.ShapeDtypeStruct((levels, rank, rank), F32),
-            jax.ShapeDtypeStruct((COUNT + 8,), jnp.int32),
+            jax.ShapeDtypeStruct((2 * LIST + 8,), jnp.int32),
             jax.ShapeDtypeStruct(shape, BF),
         ],
         compiler_params=params(6),
@@ -295,142 +302,165 @@
     )(near_list_t, *args)
 
 
-def tail_body(more, plan, couple_list, *refs):
-    got_va, got_vb, got_ca, got_cb, sent_c, top, basis, trans, couple = refs[:9]
-    refs = refs[9:]
-    near, partial, refs = refs[0], refs[1 : 1 + PIECES], refs[1 + PIECES :]
-    if more:
-        image, own_v, va, vb, coef, node, table_ref, wide, acc, total_ref, sems = refs
-    else:
-        image, own_v, table_ref, wide, acc, sems = refs
-    leaves, rank, points = basis.shape
-    some = leaves // PIECES
-    half = leaves // 2 * points
-    even = is_even()
-    first = lax.axis_index("leaf") * leaves
-    start_a = jnp.where(even, half, 0)
-    copies = [
-        pltpu.make_async_copy(ref, wide.at[:, columns_of(start, half)], sems.at[i])
-        for i, (ref, start) in enumerate(((got_va, start_a), (got_vb, half - start_a)))
-    ]
-    for copy in copies:
-        copy.start()
-    row = lax.broadcasted_iota(jnp.int32, (2 * rank, 2 * rank), 0)
-    lane = lax.broadcasted_iota(jnp.int32, (2 * rank, 2 * rank), 1)
-    swap = jnp.where(jnp.bitwise_xor(row, rank) == lane, 1.0, 0.0).astype(BF)
-    base_a = jnp.where(even, 2 * leaves, 0)
-    for ref, base in ((got_ca, base_a), (sent_c, leaves), (got_cb, 2 * leaves - base_a)):
-        for pair in range(leaves // 2):
-            both = ref[:, 2 * rank * pair : 2 * rank * (pair + 1)]
-            table_ref[base + 2 * pair] = both
-            table_ref[base + 2 * pair + 1] = mm(both, swap).astype(BF)
-    descent = top[...].astype(BF)
-    if more:
-        total_ref[...] = jnp.zeros_like(total_ref)
-    for piece in range(PIECES):
-        width = some * points
-        acc[:, piece * width : (piece + 1) * width] = partial[piece][...]
-    for copy in copies:
-        copy.wait()
+def add_halo(side, plan, v, near, acc):
+    leaves, _, points, _ = near.shape
 
     def add(j, carry):
         terms = []
         for i in range(TOGETHER):
-            code = plan[j * TOGETHER + i]
-            leaf = lax.shift_right_logical(code, 8)
-            slot = lax.shift_right_logical(code, 5) & 7
-            rows = wide[:, columns_of((code & 31) * points, points)]
+            code = plan[side * LIST + j * TOGETHER + i]
+            leaf = lax.shift_right_logical(code, 7)
+            slot = lax.shift_right_logical(code, 4) & 7
+            rows = v[:, columns_of((code & 15) * points, points)]
             term = mm(rows, near[leaf & (leaves - 1), slot], NT)
             terms.append((columns_of(leaf * points, points), term))
         for here, term in terms:
             acc[:, here] += term
         return carry
 
-    lax.fori_loop(0, plan[COUNT], add, 0)
+    lax.fori_loop(0, plan[2 * LIST + side], add, 0)
+
+
+def unpack(coef, base, table_ref):
+    wide = table_ref.shape[2]
+    row = lax.broadcasted_iota(jnp.int32, (wide, wide), 0)
+    lane = lax.broadcasted_iota(jnp.int32, (wide, wide), 1)
+    swap = jnp.where(jnp.bitwise_xor(row, wide // 2) == lane, 1.0, 0.0).astype(BF)
+    for pair in range(coef.shape[1] // wide):
+        both = coef[:, wide * pair : wide * (pair + 1)]
+        table_ref[base + 2 * pair] = both
+        table_ref[base + 2 * pair + 1] = mm(both, swap).astype(BF)
+
+
+def side_body(plan, got_va, got_ca, sent_c, near, *refs):
+    partial, (acc, table_ref) = refs[:PIECES], refs[PIECES:]
+    leaves = near.shape[0]
+    for piece, part in enumerate(partial):
+        width = part.shape[1]
+        acc[:, piece * width : (piece + 1) * width] = part[...]
+    unpack(sent_c, leaves, table_ref)
+    unpack(got_ca, jnp.where(is_even(), 2 * leaves, 0), table_ref)
+    add_halo(0, plan, got_va, near, acc)
+
+
+def side_a(plan, got_va, got_ca, sent_c, kept, partial):
+    columns = sent_c.shape[0]
+    leaves, _, points, _ = kept.shape
+    rank = sent_c.shape[1] // leaves
+    return pl.pallas_call(
+        side_body,
+        grid_spec=pltpu.PrefetchScalarGridSpec(
+            num_scalar_prefetch=1,
+            in_specs=[VMEM] * (4 + PIECES),
+            out_specs=[VMEM] * 2,
+        ),
+        out_shape=[
+            jax.ShapeDtypeStruct((columns, (leaves + 1) * points), F32),
+            jax.ShapeDtypeStruct((3 * leaves, columns, 2 * rank), BF),
+        ],
+        compiler_params=params(4),
+        cost_estimate=cost(400_000_000, 6_000_000),
+        name="side",
+    )(plan, got_va, got_ca, sent_c, kept, *partial)
+
+
+def tail_body(names, sides, more, *refs):
+    r = dict(zip(names, refs))
+    acc, table_ref, couple_list = r["acc"], r["table"], r["couple_list"]
+    basis, trans, couple, image = r["basis"], r["trans"], r["couple"], r["image"]
+    leaves, rank, points = basis.shape
+    group = leaves // 4
+    even = is_even()
+    first = lax.axis_index("leaf") * leaves
+    first_b = jnp.where(even, 0, leaves // 2)
+    descent = r["top"][...].astype(BF)
+    if "b" in sides:
+        unpack(r["got_cb"], jnp.where(even, 0, 2 * leaves), table_ref)
+        add_halo(1, r["plan"], r["got_vb"], r["near"], acc)
+    own_v = r["own_v"]
     writes = []
-    for piece in range(PIECES):
-        results = []
-        for i in range(some):
-            leaf = piece * some + i
-            moved = trans[leaf * rank : (leaf + 1) * rank, :]
-            local = mm(descent, moved, NT)
-            for s in range(couple.shape[1]):
-                source = couple_list[s, leaf] - first + FARR
-                local += mm(table_ref[source, :, :rank], couple[leaf, s], NT)
-            here = slice(leaf * points, (leaf + 1) * points)
-            value = (acc[:, here] + mm(local.astype(BF), basis[leaf])).astype(BF)
-            results.append(value)
-            own_v[:, here] = value
-        here = pl.ds(piece * some * points, some * points)
-        writes.append(pltpu.make_async_copy(own_v.at[:, here], image.at[:, here], sems.at[2 + piece]))
-        writes[-1].start()
-        if not more:
-            continue
-        for pair in range(some // 2):
-            leaf = piece * some + 2 * pair
-            rows = jnp.concatenate(results[2 * pair : 2 * pair + 2], axis=1)
-            both = paired_coef(rows, basis[leaf], basis[leaf + 1])
-            coef[:, leaf * rank : (leaf + 2) * rank] = both
-            total_ref[...] += mm(both, trans[leaf * rank : (leaf + 2) * rank, :])
-        in_right = piece >= PIECES // 2
-        start = piece % (PIECES // 2) * some * points
-
-        def put(message, results=results, start=start):
-            for i, value in enumerate(results):
-                message[:, start + i * points : start + (i + 1) * points] = value
-
-        @pl.when(even == in_right)
-        def _():
-            put(va)
-
-        @pl.when(even != in_right)
-        def _():
-            put(vb)
-
+    total = r["node_in"][...] if "node_in" in r else None
+    for side in sides:
+        start = first_b if side == "b" else leaves // 2 - first_b
+        for part in range(2):
+            base = start + part * group
+            results = []
+            for i in range(group):
+                leaf = base + i
+                moved = trans[columns_of(leaf * rank, rank), :]
+                local = mm(descent, moved, NT)
+                for s in range(couple.shape[1]):
+                    source = couple_list[s, leaf] - first + FARR
+                    local += mm(table_ref[source, :, :rank], couple[leaf, s], NT)
+                here = columns_of(leaf * points, points)
+                value = (acc[:, here] + mm(local.astype(BF), basis[leaf])).astype(BF)
+                results.append(value)
+                own_v[:, here] = value
+                if more:
+                    at = (part * group + i) * points
+                    r["message"][:, at : at + points] = value
+            here = columns_of(base * points, group * points)
+            writes.append(
+                pltpu.make_async_copy(own_v.at[:, here], image.at[:, here], r["sems"].at[len(writes)])
+            )
+            writes[-1].start()
+            if not more:
+                continue
+            for pair in range(group // 2):
+                leaf = base + 2 * pair
+                rows = jnp.concatenate(results[2 * pair : 2 * pair + 2], axis=1)
+                both = paired_coef(rows, basis[leaf], basis[leaf + 1])
+                at = columns_of((base // 2 + pair) * 2 * rank, 2 * rank)
+                r["coef"][:, at] = both
+                term = mm(both, trans[at, :])
+                total = term if total is None else total + term
     if more:
-        node[...] = total_ref[...]
+        r["node"][...] = total
     for write in writes:
         write.wait()
 
 
-def tail(more, lists, got, sent_c, top, kept, partial, basis_t, trans2, leaf_couple):
-    columns = sent_c.shape[0]
-    leaves, rank, points = basis_t.shape
+def tail(sides, more, scalars, inputs, carried):
+    leaves, rank, points = inputs["basis"].shape
+    columns = inputs["top"].shape[0]
     own = leaves * points
-    image = jax.ShapeDtypeStruct((columns, own), BF)
-    out_shape, out_specs = [image], [HBM]
-    scratch = [
-        pltpu.VMEM((3 * leaves, columns, 2 * rank), BF),
-        pltpu.VMEM((columns, own), BF),
-        pltpu.VMEM((columns, own + points), F32),
-    ]
+    fresh = {}
+    if "image" not in carried:
+        fresh["image"] = jax.ShapeDtypeStruct((columns, own), BF)
     if more:
-        half = jax.ShapeDtypeStruct((columns, own // 2), BF)
-        out_shape += [
-            image,
-            half,
-            half,
-            jax.ShapeDtypeStruct((columns, leaves * rank), BF),
-            jax.ShapeDtypeStruct((columns, rank), F32),
-        ]
-        out_specs += [VMEM] * 5
-        scratch.append(pltpu.VMEM((columns, rank), F32))
-    else:
-        scratch.insert(0, pltpu.VMEM((columns, own), BF))
-    scratch.append(pltpu.SemaphoreType.DMA((2 + PIECES,)))
-    return pl.pallas_call(
-        lambda *refs: tail_body(more, *refs),
+        if "own_v" not in carried:
+            fresh["own_v"] = jax.ShapeDtypeStruct((columns, own), BF)
+            fresh["coef"] = jax.ShapeDtypeStruct((columns, leaves * rank), BF)
+        fresh["message"] = jax.ShapeDtypeStruct((columns, own // 2), BF)
+        fresh["node"] = jax.ShapeDtypeStruct((columns, rank), F32)
+    outs = [*carried, *fresh]
+    before = [*scalars, *inputs]
+    names = [*before, *(f"old_{name}" for name in carried), *outs]
+    scratch = [pltpu.SemaphoreType.DMA((4,))]
+    names.append("sems")
+    if not more:
+        scratch.append(pltpu.VMEM((columns, own), BF))
+        names.append("own_v")
+    spec = lambda name: HBM if name == "image" else VMEM
+    result = pl.pallas_call(
+        lambda *refs: tail_body(names, sides, more, *refs),
         grid_spec=pltpu.PrefetchScalarGridSpec(
-            num_scalar_prefetch=2,
-            in_specs=[VMEM] * (10 + PIECES),
-            out_specs=out_specs,
+            num_scalar_prefetch=len(scalars),
+            in_specs=[VMEM] * len(inputs) + [spec(name) for name in carried],
+            out_specs=[spec(name) for name in outs],
             scratch_shapes=scratch,
         ),
-        out_shape=out_shape,
-        compiler_params=params(12),
-        cost_estimate=cost(1_000_000_000, 10_000_000),
-        name="tail",
-    )(*lists, *got, sent_c, top, basis_t, trans2, leaf_couple, kept, *partial)
+        out_shape=[
+            jax.ShapeDtypeStruct(carried[name].shape, carried[name].dtype)
+            if name in carried
+            else fresh[name]
+            for name in outs
+        ],
+        input_output_aliases={len(before) + i: i for i in range(len(carried))},
+        compiler_params=params(6),
+        cost_estimate=cost(600_000_000, 6_000_000),
+    )(*scalars.values(), *inputs.values(), *carried.values())
+    return dict(zip(outs, result))
 
 
 def swapped(value, mask):
@@ -443,7 +473,7 @@
     return lax.ppermute(value, "leaf", pairs + [(j, i) for i, j in pairs])
 
 
-def one_product(node, va, vb, coef, got_va, got_vb, fill, tables):
+def one_product(node, va, coef, got_va, fill, tables):
     levels = lax.axis_size("leaf").bit_length() - 1
     top = jnp.zeros_like(node)
     got_ca = got_cb = None
@@ -459,16 +489,14 @@
                 got_va = swapped(va, 1)
             got_ca = swapped(coef, 1)
         if t == 3:
-            vb, later, other = lax.optimization_barrier((vb, coef, other))
-            if got_vb is None:
-                got_vb = swapped_odd(vb)
+            later, other = lax.optimization_barrier((coef, other))
             got_cb = swapped_odd(later)
         if t + 1 < levels:
             node = exact(node, up[0, t]) + exact(other, up[1, t])
         others.append(other)
     for t, other in enumerate(others):
         top += exact(other, down[t], NT)
-    return top, (got_va, got_vb, got_ca, got_cb)
+    return top, got_va, got_ca, got_cb
 
 
 def on_device(
@@ -486,7 +514,7 @@
     trans2 = leaf_transfer.reshape(leaves * rank, rank)
     near_list_t, couple_list_t = near_list.T, couple_list.T
     made = {}
-    partial = []
+    partial, again = [], []
 
     def fill_first(t):
         if t == 0:
@@ -505,28 +533,37 @@
             made["down"] = chain(made["up"], made["pair"])
         return made["up"], made.get("down")
 
+    def fill_second(t):
+        for piece in {1: (0, 1), 4: (2, 3)}.get(t, ()):
+            (out,) = near_piece(piece, near_list_t, made["own_v"], near_blocks, made["kept"], False)
+            again.append(out)
+
+    def parts(top, got_vb, got_cb):
+        scalars = {"plan": made["plan"], "couple_list": couple_list_t}
+        inputs = {"top": top, "basis": basis_t, "trans": trans2, "couple": leaf_couple}
+        on_b = {"got_vb": got_vb, "got_cb": got_cb, "near": made["kept"]}
+        return scalars, inputs, on_b
+
     va, vb = split(rhs_block)
     got_va = swapped(va, 1)
     got_vb = swapped_odd(vb)
     coef, node = head(va, vb, basis_t, trans2)
-    top, got = one_product(node, va, vb, coef, got_va, got_vb, fill_first, tables)
-    lists = (made["plan"], couple_list_t)
-    first_image, own_v, va, vb, coef_next, node = tail(
-        True, lists, got, coef, top, made["kept"], partial, basis_t, trans2, leaf_couple
+    top, _, got_ca, got_cb = one_product(node, va, coef, got_va, fill_first, tables)
+    acc, entries = side_a(made["plan"], got_va, got_ca, coef, made["kept"], partial)
+    scalars, inputs, on_b = parts(top, got_vb, got_cb)
+    half = tail("b", True, scalars, {**inputs, **on_b}, {"acc": acc, "table": entries})
+    got_vb = swapped_odd(half["message"])
+    inputs["node_in"] = half["node"]
+    carried = {k: half[k] for k in ("acc", "table", "image", "own_v", "coef")}
+    rest = tail("a", True, scalars, inputs, carried)
+    first_image, coef, made["own_v"] = rest["image"], rest["coef"], rest["own_v"]
+    top, got_va, got_ca, got_cb = one_product(
+        rest["node"], rest["message"], coef, None, fill_second, tables
     )
-    again = []
-
-    def fill_second(t):
-        if t == 4:
-            for piece in range(PIECES):
-                (out,) = near_piece(piece, near_list_t, own_v, near_blocks, made["kept"], False)
-                again.append(out)
-
-    top, got = one_product(node, va, vb, coef_next, None, None, fill_second, tables)
-    (second_image,) = tail(
-        False, lists, got, coef_next, top, made["kept"], again, basis_t, trans2, leaf_couple
-    )
-    return (first_image, second_image)
+    acc, entries = side_a(made["plan"], got_va, got_ca, coef, made["kept"], again)
+    scalars, inputs, on_b = parts(top, got_vb, got_cb)
+    last = tail("ba", False, scalars, {**inputs, **on_b}, {"acc": acc, "table": entries})
+    return (first_image, last["image"])
 
 
 def solution(mesh):

time: 139 us -> 128 us (0.921); the launches traced: 139 us -> 126 us
  starting transfers between devices: 39.3 us -> 31.9 us
  waiting for transfers between devices: 37.1 us -> 31.7 us
    ppermute x16, starting transfers between devices: 18.3 us -> 11.7 us  [swapped(): lax.ppermute(value, 'leaf', [(i, i ^ mask) for i in range(lax.axis_size('...]
    ppermute x4, waiting for transfers between devices: 4.31 us -> 0.21 us  [swapped_odd(): return lax.ppermute(value, 'leaf', pairs + [(j, i) for i, j in pairs])]
    pallas_call x2 -> x5, Pallas kernels: 24.4 us -> 25.3 us  [the longest x3 21.3 us: tail(): pl.pallas_call(lambda *refs: tail_body(names, sides, more, *refs), grid_s...]
  transfers between devices with their start and end apart: 20 -> 20, of which waited for: 11 -> 9; matrix products, arithmetic and copies ran while one was open for 4% -> 4% of each run, Pallas kernels for 16% -> 21%
where the time goes in v5:
time: 128 us; the launch traced here: 126 us
  Pallas kernels  55.5 us (43%)
  starting transfers between devices  31.9 us (25%)
  waiting for transfers between devices  31.7 us (25%)
  matrix products  5.45 us (4%)
  between operations  1.38 us (1%)
    ppermute x16, waiting for transfers between devices, swapped(): lax.ppermute(value, 'leaf', [(i, i ^ mask) for i in range(lax.axis_size('...  31.5 us
    pallas_call x3, Pallas kernels, tail(): pl.pallas_call(lambda *refs: tail_body(names, sides, more, *refs), grid_s...  21.3 us
    pallas_call x8, Pallas kernels, near_piece(): pl.pallas_call(lambda *refs: near_body(piece, load, *refs), grid_spec=plt...  20.9 us
    ppermute x4, starting transfers between devices, swapped_odd(): return lax.ppermute(value, 'leaf', pairs + [(j, i) for i, j in pairs])  20.2 us
    ppermute x16, starting transfers between devices, swapped(): lax.ppermute(value, 'leaf', [(i, i ^ mask) for i in range(lax.axis_size('...  11.7 us
    dot_general x32, matrix products, exact(): lax.dot_general(a, b, dims, precision=lax.Precision.HIGHEST, preferred_el...  5.45 us
    pallas_call x1, Pallas kernels, table(): pl.pallas_call(lambda *refs: table_body(levels, *refs), grid_spec=pltpu.P...  4.37 us
    pallas_call x2, Pallas kernels, side_a(): pl.pallas_call(side_body, grid_spec=pltpu.PrefetchScalarGridSpec(num_scal...  4 us
  transfers between devices with their start and end apart: 20, of which 9 were waited for; matrix products, arithmetic and copies ran while one was open for 4% of the time, Pallas kernels for 21%

profile of v5, /device:TPU:96, one launch (start us, length us, event | category | flops | bytes accessed | tf_op | source)
XLA Modules:
  0.0 125.9 jit_solution(33549702875217900)
XLA Ops:
  3.4 6.3 %collective-permute-start.6 = (bf16[64,4096]{1,0:T(8,128)(2,1)S(1)}, bf16[64,4096]{1,0:T(8,128)(2,1)S(1)}, u32[]{:S(2)}, u32[]{:S(2)}) collective-permute-start(bf16[64,4096]{1,0:T(8,128)(2,1)S(1)} %get-tuple-element.44.vb), channel_id=1, source_target_pairs={{2,4},{6,8},{10,12},{14,16},{18,20},{22,24},{26,28},{30,32},{34,36... | collective-permute-start | bytes 1572872 | tf_op jit(solution)/shard_map/ppermute | solution.py:473
  9.7 2.8 %head.1 = (bf16[64,2048]{1,0:T(8,128)(2,1)S(1)}, f32[64,64]{1,0:T(8,128)S(1)}) custom-call(bf16[64,4096]{1,0:T(8,128)(2,1)S(1)} %get-tuple-element.43.va, bf16[64,4096]{1,0:T(8,128)(2,1)S(1)} %get-tuple-element.44.vb, bf16[32,64,256]{2,1,0:T(8,128)(2,1)} %refs_3_.13, bf16[2048,64]{1,0:T(8,128)(2,1)} %bitcast.111), custom_call_target="tpu_custom_call" | custom-call | flops 200000000 | bytes 6000000 | tf_op jit(solution)/shard_map/head/pallas_call | solution.py:115
  12.7 4.4 %table.1 = (f32[2,6,64,64]{3,2,1,0:T(8,128)S(1)}, f32[6,64,64]{2,1,0:T(8,128)S(1)}, s32[168]{0:T(256)S(1)}, bf16[32,5,256,256]{3,2,1,0:T(8,128)(2,1)S(1)}) custom-call(s32[5,32]{1,0:T(8,128)S(1)} %bitcast.115, bf16[64,64,126]{2,1,0:T(8,128)(2,1)} %bitcast.127, bf16[64,64,126]{2,1,0:T(8,128)(2,1)} %bitcast.128, bf16[32,5,256,256]{3,2,1,0:T(8,128)(2,1)} %refs_3_.10), custom_call_target="tpu_custom_call" | custom-call | flops 10000000 | bytes 8000000 | tf_op jit(solution)/shard_map/table/pallas_call | solution.py:227
  17.0 3.1 %shard_map.104 = (f32[64,2048]{1,0:T(8,128)S(1)}, bf16[32,5,256,256]{3,2,1,0:T(8,128)(2,1)S(1)}) custom-call(s32[5,32]{1,0:T(8,128)S(1)} %bitcast.116, bf16[64,8192]{1,0:T(8,128)(2,1)S(1)} %copy-done, bf16[32,5,256,256]{3,2,1,0:T(8,128)(2,1)S(1)} %get-tuple-element.53.refs_2_, bf16[32,5,256,256]{3,2,1,0:T(8,128)(2,1)} %refs_3_.10), custom_call_target="tpu_custom_call", output_to_operand_aliasing={{1}: (2, {})} | custom-call | flops 350000000 | bytes 6000000 | tf_op jit(solution)/shard_map/pallas_call | solution.py:290
  20.2 3.1 %shard_map.105 = (f32[64,2048]{1,0:T(8,128)S(1)}, bf16[32,5,256,256]{3,2,1,0:T(8,128)(2,1)S(1)}) custom-call(s32[5,32]{1,0:T(8,128)S(1)} %bitcast.117, bf16[64,8192]{1,0:T(8,128)(2,1)S(1)} %copy-done, bf16[32,5,256,256]{3,2,1,0:T(8,128)(2,1)S(1)} %get-tuple-element.54.refs_2_, bf16[32,5,256,256]{3,2,1,0:T(8,128)(2,1)} %refs_3_.10), custom_call_target="tpu_custom_call", output_to_operand_aliasing={{1}: (2, {})} | custom-call | flops 350000000 | bytes 6000000 | tf_op jit(solution)/shard_map/pallas_call | solution.py:290
  23.3 3.1 %shard_map.106 = (f32[64,2048]{1,0:T(8,128)S(1)}, bf16[32,5,256,256]{3,2,1,0:T(8,128)(2,1)S(1)}) custom-call(s32[5,32]{1,0:T(8,128)S(1)} %bitcast.118, bf16[64,8192]{1,0:T(8,128)(2,1)S(1)} %copy-done, bf16[32,5,256,256]{3,2,1,0:T(8,128)(2,1)S(1)} %get-tuple-element.55.refs_2_, bf16[32,5,256,256]{3,2,1,0:T(8,128)(2,1)} %refs_3_.10), custom_call_target="tpu_custom_call", output_to_operand_aliasing={{1}: (2, {})} | custom-call | flops 350000000 | bytes 6000000 | tf_op jit(solution)/shard_map/pallas_call | solution.py:290
  26.7 2.3 %shard_map.107.refs_3_ = f32[64,2048]{1,0:T(8,128)S(1)} custom-call(s32[5,32]{1,0:T(8,128)S(1)} %bitcast.119, bf16[64,8192]{1,0:T(8,128)(2,1)S(1)} %copy-done, bf16[32,5,256,256]{3,2,1,0:T(8,128)(2,1)S(1)} %get-tuple-element.56.refs_2_.near.refs_8_), custom_call_target="tpu_custom_call" | custom-call | flops 350000000 | bytes 6000000 | tf_op jit(solution)/shard_map/pallas_call | solution.py:290
  32.4 2.9 %collective-permute-done.1 = f32[64,64]{1,0:T(8,128)S(1)} collective-permute-done((f32[64,64]{1,0:T(8,128)S(1)}, f32[64,64]{1,0:T(8,128)S(1)}, u32[]{:S(2)}, u32[]{:S(2)}) %collective-permute-start.1) | collective-permute-done | bytes 16416 | tf_op jit(solution)/shard_map/ppermute | solution.py:467
  35.9 3.5 %collective-permute-done.2 = f32[64,64]{1,0:T(8,128)S(1)} collective-permute-done((f32[64,64]{1,0:T(8,128)S(1)}, f32[64,64]{1,0:T(8,128)S(1)}, u32[]{:S(2)}, u32[]{:S(2)}) %collective-permute-start.2) | collective-permute-done | bytes 16416 | tf_op jit(solution)/shard_map/ppermute | solution.py:467
  41.3 3.5 %collective-permute-done.3 = f32[64,64]{1,0:T(8,128)S(1)} collective-permute-done((f32[64,64]{1,0:T(8,128)S(1)}, f32[64,64]{1,0:T(8,128)S(1)}, u32[]{:S(2)}, u32[]{:S(2)}) %collective-permute-start.3) | collective-permute-done | bytes 16416 | tf_op jit(solution)/shard_map/ppermute | solution.py:467
  45.5 4.6 %collective-permute-start.7 = (bf16[64,2048]{1,0:T(8,128)(2,1)S(1)}, bf16[64,2048]{1,0:T(8,128)(2,1)S(1)}, u32[]{:S(2)}, u32[]{:S(2)}) collective-permute-start(bf16[64,2048]{1,0:T(8,128)(2,1)S(1)} %get-tuple-element.52.sent_c), channel_id=1, source_target_pairs={{2,4},{6,8},{10,12},{14,16},{18,20},{22,24},{26,28},{30,32},{34,36... | collective-permute-start | bytes 786440 | tf_op jit(solution)/shard_map/ppermute | solution.py:473
  50.6 4.9 %collective-permute-done.5 = f32[64,64]{1,0:T(8,128)S(1)} collective-permute-done((f32[64,64]{1,0:T(8,128)S(1)}, f32[64,64]{1,0:T(8,128)S(1)}, u32[]{:S(2)}, u32[]{:S(2)}) %collective-permute-start.5) | collective-permute-done | bytes 16416 | tf_op jit(solution)/shard_map/ppermute | solution.py:467
  58.0 6.7 %shard_map.108 = (f32[64,8448]{1,0:T(8,128)S(1)}, bf16[96,64,128]{2,1,0:T(8,128)(2,1)S(1)}, bf16[64,8192]{1,0:T(8,128)(2,1)}, bf16[64,8192]{1,0:T(8,128)(2,1)S(1...) custom-call(s32[168]{0:T(256)S(1)} %get-tuple-element.42.plan.refs_0, ...), custom_call_target="tpu_custom_call", output_to_operand_aliasing={{0}: (9, {}), {1}: (10, {})} | custom-call | flops 600000000 | bytes 6000000 | tf_op jit(solution)/shard_map/pallas_call | solution.py:445
  64.7 5.1 %shard_map.109 = (f32[64,8448]{1,0:T(8,128)S(1)}, bf16[96,64,128]{2,1,0:T(8,128)(2,1)S(1)}, bf16[64,8192]{1,0:T(8,128)(2,1)}, bf16[64,8192]{1,0:T(8,128)(2,1)S(1...) custom-call(s32[168]{0:T(256)S(1)} %get-tuple-element.42.plan.refs_0, ...), custom_call_target="tpu_custom_call", output_to_operand_aliasing={{0}: (7, {}), {1}: (8, {}), {2}: (9, {}), {3}: (10, {}), {4... | custom-call | flops 600000000 | bytes 6000000 | tf_op jit(solution)/shard_map/pallas_call | solution.py:445
  72.1 2.3 %shard_map.112.refs_2_ = f32[64,2048]{1,0:T(8,128)S(1)} custom-call(s32[5,32]{1,0:T(8,128)S(1)} %bitcast.121, bf16[64,8192]{1,0:T(8,128)(2,1)S(1)} %get-tuple-element.78.refs_1_, bf16[32,5,256,256]{3,2,1,0:T(8,128)(2,1)S(1)} %get-tuple-element.56.refs_2_.near.refs_8_), custom_call_target="tpu_custom_call" | custom-call | flops 350000000 | bytes 6000000 | tf_op jit(solution)/shard_map/pallas_call | solution.py:290
  74.4 2.3 %shard_map.111.refs_1_ = f32[64,2048]{1,0:T(8,128)S(1)} custom-call(s32[5,32]{1,0:T(8,128)S(1)} %bitcast.122, bf16[64,8192]{1,0:T(8,128)(2,1)S(1)} %get-tuple-element.78.refs_1_, bf16[32,5,256,256]{3,2,1,0:T(8,128)(2,1)S(1)} %get-tuple-element.56.refs_2_.near.refs_8_), custom_call_target="tpu_custom_call" | custom-call | flops 350000000 | bytes 6000000 | tf_op jit(solution)/shard_map/pallas_call | solution.py:290
  79.3 4.8 %collective-permute-start.16 = (bf16[64,4096]{1,0:T(8,128)(2,1)S(1)}, bf16[64,4096]{1,0:T(8,128)(2,1)S(1)}, u32[]{:S(2)}, u32[]{:S(2)}) collective-permute-start(bf16[64,4096]{1,0:T(8,128)(2,1)S(1)} %get-tuple-element.75), channel_id=1, source_target_pairs={{2,4},{6,8},{10,12},{14,16},{18,20},{22,24},{26,28},{30,32},{34,36... | collective-permute-start | bytes 1572872 | tf_op jit(solution)/shard_map/ppermute | solution.py:473
  86.8 4.5 %collective-permute-done.11 = f32[64,64]{1,0:T(8,128)S(1)} collective-permute-done((f32[64,64]{1,0:T(8,128)S(1)}, f32[64,64]{1,0:T(8,128)S(1)}, u32[]{:S(2)}, u32[]{:S(2)}) %collective-permute-start.11) | collective-permute-done | bytes 16416 | tf_op jit(solution)/shard_map/ppermute | solution.py:467
  91.9 3.5 %collective-permute-done.12 = f32[64,64]{1,0:T(8,128)S(1)} collective-permute-done((f32[64,64]{1,0:T(8,128)S(1)}, f32[64,64]{1,0:T(8,128)S(1)}, u32[]{:S(2)}, u32[]{:S(2)}) %collective-permute-start.12) | collective-permute-done | bytes 16416 | tf_op jit(solution)/shard_map/ppermute | solution.py:467
  97.1 3.7 %collective-permute-done.13 = f32[64,64]{1,0:T(8,128)S(1)} collective-permute-done((f32[64,64]{1,0:T(8,128)S(1)}, f32[64,64]{1,0:T(8,128)S(1)}, u32[]{:S(2)}, u32[]{:S(2)}) %collective-permute-start.13) | collective-permute-done | bytes 16416 | tf_op jit(solution)/shard_map/ppermute | solution.py:467
  101.2 2.4 %collective-permute-start.14 = (f32[64,64]{1,0:T(8,128)S(1)}, f32[64,64]{1,0:T(8,128)S(1)}, u32[]{:S(2)}, u32[]{:S(2)}) collective-permute-start(f32[64,64]{1,0:T(8,128)S(1)} %convolution_add_fusion.1), channel_id=1, source_target_pairs={{0,32},{2,34},{4,36},{6,38},{8,40},{10,42},{12,44},{14,46},{16,48}... | collective-permute-start | bytes 49160 | tf_op jit(solution)/shard_map/ppermute | solution.py:467
  103.7 4.5 %collective-permute-start.17 = (bf16[64,2048]{1,0:T(8,128)(2,1)S(1)}, bf16[64,2048]{1,0:T(8,128)(2,1)S(1)}, u32[]{:S(2)}, u32[]{:S(2)}) collective-permute-start(bf16[64,2048]{1,0:T(8,128)(2,1)S(1)} %get-tuple-element.76.sent_c), channel_id=1, source_target_pairs={{2,4},{6,8},{10,12},{14,16},{18,20},{22,24},{26,28},{30,32},{34,36... | collective-permute-start | bytes 786440 | tf_op jit(solution)/shard_map/ppermute | solution.py:473
  108.7 4.9 %collective-permute-done.15 = f32[64,64]{1,0:T(8,128)S(1)} collective-permute-done((f32[64,64]{1,0:T(8,128)S(1)}, f32[64,64]{1,0:T(8,128)S(1)}, u32[]{:S(2)}, u32[]{:S(2)}) %collective-permute-start.15) | collective-permute-done | bytes 16416 | tf_op jit(solution)/shard_map/ppermute | solution.py:467
  116.2 9.6 %shard_map.114 = (f32[64,8448]{1,0:T(8,128)S(1)}, bf16[96,64,128]{2,1,0:T(8,128)(2,1)S(1)}, bf16[64,8192]{1,0:T(8,128)(2,1)}) custom-call(s32[168]{0:T(256)S(1)} %get-tuple-element.42.plan.refs_0_, s32[4,32]{1,0:T(4,128)S(1)} %bitcast.126, f32[64,64]{1,0:T(8,128)S(1)} %fusion.3.refs_2_, ...), custom_call_target="tpu_custom_call", output_to_operand_aliasing={{0}: (9, {}), {1}: (10, {})} | custom-call | flops 600000000 | bytes 6000000 | tf_op jit(solution)/shard_map/pallas_call | solution.py:445
  (77 shorter events, 25.8 us)
Async XLA Ops:
  0.6 12.0 %copy-start.4 = (s32[32,5]{0,1:T(8,128)S(1)}, s32[32,5]{0,1:T(8,128)}, u32[]{:S(2)}) copy-start(s32[32,5]{0,1:T(8,128)} %param.12) | copy-start | bytes 1924
  1.9 54.0 %collective-permute-start.8 = (bf16[64,4096]{1,0:T(8,128)(2,1)S(1)}, bf16[64,4096]{1,0:T(8,128)(2,1)S(1)}, u32[]{:S(2)}, u32[]{:S(2)}) collective-permute-start(bf16[64,4096]{1,0:T(8,128)(2,1)S(1)} %get-tuple-element.43.va), channel_id=1, source_target_pairs={{0,2},{2,0},{4,6},{6,4},{8,10},{10,8},{12,14},{14,12},{16,18},{18,... | collective-permute-start | bytes 1572872 | tf_op jit(solution)/shard_map/ppermute | solution.py:467
  3.4 54.6 %collective-permute-start.6 = (bf16[64,4096]{1,0:T(8,128)(2,1)S(1)}, bf16[64,4096]{1,0:T(8,128)(2,1)S(1)}, u32[]{:S(2)}, u32[]{:S(2)}) collective-permute-start(bf16[64,4096]{1,0:T(8,128)(2,1)S(1)} %get-tuple-element.44.vb), channel_id=1, source_target_pairs={{2,4},{6,8},{10,12},{14,16},{18,20},{22,24},{26,28},{30,32},{34,36... | collective-permute-start | bytes 1572872 | tf_op jit(solution)/shard_map/ppermute | solution.py:473
  12.5 17.3 %collective-permute-start = (f32[64,64]{1,0:T(8,128)S(1)}, f32[64,64]{1,0:T(8,128)S(1)}, u32[]{:S(2)}, u32[]{:S(2)}) collective-permute-start(f32[64,64]{1,0:T(8,128)S(1)} %get-tuple-element.46), channel_id=1, source_target_pairs={{0,2},{2,0},{4,6},{6,4},{8,10},{10,8},{12,14},{14,12},{16,18},{18,... | collective-permute-start | bytes 49160 | tf_op jit(solution)/shard_map/ppermute | solution.py:467
  12.7 4.4 %copy-start = (bf16[64,8192]{1,0:T(8,128)(2,1)S(1)}, bf16[64,8192]{1,0:T(8,128)(2,1)}, u32[]{:S(2)}) copy-start(bf16[64,8192]{1,0:T(8,128)(2,1)} %refs_1_.7) | copy-start | bytes 3145732
  30.1 5.2 %collective-permute-start.1 = (f32[64,64]{1,0:T(8,128)S(1)}, f32[64,64]{1,0:T(8,128)S(1)}, u32[]{:S(2)}, u32[]{:S(2)}) collective-permute-start(f32[64,64]{1,0:T(8,128)S(1)} %convolution_add_fusion.10), channel_id=1, source_target_pairs={{0,6},{2,4},{4,2},{6,0},{8,14},{10,12},{12,10},{14,8},{16,22},{18,... | collective-permute-start | bytes 49160 | tf_op jit(solution)/shard_map/ppermute | solution.py:467
  30.3 25.6 %collective-permute-start.9 = (bf16[64,2048]{1,0:T(8,128)(2,1)S(1)}, bf16[64,2048]{1,0:T(8,128)(2,1)S(1)}, u32[]{:S(2)}, u32[]{:S(2)}) collective-permute-start(bf16[64,2048]{1,0:T(8,128)(2,1)S(1)} %get-tuple-element.52.sent_c), channel_id=1, source_target_pairs={{0,2},{2,0},{4,6},{6,4},{8,10},{10,8},{12,14},{14,12},{16,18},{18,... | collective-permute-start | bytes 786440 | tf_op jit(solution)/shard_map/ppermute | solution.py:467
  35.4 4.0 %collective-permute-start.2 = (f32[64,64]{1,0:T(8,128)S(1)}, f32[64,64]{1,0:T(8,128)S(1)}, u32[]{:S(2)}, u32[]{:S(2)}) collective-permute-start(f32[64,64]{1,0:T(8,128)S(1)} %convolution_add_fusion.9), channel_id=1, source_target_pairs={{0,8},{2,10},{4,12},{6,14},{8,0},{10,2},{12,4},{14,6},{16,24},{18,... | collective-permute-start | bytes 49160 | tf_op jit(solution)/shard_map/ppermute | solution.py:467
  39.6 5.2 %collective-permute-start.3 = (f32[64,64]{1,0:T(8,128)S(1)}, f32[64,64]{1,0:T(8,128)S(1)}, u32[]{:S(2)}, u32[]{:S(2)}) collective-permute-start(f32[64,64]{1,0:T(8,128)S(1)} %convolution_add_fusion.8), channel_id=1, source_target_pairs={{0,24},{2,26},{4,28},{6,30},{8,16},{10,18},{12,20},{14,22},{16,8},... | collective-permute-start | bytes 49160 | tf_op jit(solution)/shard_map/ppermute | solution.py:467
  45.2 5.0 %collective-permute-start.4 = (f32[64,64]{1,0:T(8,128)S(1)}, f32[64,64]{1,0:T(8,128)S(1)}, u32[]{:S(2)}, u32[]{:S(2)}) collective-permute-start(f32[64,64]{1,0:T(8,128)S(1)} %convolution_add_fusion.7), channel_id=1, source_target_pairs={{0,32},{2,34},{4,36},{6,38},{8,40},{10,42},{12,44},{14,46},{16,48}... | collective-permute-start | bytes 49160 | tf_op jit(solution)/shard_map/ppermute | solution.py:467
  45.5 12.5 %collective-permute-start.7 = (bf16[64,2048]{1,0:T(8,128)(2,1)S(1)}, bf16[64,2048]{1,0:T(8,128)(2,1)S(1)}, u32[]{:S(2)}, u32[]{:S(2)}) collective-permute-start(bf16[64,2048]{1,0:T(8,128)(2,1)S(1)} %get-tuple-element.52.sent_c), channel_id=1, source_target_pairs={{2,4},{6,8},{10,12},{14,16},{18,20},{22,24},{26,28},{30,32},{34,36... | collective-permute-start | bytes 786440 | tf_op jit(solution)/shard_map/ppermute | solution.py:473
  50.3 5.2 %collective-permute-start.5 = (f32[64,64]{1,0:T(8,128)S(1)}, f32[64,64]{1,0:T(8,128)S(1)}, u32[]{:S(2)}, u32[]{:S(2)}) collective-permute-start(f32[64,64]{1,0:T(8,128)S(1)} %convolution_add_fusion.6), channel_id=1, source_target_pairs={{0,96},{2,98},{4,100},{6,102},{8,104},{10,106},{12,108},{14,110},{... | collective-permute-start | bytes 49160 | tf_op jit(solution)/shard_map/ppermute | solution.py:467
  55.9 2.1 %copy-start.1 = (bf16[32,4,64,64]{3,2,1,0:T(8,128)(2,1)S(1)}, bf16[32,4,64,64]{3,2,1,0:T(8,128)(2,1)}, u32[]{:S(2)}) copy-start(bf16[32,4,64,64]{3,2,1,0:T(8,128)(2,1)} %refs_5_.5) | copy-start | bytes 3145732
  55.9 2.1 %copy-start.2 = (bf16[32,64,256]{2,1,0:T(8,128)(2,1)S(1)}, bf16[32,64,256]{2,1,0:T(8,128)(2,1)}, u32[]{:S(2)}) copy-start(bf16[32,64,256]{2,1,0:T(8,128)(2,1)} %refs_3_.13) | copy-start | bytes 3145732
  76.7 7.4 %collective-permute-start.10 = (f32[64,64]{1,0:T(8,128)S(1)}, f32[64,64]{1,0:T(8,128)S(1)}, u32[]{:S(2)}, u32[]{:S(2)}) collective-permute-start(f32[64,64]{1,0:T(8,128)S(1)} %get-tuple-element.71), channel_id=1, source_target_pairs={{0,2},{2,0},{4,6},{6,4},{8,10},{10,8},{12,14},{14,12},{16,18},{18,... | collective-permute-start | bytes 49160 | tf_op jit(solution)/shard_map/ppermute | solution.py:467
  79.3 36.9 %collective-permute-start.16 = (bf16[64,4096]{1,0:T(8,128)(2,1)S(1)}, bf16[64,4096]{1,0:T(8,128)(2,1)S(1)}, u32[]{:S(2)}, u32[]{:S(2)}) collective-permute-start(bf16[64,4096]{1,0:T(8,128)(2,1)S(1)} %get-tuple-element.75), channel_id=1, source_target_pairs={{2,4},{6,8},{10,12},{14,16},{18,20},{22,24},{26,28},{30,32},{34,36... | collective-permute-start | bytes 1572872 | tf_op jit(solution)/shard_map/ppermute | solution.py:473
  84.4 6.8 %collective-permute-start.11 = (f32[64,64]{1,0:T(8,128)S(1)}, f32[64,64]{1,0:T(8,128)S(1)}, u32[]{:S(2)}, u32[]{:S(2)}) collective-permute-start(f32[64,64]{1,0:T(8,128)S(1)} %convolution_add_fusion.4), channel_id=1, source_target_pairs={{0,6},{2,4},{4,2},{6,0},{8,14},{10,12},{12,10},{14,8},{16,22},{18,... | collective-permute-start | bytes 49160 | tf_op jit(solution)/shard_map/ppermute | solution.py:467
  84.7 29.3 %collective-permute-start.18 = (bf16[64,4096]{1,0:T(8,128)(2,1)S(1)}, bf16[64,4096]{1,0:T(8,128)(2,1)S(1)}, u32[]{:S(2)}, u32[]{:S(2)}) collective-permute-start(bf16[64,4096]{1,0:T(8,128)(2,1)S(1)} %get-tuple-element.77), channel_id=1, source_target_pairs={{0,2},{2,0},{4,6},{6,4},{8,10},{10,8},{12,14},{14,12},{16,18},{18,... | collective-permute-start | bytes 1572872 | tf_op jit(solution)/shard_map/ppermute | solution.py:467
  85.7 28.3 %collective-permute-start.19 = (bf16[64,2048]{1,0:T(8,128)(2,1)S(1)}, bf16[64,2048]{1,0:T(8,128)(2,1)S(1)}, u32[]{:S(2)}, u32[]{:S(2)}) collective-permute-start(bf16[64,2048]{1,0:T(8,128)(2,1)S(1)} %get-tuple-element.76.sent_c), channel_id=1, source_target_pairs={{0,2},{2,0},{4,6},{6,4},{8,10},{10,8},{12,14},{14,12},{16,18},{18,... | collective-permute-start | bytes 786440 | tf_op jit(solution)/shard_map/ppermute | solution.py:467
  91.4 4.0 %collective-permute-start.12 = (f32[64,64]{1,0:T(8,128)S(1)}, f32[64,64]{1,0:T(8,128)S(1)}, u32[]{:S(2)}, u32[]{:S(2)}) collective-permute-start(f32[64,64]{1,0:T(8,128)S(1)} %convolution_add_fusion.3), channel_id=1, source_target_pairs={{0,8},{2,10},{4,12},{6,14},{8,0},{10,2},{12,4},{14,6},{16,24},{18,... | collective-permute-start | bytes 49160 | tf_op jit(solution)/shard_map/ppermute | solution.py:467
  95.6 5.2 %collective-permute-start.13 = (f32[64,64]{1,0:T(8,128)S(1)}, f32[64,64]{1,0:T(8,128)S(1)}, u32[]{:S(2)}, u32[]{:S(2)}) collective-permute-start(f32[64,64]{1,0:T(8,128)S(1)} %convolution_add_fusion.2), channel_id=1, source_target_pairs={{0,24},{2,26},{4,28},{6,30},{8,16},{10,18},{12,20},{14,22},{16,8},... | collective-permute-start | bytes 49160 | tf_op jit(solution)/shard_map/ppermute | solution.py:467
  101.2 7.1 %collective-permute-start.14 = (f32[64,64]{1,0:T(8,128)S(1)}, f32[64,64]{1,0:T(8,128)S(1)}, u32[]{:S(2)}, u32[]{:S(2)}) collective-permute-start(f32[64,64]{1,0:T(8,128)S(1)} %convolution_add_fusion.1), channel_id=1, source_target_pairs={{0,32},{2,34},{4,36},{6,38},{8,40},{10,42},{12,44},{14,46},{16,48}... | collective-permute-start | bytes 49160 | tf_op jit(solution)/shard_map/ppermute | solution.py:467
  103.7 12.5 %collective-permute-start.17 = (bf16[64,2048]{1,0:T(8,128)(2,1)S(1)}, bf16[64,2048]{1,0:T(8,128)(2,1)S(1)}, u32[]{:S(2)}, u32[]{:S(2)}) collective-permute-start(bf16[64,2048]{1,0:T(8,128)(2,1)S(1)} %get-tuple-element.76.sent_c), channel_id=1, source_target_pairs={{2,4},{6,8},{10,12},{14,16},{18,20},{22,24},{26,28},{30,32},{34,36... | collective-permute-start | bytes 786440 | tf_op jit(solution)/shard_map/ppermute | solution.py:473
  108.4 5.2 %collective-permute-start.15 = (f32[64,64]{1,0:T(8,128)S(1)}, f32[64,64]{1,0:T(8,128)S(1)}, u32[]{:S(2)}, u32[]{:S(2)}) collective-permute-start(f32[64,64]{1,0:T(8,128)S(1)} %convolution_add_fusion), channel_id=1, source_target_pairs={{0,96},{2,98},{4,100},{6,102},{8,104},{10,106},{12,108},{14,110},{... | collective-permute-start | bytes 49160 | tf_op jit(solution)/shard_map/ppermute | solution.py:467
  (2 other events, 4.1 us)

commit v6 on v5

--- a/solution.py
+++ b/solution.py
@@ -484,13 +484,10 @@
         fill(t)
         up, down = tables(t)
         if t == 0:
-            va, coef, other = lax.optimization_barrier((va, coef, other))
             if got_va is None:
                 got_va = swapped(va, 1)
             got_ca = swapped(coef, 1)
-        if t == 3:
-            later, other = lax.optimization_barrier((coef, other))
-            got_cb = swapped_odd(later)
+            got_cb = swapped_odd(coef)
         if t + 1 < levels:
             node = exact(node, up[0, t]) + exact(other, up[1, t])
         others.append(other)
@@ -534,7 +531,7 @@
         return made["up"], made.get("down")
 
     def fill_second(t):
-        for piece in {1: (0, 1), 4: (2, 3)}.get(t, ()):
+        for piece in {1: (0, 1), 2: (2,), 3: (3,)}.get(t, ()):
             (out,) = near_piece(piece, near_list_t, made["own_v"], near_blocks, made["kept"], False)
             again.append(out)
 

time: 128 us -> 137 us (1.070)
  the two profiles are of different devices: /device:TPU:96 before, /device:TPU:24 now
where the time goes in v6:
time: 137 us
  Pallas kernels  55.5 us (41%)
  starting transfers between devices  37.6 us (27%)
  waiting for transfers between devices  37 us (27%)
  matrix products  5.45 us (4%)
  between operations  1.38 us (1%)
    ppermute x16, waiting for transfers between devices, swapped(): lax.ppermute(value, 'leaf', [(i, i ^ mask) for i in range(lax.axis_size('...  37 us
    ppermute x16, starting transfers between devices, swapped(): lax.ppermute(value, 'leaf', [(i, i ^ mask) for i in range(lax.axis_size('...  23.8 us
    pallas_call x3, Pallas kernels, tail(): pl.pallas_call(lambda *refs: tail_body(names, sides, more, *refs), grid_s...  21.3 us
    pallas_call x8, Pallas kernels, near_piece(): pl.pallas_call(lambda *refs: near_body(piece, load, *refs), grid_spec=plt...  20.9 us
    ppermute x4, starting transfers between devices, swapped_odd(): return lax.ppermute(value, 'leaf', pairs + [(j, i) for i, j in pairs])  13.8 us
    dot_general x32, matrix products, exact(): lax.dot_general(a, b, dims, precision=lax.Precision.HIGHEST, preferred_el...  5.45 us
    pallas_call x1, Pallas kernels, table(): pl.pallas_call(lambda *refs: table_body(levels, *refs), grid_spec=pltpu.P...  4.37 us
    pallas_call x2, Pallas kernels, side_a(): pl.pallas_call(side_body, grid_spec=pltpu.PrefetchScalarGridSpec(num_scal...  4.01 us
  transfers between devices with their start and end apart: 20, of which 10 were waited for; matrix products, arithmetic and copies ran while one was open for 4% of the time, Pallas kernels for 19%

profile of v6, /device:TPU:24, one launch (start us, length us, event | category | flops | bytes accessed | tf_op | source)
XLA Modules:
  0.0 137.0 jit_solution(925839356017757731)
XLA Ops:
  3.4 2.8 %head.1 = (bf16[64,2048]{1,0:T(8,128)(2,1)S(1)}, f32[64,64]{1,0:T(8,128)S(1)}) custom-call(bf16[64,4096]{1,0:T(8,128)(2,1)S(1)} %get-tuple-element.34.va, bf16[64,4096]{1,0:T(8,128)(2,1)S(1)} %get-tuple-element.35.vb, bf16[32,64,256]{2,1,0:T(8,128)(2,1)} %refs_3_.13, bf16[2048,64]{1,0:T(8,128)(2,1)} %bitcast.111), custom_call_target="tpu_custom_call" | custom-call | flops 200000000 | bytes 6000000 | tf_op jit(solution)/shard_map/head/pallas_call | solution.py:115
  6.9 4.8 %collective-permute-start.7 = (bf16[64,2048]{1,0:T(8,128)(2,1)S(1)}, bf16[64,2048]{1,0:T(8,128)(2,1)S(1)}, u32[]{:S(2)}, u32[]{:S(2)}) collective-permute-start(bf16[64,2048]{1,0:T(8,128)(2,1)S(1)} %get-tuple-element.39.sent_c), channel_id=1, source_target_pairs={{2,4},{6,8},{10,12},{14,16},{18,20},{22,24},{26,28},{30,32},{34,36... | collective-permute-start | bytes 786440 | tf_op jit(solution)/shard_map/ppermute | solution.py:473
  11.7 3.1 %collective-permute-start.6 = (bf16[64,4096]{1,0:T(8,128)(2,1)S(1)}, bf16[64,4096]{1,0:T(8,128)(2,1)S(1)}, u32[]{:S(2)}, u32[]{:S(2)}) collective-permute-start(bf16[64,4096]{1,0:T(8,128)(2,1)S(1)} %get-tuple-element.35.vb), channel_id=1, source_target_pairs={{2,4},{6,8},{10,12},{14,16},{18,20},{22,24},{26,28},{30,32},{34,36... | collective-permute-start | bytes 1572872 | tf_op jit(solution)/shard_map/ppermute | solution.py:473
  14.9 4.4 %table.1 = (f32[2,6,64,64]{3,2,1,0:T(8,128)S(1)}, f32[6,64,64]{2,1,0:T(8,128)S(1)}, s32[168]{0:T(256)S(1)}, bf16[32,5,256,256]{3,2,1,0:T(8,128)(2,1)S(1)}) custom-call(s32[5,32]{1,0:T(8,128)S(1)} %bitcast.115, bf16[64,64,126]{2,1,0:T(8,128)(2,1)} %bitcast.127, bf16[64,64,126]{2,1,0:T(8,128)(2,1)} %bitcast.128, bf16[32,5,256,256]{3,2,1,0:T(8,128)(2,1)} %refs_3_.10), custom_call_target="tpu_custom_call" | custom-call | flops 10000000 | bytes 8000000 | tf_op jit(solution)/shard_map/table/pallas_call | solution.py:227
  19.3 3.1 %shard_map.104 = (f32[64,2048]{1,0:T(8,128)S(1)}, bf16[32,5,256,256]{3,2,1,0:T(8,128)(2,1)S(1)}) custom-call(s32[5,32]{1,0:T(8,128)S(1)} %bitcast.116, bf16[64,8192]{1,0:T(8,128)(2,1)S(1)} %copy-done, bf16[32,5,256,256]{3,2,1,0:T(8,128)(2,1)S(1)} %get-tuple-element.40.refs_2_, bf16[32,5,256,256]{3,2,1,0:T(8,128)(2,1)} %refs_3_.10), custom_call_target="tpu_custom_call", output_to_operand_aliasing={{1}: (2, {})} | custom-call | flops 350000000 | bytes 6000000 | tf_op jit(solution)/shard_map/pallas_call | solution.py:290
  22.5 3.1 %shard_map.105 = (f32[64,2048]{1,0:T(8,128)S(1)}, bf16[32,5,256,256]{3,2,1,0:T(8,128)(2,1)S(1)}) custom-call(s32[5,32]{1,0:T(8,128)S(1)} %bitcast.117, bf16[64,8192]{1,0:T(8,128)(2,1)S(1)} %copy-done, bf16[32,5,256,256]{3,2,1,0:T(8,128)(2,1)S(1)} %get-tuple-element.41.refs_2_, bf16[32,5,256,256]{3,2,1,0:T(8,128)(2,1)} %refs_3_.10), custom_call_target="tpu_custom_call", output_to_operand_aliasing={{1}: (2, {})} | custom-call | flops 350000000 | bytes 6000000 | tf_op jit(solution)/shard_map/pallas_call | solution.py:290
  25.6 3.1 %shard_map.106 = (f32[64,2048]{1,0:T(8,128)S(1)}, bf16[32,5,256,256]{3,2,1,0:T(8,128)(2,1)S(1)}) custom-call(s32[5,32]{1,0:T(8,128)S(1)} %bitcast.118, bf16[64,8192]{1,0:T(8,128)(2,1)S(1)} %copy-done, bf16[32,5,256,256]{3,2,1,0:T(8,128)(2,1)S(1)} %get-tuple-element.42.refs_2_, bf16[32,5,256,256]{3,2,1,0:T(8,128)(2,1)} %refs_3_.10), custom_call_target="tpu_custom_call", output_to_operand_aliasing={{1}: (2, {})} | custom-call | flops 350000000 | bytes 6000000 | tf_op jit(solution)/shard_map/pallas_call | solution.py:290
  32.3 5.0 %collective-permute-start.1 = (f32[64,64]{1,0:T(8,128)S(1)}, f32[64,64]{1,0:T(8,128)S(1)}, u32[]{:S(2)}, u32[]{:S(2)}) collective-permute-start(f32[64,64]{1,0:T(8,128)S(1)} %convolution_add_fusion.10), channel_id=1, source_target_pairs={{0,6},{2,4},{4,2},{6,0},{8,14},{10,12},{12,10},{14,8},{16,22},{18,... | collective-permute-start | bytes 49160 | tf_op jit(solution)/shard_map/ppermute | solution.py:467
  39.8 3.5 %collective-permute-done.2 = f32[64,64]{1,0:T(8,128)S(1)} collective-permute-done((f32[64,64]{1,0:T(8,128)S(1)}, f32[64,64]{1,0:T(8,128)S(1)}, u32[]{:S(2)}, u32[]{:S(2)}) %collective-permute-start.2) | collective-permute-done | bytes 16416 | tf_op jit(solution)/shard_map/ppermute | solution.py:467
  44.0 4.8 %collective-permute-done.3 = f32[64,64]{1,0:T(8,128)S(1)} collective-permute-done((f32[64,64]{1,0:T(8,128)S(1)}, f32[64,64]{1,0:T(8,128)S(1)}, u32[]{:S(2)}, u32[]{:S(2)}) %collective-permute-start.3) | collective-permute-done | bytes 16416 | tf_op jit(solution)/shard_map/ppermute | solution.py:467
  53.0 2.5 %collective-permute-start.5 = (f32[64,64]{1,0:T(8,128)S(1)}, f32[64,64]{1,0:T(8,128)S(1)}, u32[]{:S(2)}, u32[]{:S(2)}) collective-permute-start(f32[64,64]{1,0:T(8,128)S(1)} %convolution_add_fusion.6), channel_id=1, source_target_pairs={{0,96},{2,98},{4,100},{6,102},{8,104},{10,106},{12,108},{14,110},{... | collective-permute-start | bytes 49160 | tf_op jit(solution)/shard_map/ppermute | solution.py:467
  55.7 2.5 %collective-permute-done.5 = f32[64,64]{1,0:T(8,128)S(1)} collective-permute-done((f32[64,64]{1,0:T(8,128)S(1)}, f32[64,64]{1,0:T(8,128)S(1)}, u32[]{:S(2)}, u32[]{:S(2)}) %collective-permute-start.5) | collective-permute-done | bytes 16416 | tf_op jit(solution)/shard_map/ppermute | solution.py:467
  60.8 6.7 %shard_map.108 = (f32[64,8448]{1,0:T(8,128)S(1)}, bf16[96,64,128]{2,1,0:T(8,128)(2,1)S(1)}, bf16[64,8192]{1,0:T(8,128)(2,1)}, bf16[64,8192]{1,0:T(8,128)(2,1)S(1...) custom-call(s32[168]{0:T(256)S(1)} %get-tuple-element.33.plan.refs_0, ...), custom_call_target="tpu_custom_call", output_to_operand_aliasing={{0}: (9, {}), {1}: (10, {})} | custom-call | flops 600000000 | bytes 6000000 | tf_op jit(solution)/shard_map/pallas_call | solution.py:445
  67.5 5.1 %shard_map.109 = (f32[64,8448]{1,0:T(8,128)S(1)}, bf16[96,64,128]{2,1,0:T(8,128)(2,1)S(1)}, bf16[64,8192]{1,0:T(8,128)(2,1)}, bf16[64,8192]{1,0:T(8,128)(2,1)S(1...) custom-call(s32[168]{0:T(256)S(1)} %get-tuple-element.33.plan.refs_0, ...), custom_call_target="tpu_custom_call", output_to_operand_aliasing={{0}: (7, {}), {1}: (8, {}), {2}: (9, {}), {3}: (10, {}), {4... | custom-call | flops 600000000 | bytes 6000000 | tf_op jit(solution)/shard_map/pallas_call | solution.py:445
  77.2 2.3 %shard_map.111.refs_1_ = f32[64,2048]{1,0:T(8,128)S(1)} custom-call(s32[5,32]{1,0:T(8,128)S(1)} %bitcast.122, bf16[64,8192]{1,0:T(8,128)(2,1)S(1)} %get-tuple-element.60.refs_1_, bf16[32,5,256,256]{3,2,1,0:T(8,128)(2,1)S(1)} %get-tuple-element.43.refs_2_.near.refs_8_), custom_call_target="tpu_custom_call" | custom-call | flops 350000000 | bytes 6000000 | tf_op jit(solution)/shard_map/pallas_call | solution.py:290
  83.9 3.3 %collective-permute-start.17 = (bf16[64,2048]{1,0:T(8,128)(2,1)S(1)}, bf16[64,2048]{1,0:T(8,128)(2,1)S(1)}, u32[]{:S(2)}, u32[]{:S(2)}) collective-permute-start(bf16[64,2048]{1,0:T(8,128)(2,1)S(1)} %get-tuple-element.58.sent_c), channel_id=1, source_target_pairs={{2,4},{6,8},{10,12},{14,16},{18,20},{22,24},{26,28},{30,32},{34,36... | collective-permute-start | bytes 786440 | tf_op jit(solution)/shard_map/ppermute | solution.py:473
  89.5 2.5 %collective-permute-start.16 = (bf16[64,4096]{1,0:T(8,128)(2,1)S(1)}, bf16[64,4096]{1,0:T(8,128)(2,1)S(1)}, u32[]{:S(2)}, u32[]{:S(2)}) collective-permute-start(bf16[64,4096]{1,0:T(8,128)(2,1)S(1)} %get-tuple-element.57), channel_id=1, source_target_pairs={{2,4},{6,8},{10,12},{14,16},{18,20},{22,24},{26,28},{30,32},{34,36... | collective-permute-start | bytes 1572872 | tf_op jit(solution)/shard_map/ppermute | solution.py:473
  92.3 6.3 %collective-permute-start.11 = (f32[64,64]{1,0:T(8,128)S(1)}, f32[64,64]{1,0:T(8,128)S(1)}, u32[]{:S(2)}, u32[]{:S(2)}) collective-permute-start(f32[64,64]{1,0:T(8,128)S(1)} %convolution_add_fusion.4), channel_id=1, source_target_pairs={{0,6},{2,4},{4,2},{6,0},{8,14},{10,12},{12,10},{14,8},{16,22},{18,... | collective-permute-start | bytes 49160 | tf_op jit(solution)/shard_map/ppermute | solution.py:467
  98.8 7.0 %collective-permute-done.11 = f32[64,64]{1,0:T(8,128)S(1)} collective-permute-done((f32[64,64]{1,0:T(8,128)S(1)}, f32[64,64]{1,0:T(8,128)S(1)}, u32[]{:S(2)}, u32[]{:S(2)}) %collective-permute-start.11) | collective-permute-done | bytes 16416 | tf_op jit(solution)/shard_map/ppermute | solution.py:467
  106.4 3.5 %collective-permute-done.12 = f32[64,64]{1,0:T(8,128)S(1)} collective-permute-done((f32[64,64]{1,0:T(8,128)S(1)}, f32[64,64]{1,0:T(8,128)S(1)}, u32[]{:S(2)}, u32[]{:S(2)}) %collective-permute-start.12) | collective-permute-done | bytes 16416 | tf_op jit(solution)/shard_map/ppermute | solution.py:467
  110.6 4.8 %collective-permute-done.13 = f32[64,64]{1,0:T(8,128)S(1)} collective-permute-done((f32[64,64]{1,0:T(8,128)S(1)}, f32[64,64]{1,0:T(8,128)S(1)}, u32[]{:S(2)}, u32[]{:S(2)}) %collective-permute-start.13) | collective-permute-done | bytes 16416 | tf_op jit(solution)/shard_map/ppermute | solution.py:467
  116.2 3.3 %collective-permute-done.14 = f32[64,64]{1,0:T(8,128)S(1)} collective-permute-done((f32[64,64]{1,0:T(8,128)S(1)}, f32[64,64]{1,0:T(8,128)S(1)}, u32[]{:S(2)}, u32[]{:S(2)}) %collective-permute-start.14) | collective-permute-done | bytes 16416 | tf_op jit(solution)/shard_map/ppermute | solution.py:467
  120.6 4.3 %collective-permute-done.15 = f32[64,64]{1,0:T(8,128)S(1)} collective-permute-done((f32[64,64]{1,0:T(8,128)S(1)}, f32[64,64]{1,0:T(8,128)S(1)}, u32[]{:S(2)}, u32[]{:S(2)}) %collective-permute-start.15) | collective-permute-done | bytes 16416 | tf_op jit(solution)/shard_map/ppermute | solution.py:467
  127.3 9.5 %shard_map.114 = (f32[64,8448]{1,0:T(8,128)S(1)}, bf16[96,64,128]{2,1,0:T(8,128)(2,1)S(1)}, bf16[64,8192]{1,0:T(8,128)(2,1)}) custom-call(s32[168]{0:T(256)S(1)} %get-tuple-element.33.plan.refs_0_, s32[4,32]{1,0:T(4,128)S(1)} %bitcast.126, f32[64,64]{1,0:T(8,128)S(1)} %fusion.3.refs_2_, ...), custom_call_target="tpu_custom_call", output_to_operand_aliasing={{0}: (9, {}), {1}: (10, {})} | custom-call | flops 600000000 | bytes 6000000 | tf_op jit(solution)/shard_map/pallas_call | solution.py:445
  (77 shorter events, 34.3 us)
Async XLA Ops:
  0.6 14.3 %copy-start.4 = (s32[32,5]{0,1:T(8,128)S(1)}, s32[32,5]{0,1:T(8,128)}, u32[]{:S(2)}) copy-start(s32[32,5]{0,1:T(8,128)} %param.12) | copy-start | bytes 1924
  1.9 56.8 %collective-permute-start.8 = (bf16[64,4096]{1,0:T(8,128)(2,1)S(1)}, bf16[64,4096]{1,0:T(8,128)(2,1)S(1)}, u32[]{:S(2)}, u32[]{:S(2)}) collective-permute-start(bf16[64,4096]{1,0:T(8,128)(2,1)S(1)} %get-tuple-element.34.va), channel_id=1, source_target_pairs={{0,2},{2,0},{4,6},{6,4},{8,10},{10,8},{12,14},{14,12},{16,18},{18,... | collective-permute-start | bytes 1572872 | tf_op jit(solution)/shard_map/ppermute | solution.py:467
  6.3 52.4 %collective-permute-start.9 = (bf16[64,2048]{1,0:T(8,128)(2,1)S(1)}, bf16[64,2048]{1,0:T(8,128)(2,1)S(1)}, u32[]{:S(2)}, u32[]{:S(2)}) collective-permute-start(bf16[64,2048]{1,0:T(8,128)(2,1)S(1)} %get-tuple-element.39.sent_c), channel_id=1, source_target_pairs={{0,2},{2,0},{4,6},{6,4},{8,10},{10,8},{12,14},{14,12},{16,18},{18,... | collective-permute-start | bytes 786440 | tf_op jit(solution)/shard_map/ppermute | solution.py:467
  6.9 53.9 %collective-permute-start.7 = (bf16[64,2048]{1,0:T(8,128)(2,1)S(1)}, bf16[64,2048]{1,0:T(8,128)(2,1)S(1)}, u32[]{:S(2)}, u32[]{:S(2)}) collective-permute-start(bf16[64,2048]{1,0:T(8,128)(2,1)S(1)} %get-tuple-element.39.sent_c), channel_id=1, source_target_pairs={{2,4},{6,8},{10,12},{14,16},{18,20},{22,24},{26,28},{30,32},{34,36... | collective-permute-start | bytes 786440 | tf_op jit(solution)/shard_map/ppermute | solution.py:473
  11.7 49.0 %collective-permute-start.6 = (bf16[64,4096]{1,0:T(8,128)(2,1)S(1)}, bf16[64,4096]{1,0:T(8,128)(2,1)S(1)}, u32[]{:S(2)}, u32[]{:S(2)}) collective-permute-start(bf16[64,4096]{1,0:T(8,128)(2,1)S(1)} %get-tuple-element.35.vb), channel_id=1, source_target_pairs={{2,4},{6,8},{10,12},{14,16},{18,20},{22,24},{26,28},{30,32},{34,36... | collective-permute-start | bytes 1572872 | tf_op jit(solution)/shard_map/ppermute | solution.py:473
  14.8 17.3 %collective-permute-start = (f32[64,64]{1,0:T(8,128)S(1)}, f32[64,64]{1,0:T(8,128)S(1)}, u32[]{:S(2)}, u32[]{:S(2)}) collective-permute-start(f32[64,64]{1,0:T(8,128)S(1)} %get-tuple-element.36), channel_id=1, source_target_pairs={{0,2},{2,0},{4,6},{6,4},{8,10},{10,8},{12,14},{14,12},{16,18},{18,... | collective-permute-start | bytes 49160 | tf_op jit(solution)/shard_map/ppermute | solution.py:467
  14.9 4.4 %copy-start = (bf16[64,8192]{1,0:T(8,128)(2,1)S(1)}, bf16[64,8192]{1,0:T(8,128)(2,1)}, u32[]{:S(2)}) copy-start(bf16[64,8192]{1,0:T(8,128)(2,1)} %refs_1_.7) | copy-start | bytes 3145732
  32.3 6.8 %collective-permute-start.1 = (f32[64,64]{1,0:T(8,128)S(1)}, f32[64,64]{1,0:T(8,128)S(1)}, u32[]{:S(2)}, u32[]{:S(2)}) collective-permute-start(f32[64,64]{1,0:T(8,128)S(1)} %convolution_add_fusion.10), channel_id=1, source_target_pairs={{0,6},{2,4},{4,2},{6,0},{8,14},{10,12},{12,10},{14,8},{16,22},{18,... | collective-permute-start | bytes 49160 | tf_op jit(solution)/shard_map/ppermute | solution.py:467
  39.3 4.0 %collective-permute-start.2 = (f32[64,64]{1,0:T(8,128)S(1)}, f32[64,64]{1,0:T(8,128)S(1)}, u32[]{:S(2)}, u32[]{:S(2)}) collective-permute-start(f32[64,64]{1,0:T(8,128)S(1)} %convolution_add_fusion.9), channel_id=1, source_target_pairs={{0,8},{2,10},{4,12},{6,14},{8,0},{10,2},{12,4},{14,6},{16,24},{18,... | collective-permute-start | bytes 49160 | tf_op jit(solution)/shard_map/ppermute | solution.py:467
  43.5 5.2 %collective-permute-start.3 = (f32[64,64]{1,0:T(8,128)S(1)}, f32[64,64]{1,0:T(8,128)S(1)}, u32[]{:S(2)}, u32[]{:S(2)}) collective-permute-start(f32[64,64]{1,0:T(8,128)S(1)} %convolution_add_fusion.8), channel_id=1, source_target_pairs={{0,24},{2,26},{4,28},{6,30},{8,16},{10,18},{12,20},{14,22},{16,8},... | collective-permute-start | bytes 49160 | tf_op jit(solution)/shard_map/ppermute | solution.py:467
  48.9 4.0 %collective-permute-start.4 = (f32[64,64]{1,0:T(8,128)S(1)}, f32[64,64]{1,0:T(8,128)S(1)}, u32[]{:S(2)}, u32[]{:S(2)}) collective-permute-start(f32[64,64]{1,0:T(8,128)S(1)} %convolution_add_fusion.7), channel_id=1, source_target_pairs={{0,32},{2,34},{4,36},{6,38},{8,40},{10,42},{12,44},{14,46},{16,48}... | collective-permute-start | bytes 49160 | tf_op jit(solution)/shard_map/ppermute | solution.py:467
  53.0 5.2 %collective-permute-start.5 = (f32[64,64]{1,0:T(8,128)S(1)}, f32[64,64]{1,0:T(8,128)S(1)}, u32[]{:S(2)}, u32[]{:S(2)}) collective-permute-start(f32[64,64]{1,0:T(8,128)S(1)} %convolution_add_fusion.6), channel_id=1, source_target_pairs={{0,96},{2,98},{4,100},{6,102},{8,104},{10,106},{12,108},{14,110},{... | collective-permute-start | bytes 49160 | tf_op jit(solution)/shard_map/ppermute | solution.py:467
  58.7 2.1 %copy-start.1 = (bf16[32,4,64,64]{3,2,1,0:T(8,128)(2,1)S(1)}, bf16[32,4,64,64]{3,2,1,0:T(8,128)(2,1)}, u32[]{:S(2)}) copy-start(bf16[32,4,64,64]{3,2,1,0:T(8,128)(2,1)} %refs_5_.5) | copy-start | bytes 3145732
  58.7 2.1 %copy-start.2 = (bf16[32,64,256]{2,1,0:T(8,128)(2,1)S(1)}, bf16[32,64,256]{2,1,0:T(8,128)(2,1)}, u32[]{:S(2)}) copy-start(bf16[32,64,256]{2,1,0:T(8,128)(2,1)} %refs_3_.13) | copy-start | bytes 3145732
  79.5 12.5 %collective-permute-start.10 = (f32[64,64]{1,0:T(8,128)S(1)}, f32[64,64]{1,0:T(8,128)S(1)}, u32[]{:S(2)}, u32[]{:S(2)}) collective-permute-start(f32[64,64]{1,0:T(8,128)S(1)} %get-tuple-element.56), channel_id=1, source_target_pairs={{0,2},{2,0},{4,6},{6,4},{8,10},{10,8},{12,14},{14,12},{16,18},{18,... | collective-permute-start | bytes 49160 | tf_op jit(solution)/shard_map/ppermute | solution.py:467
  83.2 42.1 %collective-permute-start.19 = (bf16[64,2048]{1,0:T(8,128)(2,1)S(1)}, bf16[64,2048]{1,0:T(8,128)(2,1)S(1)}, u32[]{:S(2)}, u32[]{:S(2)}) collective-permute-start(bf16[64,2048]{1,0:T(8,128)(2,1)S(1)} %get-tuple-element.58.sent_c), channel_id=1, source_target_pairs={{0,2},{2,0},{4,6},{6,4},{8,10},{10,8},{12,14},{14,12},{16,18},{18,... | collective-permute-start | bytes 786440 | tf_op jit(solution)/shard_map/ppermute | solution.py:467
  83.9 43.4 %collective-permute-start.17 = (bf16[64,2048]{1,0:T(8,128)(2,1)S(1)}, bf16[64,2048]{1,0:T(8,128)(2,1)S(1)}, u32[]{:S(2)}, u32[]{:S(2)}) collective-permute-start(bf16[64,2048]{1,0:T(8,128)(2,1)S(1)} %get-tuple-element.58.sent_c), channel_id=1, source_target_pairs={{2,4},{6,8},{10,12},{14,16},{18,20},{22,24},{26,28},{30,32},{34,36... | collective-permute-start | bytes 786440 | tf_op jit(solution)/shard_map/ppermute | solution.py:473
  87.3 38.0 %collective-permute-start.18 = (bf16[64,4096]{1,0:T(8,128)(2,1)S(1)}, bf16[64,4096]{1,0:T(8,128)(2,1)S(1)}, u32[]{:S(2)}, u32[]{:S(2)}) collective-permute-start(bf16[64,4096]{1,0:T(8,128)(2,1)S(1)} %get-tuple-element.59), channel_id=1, source_target_pairs={{0,2},{2,0},{4,6},{6,4},{8,10},{10,8},{12,14},{14,12},{16,18},{18,... | collective-permute-start | bytes 1572872 | tf_op jit(solution)/shard_map/ppermute | solution.py:467
  89.5 37.8 %collective-permute-start.16 = (bf16[64,4096]{1,0:T(8,128)(2,1)S(1)}, bf16[64,4096]{1,0:T(8,128)(2,1)S(1)}, u32[]{:S(2)}, u32[]{:S(2)}) collective-permute-start(bf16[64,4096]{1,0:T(8,128)(2,1)S(1)} %get-tuple-element.57), channel_id=1, source_target_pairs={{2,4},{6,8},{10,12},{14,16},{18,20},{22,24},{26,28},{30,32},{34,36... | collective-permute-start | bytes 1572872 | tf_op jit(solution)/shard_map/ppermute | solution.py:473
  92.3 13.5 %collective-permute-start.11 = (f32[64,64]{1,0:T(8,128)S(1)}, f32[64,64]{1,0:T(8,128)S(1)}, u32[]{:S(2)}, u32[]{:S(2)}) collective-permute-start(f32[64,64]{1,0:T(8,128)S(1)} %convolution_add_fusion.4), channel_id=1, source_target_pairs={{0,6},{2,4},{4,2},{6,0},{8,14},{10,12},{12,10},{14,8},{16,22},{18,... | collective-permute-start | bytes 49160 | tf_op jit(solution)/shard_map/ppermute | solution.py:467
  106.0 4.0 %collective-permute-start.12 = (f32[64,64]{1,0:T(8,128)S(1)}, f32[64,64]{1,0:T(8,128)S(1)}, u32[]{:S(2)}, u32[]{:S(2)}) collective-permute-start(f32[64,64]{1,0:T(8,128)S(1)} %convolution_add_fusion.3), channel_id=1, source_target_pairs={{0,8},{2,10},{4,12},{6,14},{8,0},{10,2},{12,4},{14,6},{16,24},{18,... | collective-permute-start | bytes 49160 | tf_op jit(solution)/shard_map/ppermute | solution.py:467
  110.1 5.2 %collective-permute-start.13 = (f32[64,64]{1,0:T(8,128)S(1)}, f32[64,64]{1,0:T(8,128)S(1)}, u32[]{:S(2)}, u32[]{:S(2)}) collective-permute-start(f32[64,64]{1,0:T(8,128)S(1)} %convolution_add_fusion.2), channel_id=1, source_target_pairs={{0,24},{2,26},{4,28},{6,30},{8,16},{10,18},{12,20},{14,22},{16,8},... | collective-permute-start | bytes 49160 | tf_op jit(solution)/shard_map/ppermute | solution.py:467
  115.5 4.0 %collective-permute-start.14 = (f32[64,64]{1,0:T(8,128)S(1)}, f32[64,64]{1,0:T(8,128)S(1)}, u32[]{:S(2)}, u32[]{:S(2)}) collective-permute-start(f32[64,64]{1,0:T(8,128)S(1)} %convolution_add_fusion.1), channel_id=1, source_target_pairs={{0,32},{2,34},{4,36},{6,38},{8,40},{10,42},{12,44},{14,46},{16,48}... | collective-permute-start | bytes 49160 | tf_op jit(solution)/shard_map/ppermute | solution.py:467
  119.7 5.2 %collective-permute-start.15 = (f32[64,64]{1,0:T(8,128)S(1)}, f32[64,64]{1,0:T(8,128)S(1)}, u32[]{:S(2)}, u32[]{:S(2)}) collective-permute-start(f32[64,64]{1,0:T(8,128)S(1)} %convolution_add_fusion), channel_id=1, source_target_pairs={{0,96},{2,98},{4,100},{6,102},{8,104},{10,106},{12,108},{14,110},{... | collective-permute-start | bytes 49160 | tf_op jit(solution)/shard_map/ppermute | solution.py:467
  (2 other events, 4.2 us)

commit v7 on v6

--- a/solution.py
+++ b/solution.py
@@ -55,6 +55,14 @@
 
 def columns_of(start, width):
     return pl.ds(pl.multiple_of(start, width), width)
+
+
+def load_piece(near, kept, piece, sems, at=0):
+    some = kept.shape[0] // PIECES
+    return [
+        pltpu.make_async_copy(near.at[piece * some + i], kept.at[piece * some + i], sems.at[at + i])
+        for i in range(some)
+    ]
 
 
 def split_body(v, va, vb, sems):
@@ -84,14 +92,15 @@
     )(pltpu.with_memory_space_constraint(vectors, pltpu.HBM))
 
 
-def head_body(va, vb, basis_hbm, trans_hbm, coef, node, basis, trans, sems):
+def head_body(va, vb, basis_hbm, trans_hbm, near, coef, node, kept, basis, trans, sems):
     leaves, rank, points = basis.shape
     first_a = jnp.where(is_even(), leaves // 2, 0)
     copies = [
         pltpu.make_async_copy(basis_hbm, basis, sems.at[0]),
         pltpu.make_async_copy(trans_hbm, trans, sems.at[1]),
     ]
-    for copy in copies:
+    later = load_piece(near, kept, 0, sems, 2)
+    for copy in copies + later:
         copy.start()
     for copy in copies:
         copy.wait()
@@ -106,24 +115,28 @@
             term = mm(both, trans[at, :])
             total = term if total is None else total + term
     node[...] = total
-
-
-def head(va, vb, basis_t, trans2):
+    for copy in later:
+        copy.wait()
+
+
+def head(va, vb, basis_t, trans2, near_blocks):
     columns = va.shape[0]
     leaves, rank, _ = basis_t.shape
-    hbm = (pltpu.with_memory_space_constraint(x, pltpu.HBM) for x in (basis_t, trans2))
+    arrays = (basis_t, trans2, near_blocks)
+    hbm = (pltpu.with_memory_space_constraint(x, pltpu.HBM) for x in arrays)
     return pl.pallas_call(
         head_body,
-        in_specs=[VMEM] * 2 + [HBM] * 2,
-        out_specs=[VMEM] * 2,
+        in_specs=[VMEM] * 2 + [HBM] * 3,
+        out_specs=[VMEM] * 3,
         out_shape=[
             jax.ShapeDtypeStruct((columns, leaves * rank), BF),
             jax.ShapeDtypeStruct((columns, rank), F32),
+            jax.ShapeDtypeStruct(near_blocks.shape, BF),
         ],
         scratch_shapes=[
             pltpu.VMEM(basis_t.shape, BF),
             pltpu.VMEM(trans2.shape, BF),
-            pltpu.SemaphoreType.DMA((2,)),
+            pltpu.SemaphoreType.DMA((2 + leaves // PIECES,)),
         ],
         compiler_params=params(6),
         cost_estimate=cost(200_000_000, 6_000_000),
@@ -131,21 +144,16 @@
     )(va, vb, *hbm)
 
 
-def load_piece(near, kept, piece, sems):
-    some = kept.shape[0] // PIECES
-    return [
-        pltpu.make_async_copy(near.at[piece * some + i], kept.at[piece * some + i], sems.at[i])
-        for i in range(some)
-    ]
-
-
-def table_body(levels, near_list, trans_hbm, couple_hbm, near, up, pair, plan, kept, *scratch):
+def table_body(
+    levels, near_list, trans_hbm, couple_hbm, near, old_kept, up, pair, plan, kept, *scratch
+):
     trans, couple, sems = scratch
     copies = [
-        pltpu.make_async_copy(trans_hbm, trans, sems.at[8]),
-        pltpu.make_async_copy(couple_hbm, couple, sems.at[9]),
+        pltpu.make_async_copy(trans_hbm, trans, sems.at[0]),
+        pltpu.make_async_copy(couple_hbm, couple, sems.at[1]),
     ]
-    copies += load_piece(near, kept, 0, sems)
+    copies += load_piece(near, kept, 1, sems, 2)
+    copies += load_piece(near, kept, 2, sems, len(copies))
     for copy in copies:
         copy.start()
     device = lax.axis_index("leaf")
@@ -215,7 +223,7 @@
     )(up, pair)
 
 
-def table(top_transfer, top_couple, near_list_t, near_blocks):
+def table(top_transfer, top_couple, near_list_t, near_blocks, kept):
     nodes, rank, _ = top_transfer.shape
     levels = lax.axis_size("leaf").bit_length() - 1
     shape = near_blocks.shape
@@ -228,12 +236,12 @@
         lambda *refs: table_body(levels, *refs),
         grid_spec=pltpu.PrefetchScalarGridSpec(
             num_scalar_prefetch=1,
-            in_specs=[HBM] * 3,
+            in_specs=[HBM] * 3 + [VMEM],
             out_specs=[VMEM, VMEM, pl.BlockSpec(memory_space=pltpu.SMEM), VMEM],
             scratch_shapes=[
                 pltpu.VMEM((rank, rank, nodes), BF),
                 pltpu.VMEM((rank, rank, nodes), BF),
-                pltpu.SemaphoreType.DMA((shape[0] // PIECES + 2,)),
+                pltpu.SemaphoreType.DMA((2 * (shape[0] // PIECES) + 2,)),
             ],
         ),
         out_shape=[
@@ -242,17 +250,18 @@
             jax.ShapeDtypeStruct((2 * LIST + 8,), jnp.int32),
             jax.ShapeDtypeStruct(shape, BF),
         ],
+        input_output_aliases={4: 3},
         compiler_params=params(6),
         cost_estimate=cost(10_000_000, 8_000_000),
         name="table",
-    )(near_list_t, *(pltpu.with_memory_space_constraint(x, pltpu.HBM) for x in hbm))
+    )(near_list_t, *(pltpu.with_memory_space_constraint(x, pltpu.HBM) for x in hbm), kept)
 
 
 def near_body(piece, load, near_list, v, kept, *refs):
     copies = []
     if load:
         near, total, kept, sems = refs
-        copies = load_piece(near, kept, piece + 1, sems)
+        copies = load_piece(near, kept, PIECES - 1, sems)
         for copy in copies:
             copy.start()
     else:
@@ -364,6 +373,31 @@
     )(plan, got_va, got_ca, sent_c, kept, *partial)
 
 
+def side_b_body(plan, got_vb, got_cb, near, old_acc, old_table, acc, table_ref):
+    leaves = near.shape[0]
+    unpack(got_cb, jnp.where(is_even(), 0, 2 * leaves), table_ref)
+    add_halo(1, plan, got_vb, near, acc)
+
+
+def side_b(plan, got_vb, got_cb, kept, acc, entries):
+    return pl.pallas_call(
+        side_b_body,
+        grid_spec=pltpu.PrefetchScalarGridSpec(
+            num_scalar_prefetch=1,
+            in_specs=[VMEM] * 5,
+            out_specs=[VMEM] * 2,
+        ),
+        out_shape=[
+            jax.ShapeDtypeStruct(acc.shape, acc.dtype),
+            jax.ShapeDtypeStruct(entries.shape, entries.dtype),
+        ],
+        input_output_aliases={4: 0, 5: 1},
+        compiler_params=params(4),
+        cost_estimate=cost(200_000_000, 3_000_000),
+        name="side_b",
+    )(plan, got_vb, got_cb, kept, acc, entries)
+
+
 def tail_body(names, sides, more, *refs):
     r = dict(zip(names, refs))
     acc, table_ref, couple_list = r["acc"], r["table"], r["couple_list"]
@@ -374,9 +408,6 @@
     first = lax.axis_index("leaf") * leaves
     first_b = jnp.where(even, 0, leaves // 2)
     descent = r["top"][...].astype(BF)
-    if "b" in sides:
-        unpack(r["got_cb"], jnp.where(even, 0, 2 * leaves), table_ref)
-        add_halo(1, r["plan"], r["got_vb"], r["near"], acc)
     own_v = r["own_v"]
     writes = []
     total = r["node_in"][...] if "node_in" in r else None
@@ -516,10 +547,10 @@
     def fill_first(t):
         if t == 0:
             made["up"], made["pair"], made["plan"], made["kept"] = table(
-                top_transfer, top_couple, near_list_t, near_blocks
+                top_transfer, top_couple, near_list_t, near_blocks, made["kept"]
             )
         elif t <= PIECES:
-            load = t < PIECES
+            load = t == 1
             out = near_piece(t - 1, near_list_t, rhs_block, near_blocks, made["kept"], load)
             partial.append(out[0])
             if load:
@@ -535,31 +566,34 @@
             (out,) = near_piece(piece, near_list_t, made["own_v"], near_blocks, made["kept"], False)
             again.append(out)
 
-    def parts(top, got_vb, got_cb):
-        scalars = {"plan": made["plan"], "couple_list": couple_list_t}
-        inputs = {"top": top, "basis": basis_t, "trans": trans2, "couple": leaf_couple}
-        on_b = {"got_vb": got_vb, "got_cb": got_cb, "near": made["kept"]}
-        return scalars, inputs, on_b
+    scalars = {"couple_list": couple_list_t}
+
+    def parts(top):
+        return {"top": top, "basis": basis_t, "trans": trans2, "couple": leaf_couple}
+
+    def sides(got_va, got_vb, got_ca, got_cb, coef, own):
+        acc, entries = side_a(made["plan"], got_va, got_ca, coef, made["kept"], own)
+        acc, entries = side_b(made["plan"], got_vb, got_cb, made["kept"], acc, entries)
+        return {"acc": acc, "table": entries}
 
     va, vb = split(rhs_block)
     got_va = swapped(va, 1)
     got_vb = swapped_odd(vb)
-    coef, node = head(va, vb, basis_t, trans2)
+    coef, node, made["kept"] = head(va, vb, basis_t, trans2, near_blocks)
     top, _, got_ca, got_cb = one_product(node, va, coef, got_va, fill_first, tables)
-    acc, entries = side_a(made["plan"], got_va, got_ca, coef, made["kept"], partial)
-    scalars, inputs, on_b = parts(top, got_vb, got_cb)
-    half = tail("b", True, scalars, {**inputs, **on_b}, {"acc": acc, "table": entries})
+    carried = sides(got_va, got_vb, got_ca, got_cb, coef, partial)
+    inputs = parts(top)
+    half = tail("b", True, scalars, inputs, carried)
     got_vb = swapped_odd(half["message"])
-    inputs["node_in"] = half["node"]
+    inputs = {**inputs, "node_in": half["node"]}
     carried = {k: half[k] for k in ("acc", "table", "image", "own_v", "coef")}
     rest = tail("a", True, scalars, inputs, carried)
     first_image, coef, made["own_v"] = rest["image"], rest["coef"], rest["own_v"]
     top, got_va, got_ca, got_cb = one_product(
         rest["node"], rest["message"], coef, None, fill_second, tables
     )
-    acc, entries = side_a(made["plan"], got_va, got_ca, coef, made["kept"], again)
-    scalars, inputs, on_b = parts(top, got_vb, got_cb)
-    last = tail("ba", False, scalars, {**inputs, **on_b}, {"acc": acc, "table": entries})
+    carried = sides(got_va, got_vb, got_ca, got_cb, coef, again)
+    last = tail("ba", False, scalars, parts(top), carried)
     return (first_image, last["image"])
 
 

time: 137 us -> 138 us (level)
    pallas_call x1 -> x3, Pallas kernels: 2.8 us -> 7.57 us  [the longest x2 4.54 us: side_b(): pl.pallas_call(side_b_body, grid_spec=pltpu.PrefetchScalarGridSpec(num_sc...]
    pallas_call x3, Pallas kernels: 21.3 us -> 17.8 us  [tail(): pl.pallas_call(lambda *refs: tail_body(names, sides, more, *refs), grid_s...]
    pallas_call x8, Pallas kernels: 20.9 us -> 19.2 us  [near_piece(): pl.pallas_call(lambda *refs: near_body(piece, load, *refs), grid_spec=plt...]
    pallas_call x1, Pallas kernels: 4.37 us -> 5.93 us  [table(): pl.pallas_call(lambda *refs: table_body(levels, *refs), grid_spec=pltpu.P...]
  transfers between devices with their start and end apart: 20 -> 20, of which waited for: 10 -> 10; matrix products, arithmetic and copies ran while one was open for 4% -> 4% of each run, Pallas kernels for 19% -> 17%
where the time goes in v7:
time: 138 us
  Pallas kernels  56.7 us (41%)
  starting transfers between devices  38.8 us (28%)
  waiting for transfers between devices  35.9 us (26%)
  matrix products  5.46 us (4%)
    ppermute x16, waiting for transfers between devices, swapped(): lax.ppermute(value, 'leaf', [(i, i ^ mask) for i in range(lax.axis_size('...  35.9 us
    ppermute x16, starting transfers between devices, swapped(): lax.ppermute(value, 'leaf', [(i, i ^ mask) for i in range(lax.axis_size('...  23.8 us
    pallas_call x8, Pallas kernels, near_piece(): pl.pallas_call(lambda *refs: near_body(piece, load, *refs), grid_spec=plt...  19.2 us
    pallas_call x3, Pallas kernels, tail(): pl.pallas_call(lambda *refs: tail_body(names, sides, more, *refs), grid_s...  17.8 us
    ppermute x4, starting transfers between devices, swapped_odd(): return lax.ppermute(value, 'leaf', pairs + [(j, i) for i, j in pairs])  15 us
    pallas_call x1, Pallas kernels, table(): pl.pallas_call(lambda *refs: table_body(levels, *refs), grid_spec=pltpu.P...  5.93 us
    dot_general x32, matrix products, exact(): lax.dot_general(a, b, dims, precision=lax.Precision.HIGHEST, preferred_el...  5.46 us
    pallas_call x2, Pallas kernels, side_b(): pl.pallas_call(side_b_body, grid_spec=pltpu.PrefetchScalarGridSpec(num_sc...  4.54 us
  transfers between devices with their start and end apart: 20, of which 10 were waited for; matrix products, arithmetic and copies ran while one was open for 4% of the time, Pallas kernels for 17%

profile of v7, /device:TPU:24, one launch (start us, length us, event | category | flops | bytes accessed | tf_op | source)
XLA Modules:
  0.0 138.3 jit_solution(407351493415223114)
XLA Ops:
  3.4 3.0 %head.1 = (bf16[64,2048]{1,0:T(8,128)(2,1)S(1)}, f32[64,64]{1,0:T(8,128)S(1)}, bf16[32,5,256,256]{3,2,1,0:T(8,128)(2,1)S(1)}) custom-call(bf16[64,4096]{1,0:T(8,128)(2,1)S(1)} %get-tuple-element.34.va, bf16[64,4096]{1,0:T(8,128)(2,1)S(1)} %get-tuple-element.35.vb, bf16[32,64,256]{2,1,0:T(8,128)(2,1)} %refs_2_.5, bf16[2048,64]{1,0:T(8,128)(2,1)} %bitcast.111, ...), custom_call_target="tpu_custom_call" | custom-call | flops 200000000 | bytes 6000000 | tf_op jit(solution)/shard_map/head/pallas_call | solution.py:127
  7.1 4.8 %collective-permute-start.7 = (bf16[64,2048]{1,0:T(8,128)(2,1)S(1)}, bf16[64,2048]{1,0:T(8,128)(2,1)S(1)}, u32[]{:S(2)}, u32[]{:S(2)}) collective-permute-start(bf16[64,2048]{1,0:T(8,128)(2,1)S(1)} %get-tuple-element.41.sent_c), channel_id=1, source_target_pairs={{2,4},{6,8},{10,12},{14,16},{18,20},{22,24},{26,28},{30,32},{34,36... | collective-permute-start | bytes 786440 | tf_op jit(solution)/shard_map/ppermute | solution.py:504
  11.9 3.1 %collective-permute-start.6 = (bf16[64,4096]{1,0:T(8,128)(2,1)S(1)}, bf16[64,4096]{1,0:T(8,128)(2,1)S(1)}, u32[]{:S(2)}, u32[]{:S(2)}) collective-permute-start(bf16[64,4096]{1,0:T(8,128)(2,1)S(1)} %get-tuple-element.35.vb), channel_id=1, source_target_pairs={{2,4},{6,8},{10,12},{14,16},{18,20},{22,24},{26,28},{30,32},{34,36... | collective-permute-start | bytes 1572872 | tf_op jit(solution)/shard_map/ppermute | solution.py:504
  15.2 5.9 %table.1 = (f32[2,6,64,64]{3,2,1,0:T(8,128)S(1)}, f32[6,64,64]{2,1,0:T(8,128)S(1)}, s32[168]{0:T(256)S(1)}, bf16[32,5,256,256]{3,2,1,0:T(8,128)(2,1)S(1)}) custom-call(s32[5,32]{1,0:T(8,128)S(1)} %bitcast.115, bf16[64,64,126]{2,1,0:T(8,128)(2,1)} %bitcast.127, bf16[64,64,126]{2,1,0:T(8,128)(2,1)} %bitcast.128, ...), custom_call_target="tpu_custom_call", output_to_operand_aliasing={{3}: (4, {})} | custom-call | flops 10000000 | bytes 8000000 | tf_op jit(solution)/shard_map/table/pallas_call | solution.py:235
  21.1 3.1 %shard_map.104 = (f32[64,2048]{1,0:T(8,128)S(1)}, bf16[32,5,256,256]{3,2,1,0:T(8,128)(2,1)S(1)}) custom-call(s32[5,32]{1,0:T(8,128)S(1)} %bitcast.116, bf16[64,8192]{1,0:T(8,128)(2,1)S(1)} %copy-done, bf16[32,5,256,256]{3,2,1,0:T(8,128)(2,1)S(1)} %get-tuple-element.42.refs_2_, bf16[32,5,256,256]{3,2,1,0:T(8,128)(2,1)} %refs_3_.3), custom_call_target="tpu_custom_call", output_to_operand_aliasing={{1}: (2, {})} | custom-call | flops 350000000 | bytes 6000000 | tf_op jit(solution)/shard_map/pallas_call | solution.py:299
  32.4 4.9 %collective-permute-start.1 = (f32[64,64]{1,0:T(8,128)S(1)}, f32[64,64]{1,0:T(8,128)S(1)}, u32[]{:S(2)}, u32[]{:S(2)}) collective-permute-start(f32[64,64]{1,0:T(8,128)S(1)} %convolution_add_fusion.10), channel_id=1, source_target_pairs={{0,6},{2,4},{4,2},{6,0},{8,14},{10,12},{12,10},{14,8},{16,22},{18,... | collective-permute-start | bytes 49160 | tf_op jit(solution)/shard_map/ppermute | solution.py:498
  39.9 3.5 %collective-permute-done.2 = f32[64,64]{1,0:T(8,128)S(1)} collective-permute-done((f32[64,64]{1,0:T(8,128)S(1)}, f32[64,64]{1,0:T(8,128)S(1)}, u32[]{:S(2)}, u32[]{:S(2)}) %collective-permute-start.2) | collective-permute-done | bytes 16416 | tf_op jit(solution)/shard_map/ppermute | solution.py:498
  44.0 4.8 %collective-permute-done.3 = f32[64,64]{1,0:T(8,128)S(1)} collective-permute-done((f32[64,64]{1,0:T(8,128)S(1)}, f32[64,64]{1,0:T(8,128)S(1)}, u32[]{:S(2)}, u32[]{:S(2)}) %collective-permute-start.3) | collective-permute-done | bytes 16416 | tf_op jit(solution)/shard_map/ppermute | solution.py:498
  53.1 2.5 %collective-permute-start.5 = (f32[64,64]{1,0:T(8,128)S(1)}, f32[64,64]{1,0:T(8,128)S(1)}, u32[]{:S(2)}, u32[]{:S(2)}) collective-permute-start(f32[64,64]{1,0:T(8,128)S(1)} %convolution_add_fusion.6), channel_id=1, source_target_pairs={{0,96},{2,98},{4,100},{6,102},{8,104},{10,106},{12,108},{14,110},{... | collective-permute-start | bytes 49160 | tf_op jit(solution)/shard_map/ppermute | solution.py:498
  55.8 2.5 %collective-permute-done.5 = f32[64,64]{1,0:T(8,128)S(1)} collective-permute-done((f32[64,64]{1,0:T(8,128)S(1)}, f32[64,64]{1,0:T(8,128)S(1)}, u32[]{:S(2)}, u32[]{:S(2)}) %collective-permute-start.5) | collective-permute-done | bytes 16416 | tf_op jit(solution)/shard_map/ppermute | solution.py:498
  60.8 2.4 %side_b.2 = (f32[64,8448]{1,0:T(8,128)S(1)}, bf16[96,64,128]{2,1,0:T(8,128)(2,1)S(1)}) custom-call(s32[168]{0:T(256)S(1)} %get-tuple-element.40.plan, bf16[64,4096]{1,0:T(8,128)(2,1)S(1)} %collective-permute-done.6.got_vb, bf16[64,2048]{1,0:T(8,128)(2,1)S(1)} %collective-permute-done.7.got_cb, ...), custom_call_target="tpu_custom_call", output_to_operand_aliasing={{0}: (4, {}), {1}: (5, {})} | custom-call | flops 200000000 | bytes 3000000 | tf_op jit(solution)/shard_map/side_b/pallas_call | solution.py:383
  63.2 4.9 %shard_map.108 = (f32[64,8448]{1,0:T(8,128)S(1)}, bf16[96,64,128]{2,1,0:T(8,128)(2,1)S(1)}, bf16[64,8192]{1,0:T(8,128)(2,1)}, bf16[64,8192]{1,0:T(8,128)(2,1)S(1...) custom-call(s32[4,32]{1,0:T(4,128)S(1)} %bitcast.124, ...), custom_call_target="tpu_custom_call", output_to_operand_aliasing={{0}: (5, {}), {1}: (6, {})} | custom-call | flops 600000000 | bytes 6000000 | tf_op jit(solution)/shard_map/pallas_call | solution.py:476
  68.1 5.1 %shard_map.109 = (f32[64,8448]{1,0:T(8,128)S(1)}, bf16[96,64,128]{2,1,0:T(8,128)(2,1)S(1)}, bf16[64,8192]{1,0:T(8,128)(2,1)}, bf16[64,8192]{1,0:T(8,128)(2,1)S(1...) custom-call(s32[4,32]{1,0:T(4,128)S(1)} %bitcast.125, ...), custom_call_target="tpu_custom_call", output_to_operand_aliasing={{0}: (6, {}), {1}: (7, {}), {2}: (8, {}), {3}: (9, {}), {4}... | custom-call | flops 600000000 | bytes 6000000 | tf_op jit(solution)/shard_map/pallas_call | solution.py:476
  77.8 2.3 %shard_map.111.refs_1_ = f32[64,2048]{1,0:T(8,128)S(1)} custom-call(s32[5,32]{1,0:T(8,128)S(1)} %bitcast.122, bf16[64,8192]{1,0:T(8,128)(2,1)S(1)} %get-tuple-element.60.refs_1_, bf16[32,5,256,256]{3,2,1,0:T(8,128)(2,1)S(1)} %get-tuple-element.43.refs_2_.near), custom_call_target="tpu_custom_call" | custom-call | flops 350000000 | bytes 6000000 | tf_op jit(solution)/shard_map/pallas_call | solution.py:299
  83.8 3.2 %collective-permute-start.17 = (bf16[64,2048]{1,0:T(8,128)(2,1)S(1)}, bf16[64,2048]{1,0:T(8,128)(2,1)S(1)}, u32[]{:S(2)}, u32[]{:S(2)}) collective-permute-start(bf16[64,2048]{1,0:T(8,128)(2,1)S(1)} %get-tuple-element.58.sent_c), channel_id=1, source_target_pairs={{2,4},{6,8},{10,12},{14,16},{18,20},{22,24},{26,28},{30,32},{34,36... | collective-permute-start | bytes 786440 | tf_op jit(solution)/shard_map/ppermute | solution.py:504
  87.0 2.9 %collective-permute-start.10 = (f32[64,64]{1,0:T(8,128)S(1)}, f32[64,64]{1,0:T(8,128)S(1)}, u32[]{:S(2)}, u32[]{:S(2)}) collective-permute-start(f32[64,64]{1,0:T(8,128)S(1)} %get-tuple-element.56), channel_id=1, source_target_pairs={{0,2},{2,0},{4,6},{6,4},{8,10},{10,8},{12,14},{14,12},{16,18},{18,... | collective-permute-start | bytes 49160 | tf_op jit(solution)/shard_map/ppermute | solution.py:498
  90.2 3.9 %collective-permute-start.16 = (bf16[64,4096]{1,0:T(8,128)(2,1)S(1)}, bf16[64,4096]{1,0:T(8,128)(2,1)S(1)}, u32[]{:S(2)}, u32[]{:S(2)}) collective-permute-start(bf16[64,4096]{1,0:T(8,128)(2,1)S(1)} %get-tuple-element.57), channel_id=1, source_target_pairs={{2,4},{6,8},{10,12},{14,16},{18,20},{22,24},{26,28},{30,32},{34,36... | collective-permute-start | bytes 1572872 | tf_op jit(solution)/shard_map/ppermute | solution.py:504
  94.3 4.9 %collective-permute-start.11 = (f32[64,64]{1,0:T(8,128)S(1)}, f32[64,64]{1,0:T(8,128)S(1)}, u32[]{:S(2)}, u32[]{:S(2)}) collective-permute-start(f32[64,64]{1,0:T(8,128)S(1)} %convolution_add_fusion.4), channel_id=1, source_target_pairs={{0,6},{2,4},{4,2},{6,0},{8,14},{10,12},{12,10},{14,8},{16,22},{18,... | collective-permute-start | bytes 49160 | tf_op jit(solution)/shard_map/ppermute | solution.py:498
  99.4 7.1 %collective-permute-done.11 = f32[64,64]{1,0:T(8,128)S(1)} collective-permute-done((f32[64,64]{1,0:T(8,128)S(1)}, f32[64,64]{1,0:T(8,128)S(1)}, u32[]{:S(2)}, u32[]{:S(2)}) %collective-permute-start.11) | collective-permute-done | bytes 16416 | tf_op jit(solution)/shard_map/ppermute | solution.py:498
  107.1 3.5 %collective-permute-done.12 = f32[64,64]{1,0:T(8,128)S(1)} collective-permute-done((f32[64,64]{1,0:T(8,128)S(1)}, f32[64,64]{1,0:T(8,128)S(1)}, u32[]{:S(2)}, u32[]{:S(2)}) %collective-permute-start.12) | collective-permute-done | bytes 16416 | tf_op jit(solution)/shard_map/ppermute | solution.py:498
  111.3 4.8 %collective-permute-done.13 = f32[64,64]{1,0:T(8,128)S(1)} collective-permute-done((f32[64,64]{1,0:T(8,128)S(1)}, f32[64,64]{1,0:T(8,128)S(1)}, u32[]{:S(2)}, u32[]{:S(2)}) %collective-permute-start.13) | collective-permute-done | bytes 16416 | tf_op jit(solution)/shard_map/ppermute | solution.py:498
  117.7 2.5 %collective-permute-done.14 = f32[64,64]{1,0:T(8,128)S(1)} collective-permute-done((f32[64,64]{1,0:T(8,128)S(1)}, f32[64,64]{1,0:T(8,128)S(1)}, u32[]{:S(2)}, u32[]{:S(2)}) %collective-permute-start.14) | collective-permute-done | bytes 16416 | tf_op jit(solution)/shard_map/ppermute | solution.py:498
  121.7 3.9 %collective-permute-done.15 = f32[64,64]{1,0:T(8,128)S(1)} collective-permute-done((f32[64,64]{1,0:T(8,128)S(1)}, f32[64,64]{1,0:T(8,128)S(1)}, u32[]{:S(2)}, u32[]{:S(2)}) %collective-permute-start.15) | collective-permute-done | bytes 16416 | tf_op jit(solution)/shard_map/ppermute | solution.py:498
  130.2 7.9 %shard_map.114 = (f32[64,8448]{1,0:T(8,128)S(1)}, bf16[96,64,128]{2,1,0:T(8,128)(2,1)S(1)}, bf16[64,8192]{1,0:T(8,128)(2,1)}) custom-call(s32[4,32]{1,0:T(4,128)S(1)} %bitcast.126, f32[64,64]{1,0:T(8,128)S(1)} %fusion.3.refs_1_, bf16[32,64,256]{2,1,0:T(8,128)(2,1)S(1)} %copy-done.2, ...), custom_call_target="tpu_custom_call", output_to_operand_aliasing={{0}: (5, {}), {1}: (6, {})} | custom-call | flops 600000000 | bytes 6000000 | tf_op jit(solution)/shard_map/pallas_call | solution.py:476
  (79 shorter events, 39.4 us)
Async XLA Ops:
  1.9 56.9 %collective-permute-start.8 = (bf16[64,4096]{1,0:T(8,128)(2,1)S(1)}, bf16[64,4096]{1,0:T(8,128)(2,1)S(1)}, u32[]{:S(2)}, u32[]{:S(2)}) collective-permute-start(bf16[64,4096]{1,0:T(8,128)(2,1)S(1)} %get-tuple-element.34.va), channel_id=1, source_target_pairs={{0,2},{2,0},{4,6},{6,4},{8,10},{10,8},{12,14},{14,12},{16,18},{18,... | collective-permute-start | bytes 1572872 | tf_op jit(solution)/shard_map/ppermute | solution.py:498
  3.4 11.7 %copy-start.4 = (s32[32,5]{0,1:T(8,128)S(1)}, s32[32,5]{0,1:T(8,128)}, u32[]{:S(2)}) copy-start(s32[32,5]{0,1:T(8,128)} %param.12) | copy-start | bytes 1924
  6.5 52.3 %collective-permute-start.9 = (bf16[64,2048]{1,0:T(8,128)(2,1)S(1)}, bf16[64,2048]{1,0:T(8,128)(2,1)S(1)}, u32[]{:S(2)}, u32[]{:S(2)}) collective-permute-start(bf16[64,2048]{1,0:T(8,128)(2,1)S(1)} %get-tuple-element.41.sent_c), channel_id=1, source_target_pairs={{0,2},{2,0},{4,6},{6,4},{8,10},{10,8},{12,14},{14,12},{16,18},{18,... | collective-permute-start | bytes 786440 | tf_op jit(solution)/shard_map/ppermute | solution.py:498
  7.1 53.7 %collective-permute-start.7 = (bf16[64,2048]{1,0:T(8,128)(2,1)S(1)}, bf16[64,2048]{1,0:T(8,128)(2,1)S(1)}, u32[]{:S(2)}, u32[]{:S(2)}) collective-permute-start(bf16[64,2048]{1,0:T(8,128)(2,1)S(1)} %get-tuple-element.41.sent_c), channel_id=1, source_target_pairs={{2,4},{6,8},{10,12},{14,16},{18,20},{22,24},{26,28},{30,32},{34,36... | collective-permute-start | bytes 786440 | tf_op jit(solution)/shard_map/ppermute | solution.py:504
  11.9 48.8 %collective-permute-start.6 = (bf16[64,4096]{1,0:T(8,128)(2,1)S(1)}, bf16[64,4096]{1,0:T(8,128)(2,1)S(1)}, u32[]{:S(2)}, u32[]{:S(2)}) collective-permute-start(bf16[64,4096]{1,0:T(8,128)(2,1)S(1)} %get-tuple-element.35.vb), channel_id=1, source_target_pairs={{2,4},{6,8},{10,12},{14,16},{18,20},{22,24},{26,28},{30,32},{34,36... | collective-permute-start | bytes 1572872 | tf_op jit(solution)/shard_map/ppermute | solution.py:504
  15.0 17.2 %collective-permute-start = (f32[64,64]{1,0:T(8,128)S(1)}, f32[64,64]{1,0:T(8,128)S(1)}, u32[]{:S(2)}, u32[]{:S(2)}) collective-permute-start(f32[64,64]{1,0:T(8,128)S(1)} %get-tuple-element.36), channel_id=1, source_target_pairs={{0,2},{2,0},{4,6},{6,4},{8,10},{10,8},{12,14},{14,12},{16,18},{18,... | collective-permute-start | bytes 49160 | tf_op jit(solution)/shard_map/ppermute | solution.py:498
  15.1 6.0 %copy-start = (bf16[64,8192]{1,0:T(8,128)(2,1)S(1)}, bf16[64,8192]{1,0:T(8,128)(2,1)}, u32[]{:S(2)}) copy-start(bf16[64,8192]{1,0:T(8,128)(2,1)} %refs_1_.7) | copy-start | bytes 3145732
  32.4 6.8 %collective-permute-start.1 = (f32[64,64]{1,0:T(8,128)S(1)}, f32[64,64]{1,0:T(8,128)S(1)}, u32[]{:S(2)}, u32[]{:S(2)}) collective-permute-start(f32[64,64]{1,0:T(8,128)S(1)} %convolution_add_fusion.10), channel_id=1, source_target_pairs={{0,6},{2,4},{4,2},{6,0},{8,14},{10,12},{12,10},{14,8},{16,22},{18,... | collective-permute-start | bytes 49160 | tf_op jit(solution)/shard_map/ppermute | solution.py:498
  39.4 4.0 %collective-permute-start.2 = (f32[64,64]{1,0:T(8,128)S(1)}, f32[64,64]{1,0:T(8,128)S(1)}, u32[]{:S(2)}, u32[]{:S(2)}) collective-permute-start(f32[64,64]{1,0:T(8,128)S(1)} %convolution_add_fusion.9), channel_id=1, source_target_pairs={{0,8},{2,10},{4,12},{6,14},{8,0},{10,2},{12,4},{14,6},{16,24},{18,... | collective-permute-start | bytes 49160 | tf_op jit(solution)/shard_map/ppermute | solution.py:498
  43.6 5.2 %collective-permute-start.3 = (f32[64,64]{1,0:T(8,128)S(1)}, f32[64,64]{1,0:T(8,128)S(1)}, u32[]{:S(2)}, u32[]{:S(2)}) collective-permute-start(f32[64,64]{1,0:T(8,128)S(1)} %convolution_add_fusion.8), channel_id=1, source_target_pairs={{0,24},{2,26},{4,28},{6,30},{8,16},{10,18},{12,20},{14,22},{16,8},... | collective-permute-start | bytes 49160 | tf_op jit(solution)/shard_map/ppermute | solution.py:498
  49.0 4.0 %collective-permute-start.4 = (f32[64,64]{1,0:T(8,128)S(1)}, f32[64,64]{1,0:T(8,128)S(1)}, u32[]{:S(2)}, u32[]{:S(2)}) collective-permute-start(f32[64,64]{1,0:T(8,128)S(1)} %convolution_add_fusion.7), channel_id=1, source_target_pairs={{0,32},{2,34},{4,36},{6,38},{8,40},{10,42},{12,44},{14,46},{16,48}... | collective-permute-start | bytes 49160 | tf_op jit(solution)/shard_map/ppermute | solution.py:498
  53.1 5.2 %collective-permute-start.5 = (f32[64,64]{1,0:T(8,128)S(1)}, f32[64,64]{1,0:T(8,128)S(1)}, u32[]{:S(2)}, u32[]{:S(2)}) collective-permute-start(f32[64,64]{1,0:T(8,128)S(1)} %convolution_add_fusion.6), channel_id=1, source_target_pairs={{0,96},{2,98},{4,100},{6,102},{8,104},{10,106},{12,108},{14,110},{... | collective-permute-start | bytes 49160 | tf_op jit(solution)/shard_map/ppermute | solution.py:498
  60.8 2.4 %copy-start.1 = (bf16[32,4,64,64]{3,2,1,0:T(8,128)(2,1)S(1)}, bf16[32,4,64,64]{3,2,1,0:T(8,128)(2,1)}, u32[]{:S(2)}) copy-start(bf16[32,4,64,64]{3,2,1,0:T(8,128)(2,1)} %refs_4_.5) | copy-start | bytes 3145732
  60.8 2.4 %copy-start.2 = (bf16[32,64,256]{2,1,0:T(8,128)(2,1)S(1)}, bf16[32,64,256]{2,1,0:T(8,128)(2,1)}, u32[]{:S(2)}) copy-start(bf16[32,64,256]{2,1,0:T(8,128)(2,1)} %refs_2_.5) | copy-start | bytes 3145732
  82.4 43.6 %collective-permute-start.19 = (bf16[64,2048]{1,0:T(8,128)(2,1)S(1)}, bf16[64,2048]{1,0:T(8,128)(2,1)S(1)}, u32[]{:S(2)}, u32[]{:S(2)}) collective-permute-start(bf16[64,2048]{1,0:T(8,128)(2,1)S(1)} %get-tuple-element.58.sent_c), channel_id=1, source_target_pairs={{0,2},{2,0},{4,6},{6,4},{8,10},{10,8},{12,14},{14,12},{16,18},{18,... | collective-permute-start | bytes 786440 | tf_op jit(solution)/shard_map/ppermute | solution.py:498
  83.8 44.2 %collective-permute-start.17 = (bf16[64,2048]{1,0:T(8,128)(2,1)S(1)}, bf16[64,2048]{1,0:T(8,128)(2,1)S(1)}, u32[]{:S(2)}, u32[]{:S(2)}) collective-permute-start(bf16[64,2048]{1,0:T(8,128)(2,1)S(1)} %get-tuple-element.58.sent_c), channel_id=1, source_target_pairs={{2,4},{6,8},{10,12},{14,16},{18,20},{22,24},{26,28},{30,32},{34,36... | collective-permute-start | bytes 786440 | tf_op jit(solution)/shard_map/ppermute | solution.py:504
  87.0 7.1 %collective-permute-start.10 = (f32[64,64]{1,0:T(8,128)S(1)}, f32[64,64]{1,0:T(8,128)S(1)}, u32[]{:S(2)}, u32[]{:S(2)}) collective-permute-start(f32[64,64]{1,0:T(8,128)S(1)} %get-tuple-element.56), channel_id=1, source_target_pairs={{0,2},{2,0},{4,6},{6,4},{8,10},{10,8},{12,14},{14,12},{16,18},{18,... | collective-permute-start | bytes 49160 | tf_op jit(solution)/shard_map/ppermute | solution.py:498
  90.1 35.8 %collective-permute-start.18 = (bf16[64,4096]{1,0:T(8,128)(2,1)S(1)}, bf16[64,4096]{1,0:T(8,128)(2,1)S(1)}, u32[]{:S(2)}, u32[]{:S(2)}) collective-permute-start(bf16[64,4096]{1,0:T(8,128)(2,1)S(1)} %get-tuple-element.59), channel_id=1, source_target_pairs={{0,2},{2,0},{4,6},{6,4},{8,10},{10,8},{12,14},{14,12},{16,18},{18,... | collective-permute-start | bytes 1572872 | tf_op jit(solution)/shard_map/ppermute | solution.py:498
  90.2 37.8 %collective-permute-start.16 = (bf16[64,4096]{1,0:T(8,128)(2,1)S(1)}, bf16[64,4096]{1,0:T(8,128)(2,1)S(1)}, u32[]{:S(2)}, u32[]{:S(2)}) collective-permute-start(bf16[64,4096]{1,0:T(8,128)(2,1)S(1)} %get-tuple-element.57), channel_id=1, source_target_pairs={{2,4},{6,8},{10,12},{14,16},{18,20},{22,24},{26,28},{30,32},{34,36... | collective-permute-start | bytes 1572872 | tf_op jit(solution)/shard_map/ppermute | solution.py:504
  94.3 12.2 %collective-permute-start.11 = (f32[64,64]{1,0:T(8,128)S(1)}, f32[64,64]{1,0:T(8,128)S(1)}, u32[]{:S(2)}, u32[]{:S(2)}) collective-permute-start(f32[64,64]{1,0:T(8,128)S(1)} %convolution_add_fusion.4), channel_id=1, source_target_pairs={{0,6},{2,4},{4,2},{6,0},{8,14},{10,12},{12,10},{14,8},{16,22},{18,... | collective-permute-start | bytes 49160 | tf_op jit(solution)/shard_map/ppermute | solution.py:498
  106.7 4.0 %collective-permute-start.12 = (f32[64,64]{1,0:T(8,128)S(1)}, f32[64,64]{1,0:T(8,128)S(1)}, u32[]{:S(2)}, u32[]{:S(2)}) collective-permute-start(f32[64,64]{1,0:T(8,128)S(1)} %convolution_add_fusion.3), channel_id=1, source_target_pairs={{0,8},{2,10},{4,12},{6,14},{8,0},{10,2},{12,4},{14,6},{16,24},{18,... | collective-permute-start | bytes 49160 | tf_op jit(solution)/shard_map/ppermute | solution.py:498
  110.8 5.2 %collective-permute-start.13 = (f32[64,64]{1,0:T(8,128)S(1)}, f32[64,64]{1,0:T(8,128)S(1)}, u32[]{:S(2)}, u32[]{:S(2)}) collective-permute-start(f32[64,64]{1,0:T(8,128)S(1)} %convolution_add_fusion.2), channel_id=1, source_target_pairs={{0,24},{2,26},{4,28},{6,30},{8,16},{10,18},{12,20},{14,22},{16,8},... | collective-permute-start | bytes 49160 | tf_op jit(solution)/shard_map/ppermute | solution.py:498
  116.2 4.0 %collective-permute-start.14 = (f32[64,64]{1,0:T(8,128)S(1)}, f32[64,64]{1,0:T(8,128)S(1)}, u32[]{:S(2)}, u32[]{:S(2)}) collective-permute-start(f32[64,64]{1,0:T(8,128)S(1)} %convolution_add_fusion.1), channel_id=1, source_target_pairs={{0,32},{2,34},{4,36},{6,38},{8,40},{10,42},{12,44},{14,46},{16,48}... | collective-permute-start | bytes 49160 | tf_op jit(solution)/shard_map/ppermute | solution.py:498
  120.4 5.2 %collective-permute-start.15 = (f32[64,64]{1,0:T(8,128)S(1)}, f32[64,64]{1,0:T(8,128)S(1)}, u32[]{:S(2)}, u32[]{:S(2)}) collective-permute-start(f32[64,64]{1,0:T(8,128)S(1)} %convolution_add_fusion), channel_id=1, source_target_pairs={{0,96},{2,98},{4,100},{6,102},{8,104},{10,106},{12,108},{14,110},{... | collective-permute-start | bytes 49160 | tf_op jit(solution)/shard_map/ppermute | solution.py:498
  (2 other events, 4.8 us)

commit v8 on v7

--- a/solution.py
+++ b/solution.py
@@ -153,7 +153,6 @@
         pltpu.make_async_copy(couple_hbm, couple, sems.at[1]),
     ]
     copies += load_piece(near, kept, 1, sems, 2)
-    copies += load_piece(near, kept, 2, sems, len(copies))
     for copy in copies:
         copy.start()
     device = lax.axis_index("leaf")
@@ -261,7 +260,7 @@
     copies = []
     if load:
         near, total, kept, sems = refs
-        copies = load_piece(near, kept, PIECES - 1, sems)
+        copies = load_piece(near, kept, piece + 2, sems)
         for copy in copies:
             copy.start()
     else:
@@ -550,7 +549,7 @@
                 top_transfer, top_couple, near_list_t, near_blocks, made["kept"]
             )
         elif t <= PIECES:
-            load = t == 1
+            load = t + 1 < PIECES
             out = near_piece(t - 1, near_list_t, rhs_block, near_blocks, made["kept"], load)
             partial.append(out[0])
             if load:

time: 138 us -> 138 us (level)
    pallas_call x1, Pallas kernels: 5.93 us -> 4.44 us  [table(): pl.pallas_call(lambda *refs: table_body(levels, *refs), grid_spec=pltpu.P...]
where the time goes in v8:
time: 138 us
  Pallas kernels  56 us (41%)
  starting transfers between devices  38.8 us (28%)
  waiting for transfers between devices  35.9 us (26%)
  matrix products  5.46 us (4%)
    ppermute x16, waiting for transfers between devices, swapped(): lax.ppermute(value, 'leaf', [(i, i ^ mask) for i in range(lax.axis_size('...  35.9 us
    ppermute x16, starting transfers between devices, swapped(): lax.ppermute(value, 'leaf', [(i, i ^ mask) for i in range(lax.axis_size('...  23.7 us
    pallas_call x8, Pallas kernels, near_piece(): pl.pallas_call(lambda *refs: near_body(piece, load, *refs), grid_spec=plt...  20 us
    pallas_call x3, Pallas kernels, tail(): pl.pallas_call(lambda *refs: tail_body(names, sides, more, *refs), grid_s...  17.8 us
    ppermute x4, starting transfers between devices, swapped_odd(): return lax.ppermute(value, 'leaf', pairs + [(j, i) for i, j in pairs])  15 us
    dot_general x32, matrix products, exact(): lax.dot_general(a, b, dims, precision=lax.Precision.HIGHEST, preferred_el...  5.46 us
    pallas_call x2, Pallas kernels, side_b(): pl.pallas_call(side_b_body, grid_spec=pltpu.PrefetchScalarGridSpec(num_sc...  4.54 us
    pallas_call x1, Pallas kernels, table(): pl.pallas_call(lambda *refs: table_body(levels, *refs), grid_spec=pltpu.P...  4.44 us
  transfers between devices with their start and end apart: 20, of which 10 were waited for; matrix products, arithmetic and copies ran while one was open for 4% of the time, Pallas kernels for 17%

profile of v8, /device:TPU:24, one launch (start us, length us, event | category | flops | bytes accessed | tf_op | source)
XLA Modules:
  0.0 137.6 jit_solution(18373345318095234260)
XLA Ops:
  3.4 3.0 %head.1 = (bf16[64,2048]{1,0:T(8,128)(2,1)S(1)}, f32[64,64]{1,0:T(8,128)S(1)}, bf16[32,5,256,256]{3,2,1,0:T(8,128)(2,1)S(1)}) custom-call(bf16[64,4096]{1,0:T(8,128)(2,1)S(1)} %get-tuple-element.36.va, bf16[64,4096]{1,0:T(8,128)(2,1)S(1)} %get-tuple-element.37.vb, bf16[32,64,256]{2,1,0:T(8,128)(2,1)} %refs_2_.5, bf16[2048,64]{1,0:T(8,128)(2,1)} %bitcast.111, ...), custom_call_target="tpu_custom_call" | custom-call | flops 200000000 | bytes 6000000 | tf_op jit(solution)/shard_map/head/pallas_call | solution.py:127
  7.1 4.8 %collective-permute-start.7 = (bf16[64,2048]{1,0:T(8,128)(2,1)S(1)}, bf16[64,2048]{1,0:T(8,128)(2,1)S(1)}, u32[]{:S(2)}, u32[]{:S(2)}) collective-permute-start(bf16[64,2048]{1,0:T(8,128)(2,1)S(1)} %get-tuple-element.43.sent_c), channel_id=1, source_target_pairs={{2,4},{6,8},{10,12},{14,16},{18,20},{22,24},{26,28},{30,32},{34,36... | collective-permute-start | bytes 786440 | tf_op jit(solution)/shard_map/ppermute | solution.py:503
  11.9 3.1 %collective-permute-start.6 = (bf16[64,4096]{1,0:T(8,128)(2,1)S(1)}, bf16[64,4096]{1,0:T(8,128)(2,1)S(1)}, u32[]{:S(2)}, u32[]{:S(2)}) collective-permute-start(bf16[64,4096]{1,0:T(8,128)(2,1)S(1)} %get-tuple-element.37.vb), channel_id=1, source_target_pairs={{2,4},{6,8},{10,12},{14,16},{18,20},{22,24},{26,28},{30,32},{34,36... | collective-permute-start | bytes 1572872 | tf_op jit(solution)/shard_map/ppermute | solution.py:503
  15.2 4.4 %table.1 = (f32[2,6,64,64]{3,2,1,0:T(8,128)S(1)}, f32[6,64,64]{2,1,0:T(8,128)S(1)}, s32[168]{0:T(256)S(1)}, bf16[32,5,256,256]{3,2,1,0:T(8,128)(2,1)S(1)}) custom-call(s32[5,32]{1,0:T(8,128)S(1)} %bitcast.115, bf16[64,64,126]{2,1,0:T(8,128)(2,1)} %bitcast.127, bf16[64,64,126]{2,1,0:T(8,128)(2,1)} %bitcast.128, ...), custom_call_target="tpu_custom_call", output_to_operand_aliasing={{3}: (4, {})} | custom-call | flops 10000000 | bytes 8000000 | tf_op jit(solution)/shard_map/table/pallas_call | solution.py:234
  19.6 3.1 %shard_map.104 = (f32[64,2048]{1,0:T(8,128)S(1)}, bf16[32,5,256,256]{3,2,1,0:T(8,128)(2,1)S(1)}) custom-call(s32[5,32]{1,0:T(8,128)S(1)} %bitcast.116, bf16[64,8192]{1,0:T(8,128)(2,1)S(1)} %copy-done, bf16[32,5,256,256]{3,2,1,0:T(8,128)(2,1)S(1)} %get-tuple-element.44.refs_2_, bf16[32,5,256,256]{3,2,1,0:T(8,128)(2,1)} %refs_3_.5), custom_call_target="tpu_custom_call", output_to_operand_aliasing={{1}: (2, {})} | custom-call | flops 350000000 | bytes 6000000 | tf_op jit(solution)/shard_map/pallas_call | solution.py:298
  22.8 3.1 %shard_map.105 = (f32[64,2048]{1,0:T(8,128)S(1)}, bf16[32,5,256,256]{3,2,1,0:T(8,128)(2,1)S(1)}) custom-call(s32[5,32]{1,0:T(8,128)S(1)} %bitcast.117, bf16[64,8192]{1,0:T(8,128)(2,1)S(1)} %copy-done, bf16[32,5,256,256]{3,2,1,0:T(8,128)(2,1)S(1)} %get-tuple-element.45.refs_2_, bf16[32,5,256,256]{3,2,1,0:T(8,128)(2,1)} %refs_3_.5), custom_call_target="tpu_custom_call", output_to_operand_aliasing={{1}: (2, {})} | custom-call | flops 350000000 | bytes 6000000 | tf_op jit(solution)/shard_map/pallas_call | solution.py:298
  31.8 4.9 %collective-permute-start.1 = (f32[64,64]{1,0:T(8,128)S(1)}, f32[64,64]{1,0:T(8,128)S(1)}, u32[]{:S(2)}, u32[]{:S(2)}) collective-permute-start(f32[64,64]{1,0:T(8,128)S(1)} %convolution_add_fusion.10), channel_id=1, source_target_pairs={{0,6},{2,4},{4,2},{6,0},{8,14},{10,12},{12,10},{14,8},{16,22},{18,... | collective-permute-start | bytes 49160 | tf_op jit(solution)/shard_map/ppermute | solution.py:497
  39.2 3.5 %collective-permute-done.2 = f32[64,64]{1,0:T(8,128)S(1)} collective-permute-done((f32[64,64]{1,0:T(8,128)S(1)}, f32[64,64]{1,0:T(8,128)S(1)}, u32[]{:S(2)}, u32[]{:S(2)}) %collective-permute-start.2) | collective-permute-done | bytes 16416 | tf_op jit(solution)/shard_map/ppermute | solution.py:497
  43.4 4.8 %collective-permute-done.3 = f32[64,64]{1,0:T(8,128)S(1)} collective-permute-done((f32[64,64]{1,0:T(8,128)S(1)}, f32[64,64]{1,0:T(8,128)S(1)}, u32[]{:S(2)}, u32[]{:S(2)}) %collective-permute-start.3) | collective-permute-done | bytes 16416 | tf_op jit(solution)/shard_map/ppermute | solution.py:497
  52.5 2.5 %collective-permute-start.5 = (f32[64,64]{1,0:T(8,128)S(1)}, f32[64,64]{1,0:T(8,128)S(1)}, u32[]{:S(2)}, u32[]{:S(2)}) collective-permute-start(f32[64,64]{1,0:T(8,128)S(1)} %convolution_add_fusion.6), channel_id=1, source_target_pairs={{0,96},{2,98},{4,100},{6,102},{8,104},{10,106},{12,108},{14,110},{... | collective-permute-start | bytes 49160 | tf_op jit(solution)/shard_map/ppermute | solution.py:497
  55.2 2.5 %collective-permute-done.5 = f32[64,64]{1,0:T(8,128)S(1)} collective-permute-done((f32[64,64]{1,0:T(8,128)S(1)}, f32[64,64]{1,0:T(8,128)S(1)}, u32[]{:S(2)}, u32[]{:S(2)}) %collective-permute-start.5) | collective-permute-done | bytes 16416 | tf_op jit(solution)/shard_map/ppermute | solution.py:497
  60.2 2.4 %side_b.2 = (f32[64,8448]{1,0:T(8,128)S(1)}, bf16[96,64,128]{2,1,0:T(8,128)(2,1)S(1)}) custom-call(s32[168]{0:T(256)S(1)} %get-tuple-element.42.plan, bf16[64,4096]{1,0:T(8,128)(2,1)S(1)} %collective-permute-done.6.got_vb, bf16[64,2048]{1,0:T(8,128)(2,1)S(1)} %collective-permute-done.7.got_cb, ...), custom_call_target="tpu_custom_call", output_to_operand_aliasing={{0}: (4, {}), {1}: (5, {})} | custom-call | flops 200000000 | bytes 3000000 | tf_op jit(solution)/shard_map/side_b/pallas_call | solution.py:382
  62.6 4.9 %shard_map.108 = (f32[64,8448]{1,0:T(8,128)S(1)}, bf16[96,64,128]{2,1,0:T(8,128)(2,1)S(1)}, bf16[64,8192]{1,0:T(8,128)(2,1)}, bf16[64,8192]{1,0:T(8,128)(2,1)S(1...) custom-call(s32[4,32]{1,0:T(4,128)S(1)} %bitcast.124, ...), custom_call_target="tpu_custom_call", output_to_operand_aliasing={{0}: (5, {}), {1}: (6, {})} | custom-call | flops 600000000 | bytes 6000000 | tf_op jit(solution)/shard_map/pallas_call | solution.py:475
  67.5 5.1 %shard_map.109 = (f32[64,8448]{1,0:T(8,128)S(1)}, bf16[96,64,128]{2,1,0:T(8,128)(2,1)S(1)}, bf16[64,8192]{1,0:T(8,128)(2,1)}, bf16[64,8192]{1,0:T(8,128)(2,1)S(1...) custom-call(s32[4,32]{1,0:T(4,128)S(1)} %bitcast.125, ...), custom_call_target="tpu_custom_call", output_to_operand_aliasing={{0}: (6, {}), {1}: (7, {}), {2}: (8, {}), {3}: (9, {}), {4}... | custom-call | flops 600000000 | bytes 6000000 | tf_op jit(solution)/shard_map/pallas_call | solution.py:475
  83.2 3.2 %collective-permute-start.17 = (bf16[64,2048]{1,0:T(8,128)(2,1)S(1)}, bf16[64,2048]{1,0:T(8,128)(2,1)S(1)}, u32[]{:S(2)}, u32[]{:S(2)}) collective-permute-start(bf16[64,2048]{1,0:T(8,128)(2,1)S(1)} %get-tuple-element.62.sent_c), channel_id=1, source_target_pairs={{2,4},{6,8},{10,12},{14,16},{18,20},{22,24},{26,28},{30,32},{34,36... | collective-permute-start | bytes 786440 | tf_op jit(solution)/shard_map/ppermute | solution.py:503
  86.4 2.9 %collective-permute-start.10 = (f32[64,64]{1,0:T(8,128)S(1)}, f32[64,64]{1,0:T(8,128)S(1)}, u32[]{:S(2)}, u32[]{:S(2)}) collective-permute-start(f32[64,64]{1,0:T(8,128)S(1)} %get-tuple-element.60), channel_id=1, source_target_pairs={{0,2},{2,0},{4,6},{6,4},{8,10},{10,8},{12,14},{14,12},{16,18},{18,... | collective-permute-start | bytes 49160 | tf_op jit(solution)/shard_map/ppermute | solution.py:497
  89.6 3.9 %collective-permute-start.16 = (bf16[64,4096]{1,0:T(8,128)(2,1)S(1)}, bf16[64,4096]{1,0:T(8,128)(2,1)S(1)}, u32[]{:S(2)}, u32[]{:S(2)}) collective-permute-start(bf16[64,4096]{1,0:T(8,128)(2,1)S(1)} %get-tuple-element.61), channel_id=1, source_target_pairs={{2,4},{6,8},{10,12},{14,16},{18,20},{22,24},{26,28},{30,32},{34,36... | collective-permute-start | bytes 1572872 | tf_op jit(solution)/shard_map/ppermute | solution.py:503
  93.7 4.9 %collective-permute-start.11 = (f32[64,64]{1,0:T(8,128)S(1)}, f32[64,64]{1,0:T(8,128)S(1)}, u32[]{:S(2)}, u32[]{:S(2)}) collective-permute-start(f32[64,64]{1,0:T(8,128)S(1)} %convolution_add_fusion.4), channel_id=1, source_target_pairs={{0,6},{2,4},{4,2},{6,0},{8,14},{10,12},{12,10},{14,8},{16,22},{18,... | collective-permute-start | bytes 49160 | tf_op jit(solution)/shard_map/ppermute | solution.py:497
  98.8 7.1 %collective-permute-done.11 = f32[64,64]{1,0:T(8,128)S(1)} collective-permute-done((f32[64,64]{1,0:T(8,128)S(1)}, f32[64,64]{1,0:T(8,128)S(1)}, u32[]{:S(2)}, u32[]{:S(2)}) %collective-permute-start.11) | collective-permute-done | bytes 16416 | tf_op jit(solution)/shard_map/ppermute | solution.py:497
  106.5 3.5 %collective-permute-done.12 = f32[64,64]{1,0:T(8,128)S(1)} collective-permute-done((f32[64,64]{1,0:T(8,128)S(1)}, f32[64,64]{1,0:T(8,128)S(1)}, u32[]{:S(2)}, u32[]{:S(2)}) %collective-permute-start.12) | collective-permute-done | bytes 16416 | tf_op jit(solution)/shard_map/ppermute | solution.py:497
  110.6 4.8 %collective-permute-done.13 = f32[64,64]{1,0:T(8,128)S(1)} collective-permute-done((f32[64,64]{1,0:T(8,128)S(1)}, f32[64,64]{1,0:T(8,128)S(1)}, u32[]{:S(2)}, u32[]{:S(2)}) %collective-permute-start.13) | collective-permute-done | bytes 16416 | tf_op jit(solution)/shard_map/ppermute | solution.py:497
  117.0 2.5 %collective-permute-done.14 = f32[64,64]{1,0:T(8,128)S(1)} collective-permute-done((f32[64,64]{1,0:T(8,128)S(1)}, f32[64,64]{1,0:T(8,128)S(1)}, u32[]{:S(2)}, u32[]{:S(2)}) %collective-permute-start.14) | collective-permute-done | bytes 16416 | tf_op jit(solution)/shard_map/ppermute | solution.py:497
  121.1 3.9 %collective-permute-done.15 = f32[64,64]{1,0:T(8,128)S(1)} collective-permute-done((f32[64,64]{1,0:T(8,128)S(1)}, f32[64,64]{1,0:T(8,128)S(1)}, u32[]{:S(2)}, u32[]{:S(2)}) %collective-permute-start.15) | collective-permute-done | bytes 16416 | tf_op jit(solution)/shard_map/ppermute | solution.py:497
  129.6 7.9 %shard_map.114 = (f32[64,8448]{1,0:T(8,128)S(1)}, bf16[96,64,128]{2,1,0:T(8,128)(2,1)S(1)}, bf16[64,8192]{1,0:T(8,128)(2,1)}) custom-call(s32[4,32]{1,0:T(4,128)S(1)} %bitcast.126, f32[64,64]{1,0:T(8,128)S(1)} %fusion.3.refs_1_, bf16[32,64,256]{2,1,0:T(8,128)(2,1)S(1)} %copy-done.2, ...), custom_call_target="tpu_custom_call", output_to_operand_aliasing={{0}: (5, {}), {1}: (6, {})} | custom-call | flops 600000000 | bytes 6000000 | tf_op jit(solution)/shard_map/pallas_call | solution.py:475
  (79 shorter events, 39.4 us)
Async XLA Ops:
  1.9 56.2 %collective-permute-start.8 = (bf16[64,4096]{1,0:T(8,128)(2,1)S(1)}, bf16[64,4096]{1,0:T(8,128)(2,1)S(1)}, u32[]{:S(2)}, u32[]{:S(2)}) collective-permute-start(bf16[64,4096]{1,0:T(8,128)(2,1)S(1)} %get-tuple-element.36.va), channel_id=1, source_target_pairs={{0,2},{2,0},{4,6},{6,4},{8,10},{10,8},{12,14},{14,12},{16,18},{18,... | collective-permute-start | bytes 1572872 | tf_op jit(solution)/shard_map/ppermute | solution.py:497
  3.4 11.7 %copy-start.4 = (s32[32,5]{0,1:T(8,128)S(1)}, s32[32,5]{0,1:T(8,128)}, u32[]{:S(2)}) copy-start(s32[32,5]{0,1:T(8,128)} %param.12) | copy-start | bytes 1924
  6.5 51.6 %collective-permute-start.9 = (bf16[64,2048]{1,0:T(8,128)(2,1)S(1)}, bf16[64,2048]{1,0:T(8,128)(2,1)S(1)}, u32[]{:S(2)}, u32[]{:S(2)}) collective-permute-start(bf16[64,2048]{1,0:T(8,128)(2,1)S(1)} %get-tuple-element.43.sent_c), channel_id=1, source_target_pairs={{0,2},{2,0},{4,6},{6,4},{8,10},{10,8},{12,14},{14,12},{16,18},{18,... | collective-permute-start | bytes 786440 | tf_op jit(solution)/shard_map/ppermute | solution.py:497
  7.1 53.0 %collective-permute-start.7 = (bf16[64,2048]{1,0:T(8,128)(2,1)S(1)}, bf16[64,2048]{1,0:T(8,128)(2,1)S(1)}, u32[]{:S(2)}, u32[]{:S(2)}) collective-permute-start(bf16[64,2048]{1,0:T(8,128)(2,1)S(1)} %get-tuple-element.43.sent_c), channel_id=1, source_target_pairs={{2,4},{6,8},{10,12},{14,16},{18,20},{22,24},{26,28},{30,32},{34,36... | collective-permute-start | bytes 786440 | tf_op jit(solution)/shard_map/ppermute | solution.py:503
  11.9 48.2 %collective-permute-start.6 = (bf16[64,4096]{1,0:T(8,128)(2,1)S(1)}, bf16[64,4096]{1,0:T(8,128)(2,1)S(1)}, u32[]{:S(2)}, u32[]{:S(2)}) collective-permute-start(bf16[64,4096]{1,0:T(8,128)(2,1)S(1)} %get-tuple-element.37.vb), channel_id=1, source_target_pairs={{2,4},{6,8},{10,12},{14,16},{18,20},{22,24},{26,28},{30,32},{34,36... | collective-permute-start | bytes 1572872 | tf_op jit(solution)/shard_map/ppermute | solution.py:503
  15.0 16.6 %collective-permute-start = (f32[64,64]{1,0:T(8,128)S(1)}, f32[64,64]{1,0:T(8,128)S(1)}, u32[]{:S(2)}, u32[]{:S(2)}) collective-permute-start(f32[64,64]{1,0:T(8,128)S(1)} %get-tuple-element.38), channel_id=1, source_target_pairs={{0,2},{2,0},{4,6},{6,4},{8,10},{10,8},{12,14},{14,12},{16,18},{18,... | collective-permute-start | bytes 49160 | tf_op jit(solution)/shard_map/ppermute | solution.py:497
  15.1 4.5 %copy-start = (bf16[64,8192]{1,0:T(8,128)(2,1)S(1)}, bf16[64,8192]{1,0:T(8,128)(2,1)}, u32[]{:S(2)}) copy-start(bf16[64,8192]{1,0:T(8,128)(2,1)} %refs_1_.7) | copy-start | bytes 3145732
  31.8 6.8 %collective-permute-start.1 = (f32[64,64]{1,0:T(8,128)S(1)}, f32[64,64]{1,0:T(8,128)S(1)}, u32[]{:S(2)}, u32[]{:S(2)}) collective-permute-start(f32[64,64]{1,0:T(8,128)S(1)} %convolution_add_fusion.10), channel_id=1, source_target_pairs={{0,6},{2,4},{4,2},{6,0},{8,14},{10,12},{12,10},{14,8},{16,22},{18,... | collective-permute-start | bytes 49160 | tf_op jit(solution)/shard_map/ppermute | solution.py:497
  38.8 4.0 %collective-permute-start.2 = (f32[64,64]{1,0:T(8,128)S(1)}, f32[64,64]{1,0:T(8,128)S(1)}, u32[]{:S(2)}, u32[]{:S(2)}) collective-permute-start(f32[64,64]{1,0:T(8,128)S(1)} %convolution_add_fusion.9), channel_id=1, source_target_pairs={{0,8},{2,10},{4,12},{6,14},{8,0},{10,2},{12,4},{14,6},{16,24},{18,... | collective-permute-start | bytes 49160 | tf_op jit(solution)/shard_map/ppermute | solution.py:497
  43.0 5.2 %collective-permute-start.3 = (f32[64,64]{1,0:T(8,128)S(1)}, f32[64,64]{1,0:T(8,128)S(1)}, u32[]{:S(2)}, u32[]{:S(2)}) collective-permute-start(f32[64,64]{1,0:T(8,128)S(1)} %convolution_add_fusion.8), channel_id=1, source_target_pairs={{0,24},{2,26},{4,28},{6,30},{8,16},{10,18},{12,20},{14,22},{16,8},... | collective-permute-start | bytes 49160 | tf_op jit(solution)/shard_map/ppermute | solution.py:497
  48.3 4.0 %collective-permute-start.4 = (f32[64,64]{1,0:T(8,128)S(1)}, f32[64,64]{1,0:T(8,128)S(1)}, u32[]{:S(2)}, u32[]{:S(2)}) collective-permute-start(f32[64,64]{1,0:T(8,128)S(1)} %convolution_add_fusion.7), channel_id=1, source_target_pairs={{0,32},{2,34},{4,36},{6,38},{8,40},{10,42},{12,44},{14,46},{16,48}... | collective-permute-start | bytes 49160 | tf_op jit(solution)/shard_map/ppermute | solution.py:497
  52.5 5.2 %collective-permute-start.5 = (f32[64,64]{1,0:T(8,128)S(1)}, f32[64,64]{1,0:T(8,128)S(1)}, u32[]{:S(2)}, u32[]{:S(2)}) collective-permute-start(f32[64,64]{1,0:T(8,128)S(1)} %convolution_add_fusion.6), channel_id=1, source_target_pairs={{0,96},{2,98},{4,100},{6,102},{8,104},{10,106},{12,108},{14,110},{... | collective-permute-start | bytes 49160 | tf_op jit(solution)/shard_map/ppermute | solution.py:497
  60.1 2.4 %copy-start.1 = (bf16[32,4,64,64]{3,2,1,0:T(8,128)(2,1)S(1)}, bf16[32,4,64,64]{3,2,1,0:T(8,128)(2,1)}, u32[]{:S(2)}) copy-start(bf16[32,4,64,64]{3,2,1,0:T(8,128)(2,1)} %refs_4_.5) | copy-start | bytes 3145732
  60.2 2.4 %copy-start.2 = (bf16[32,64,256]{2,1,0:T(8,128)(2,1)S(1)}, bf16[32,64,256]{2,1,0:T(8,128)(2,1)}, u32[]{:S(2)}) copy-start(bf16[32,64,256]{2,1,0:T(8,128)(2,1)} %refs_2_.5) | copy-start | bytes 3145732
  81.7 43.6 %collective-permute-start.19 = (bf16[64,2048]{1,0:T(8,128)(2,1)S(1)}, bf16[64,2048]{1,0:T(8,128)(2,1)S(1)}, u32[]{:S(2)}, u32[]{:S(2)}) collective-permute-start(bf16[64,2048]{1,0:T(8,128)(2,1)S(1)} %get-tuple-element.62.sent_c), channel_id=1, source_target_pairs={{0,2},{2,0},{4,6},{6,4},{8,10},{10,8},{12,14},{14,12},{16,18},{18,... | collective-permute-start | bytes 786440 | tf_op jit(solution)/shard_map/ppermute | solution.py:497
  83.2 44.2 %collective-permute-start.17 = (bf16[64,2048]{1,0:T(8,128)(2,1)S(1)}, bf16[64,2048]{1,0:T(8,128)(2,1)S(1)}, u32[]{:S(2)}, u32[]{:S(2)}) collective-permute-start(bf16[64,2048]{1,0:T(8,128)(2,1)S(1)} %get-tuple-element.62.sent_c), channel_id=1, source_target_pairs={{2,4},{6,8},{10,12},{14,16},{18,20},{22,24},{26,28},{30,32},{34,36... | collective-permute-start | bytes 786440 | tf_op jit(solution)/shard_map/ppermute | solution.py:503
  86.4 7.1 %collective-permute-start.10 = (f32[64,64]{1,0:T(8,128)S(1)}, f32[64,64]{1,0:T(8,128)S(1)}, u32[]{:S(2)}, u32[]{:S(2)}) collective-permute-start(f32[64,64]{1,0:T(8,128)S(1)} %get-tuple-element.60), channel_id=1, source_target_pairs={{0,2},{2,0},{4,6},{6,4},{8,10},{10,8},{12,14},{14,12},{16,18},{18,... | collective-permute-start | bytes 49160 | tf_op jit(solution)/shard_map/ppermute | solution.py:497
  89.5 35.8 %collective-permute-start.18 = (bf16[64,4096]{1,0:T(8,128)(2,1)S(1)}, bf16[64,4096]{1,0:T(8,128)(2,1)S(1)}, u32[]{:S(2)}, u32[]{:S(2)}) collective-permute-start(bf16[64,4096]{1,0:T(8,128)(2,1)S(1)} %get-tuple-element.63), channel_id=1, source_target_pairs={{0,2},{2,0},{4,6},{6,4},{8,10},{10,8},{12,14},{14,12},{16,18},{18,... | collective-permute-start | bytes 1572872 | tf_op jit(solution)/shard_map/ppermute | solution.py:497
  89.6 37.8 %collective-permute-start.16 = (bf16[64,4096]{1,0:T(8,128)(2,1)S(1)}, bf16[64,4096]{1,0:T(8,128)(2,1)S(1)}, u32[]{:S(2)}, u32[]{:S(2)}) collective-permute-start(bf16[64,4096]{1,0:T(8,128)(2,1)S(1)} %get-tuple-element.61), channel_id=1, source_target_pairs={{2,4},{6,8},{10,12},{14,16},{18,20},{22,24},{26,28},{30,32},{34,36... | collective-permute-start | bytes 1572872 | tf_op jit(solution)/shard_map/ppermute | solution.py:503
  93.7 12.2 %collective-permute-start.11 = (f32[64,64]{1,0:T(8,128)S(1)}, f32[64,64]{1,0:T(8,128)S(1)}, u32[]{:S(2)}, u32[]{:S(2)}) collective-permute-start(f32[64,64]{1,0:T(8,128)S(1)} %convolution_add_fusion.4), channel_id=1, source_target_pairs={{0,6},{2,4},{4,2},{6,0},{8,14},{10,12},{12,10},{14,8},{16,22},{18,... | collective-permute-start | bytes 49160 | tf_op jit(solution)/shard_map/ppermute | solution.py:497
  106.0 4.0 %collective-permute-start.12 = (f32[64,64]{1,0:T(8,128)S(1)}, f32[64,64]{1,0:T(8,128)S(1)}, u32[]{:S(2)}, u32[]{:S(2)}) collective-permute-start(f32[64,64]{1,0:T(8,128)S(1)} %convolution_add_fusion.3), channel_id=1, source_target_pairs={{0,8},{2,10},{4,12},{6,14},{8,0},{10,2},{12,4},{14,6},{16,24},{18,... | collective-permute-start | bytes 49160 | tf_op jit(solution)/shard_map/ppermute | solution.py:497
  110.2 5.2 %collective-permute-start.13 = (f32[64,64]{1,0:T(8,128)S(1)}, f32[64,64]{1,0:T(8,128)S(1)}, u32[]{:S(2)}, u32[]{:S(2)}) collective-permute-start(f32[64,64]{1,0:T(8,128)S(1)} %convolution_add_fusion.2), channel_id=1, source_target_pairs={{0,24},{2,26},{4,28},{6,30},{8,16},{10,18},{12,20},{14,22},{16,8},... | collective-permute-start | bytes 49160 | tf_op jit(solution)/shard_map/ppermute | solution.py:497
  115.6 4.0 %collective-permute-start.14 = (f32[64,64]{1,0:T(8,128)S(1)}, f32[64,64]{1,0:T(8,128)S(1)}, u32[]{:S(2)}, u32[]{:S(2)}) collective-permute-start(f32[64,64]{1,0:T(8,128)S(1)} %convolution_add_fusion.1), channel_id=1, source_target_pairs={{0,32},{2,34},{4,36},{6,38},{8,40},{10,42},{12,44},{14,46},{16,48}... | collective-permute-start | bytes 49160 | tf_op jit(solution)/shard_map/ppermute | solution.py:497
  119.7 5.2 %collective-permute-start.15 = (f32[64,64]{1,0:T(8,128)S(1)}, f32[64,64]{1,0:T(8,128)S(1)}, u32[]{:S(2)}, u32[]{:S(2)}) collective-permute-start(f32[64,64]{1,0:T(8,128)S(1)} %convolution_add_fusion), channel_id=1, source_target_pairs={{0,96},{2,98},{4,100},{6,102},{8,104},{10,106},{12,108},{14,110},{... | collective-permute-start | bytes 49160 | tf_op jit(solution)/shard_map/ppermute | solution.py:497
  (2 other events, 4.8 us)
